TPU v7x, 32 devices: a whole 2x2x4 slice. The times are simulated.
32 devices in a mesh: dp: 8 (over z, x), tensor: 4 (over y, core).
Axes of the slice: x: 2, y: 2, z: 4, core: 2. Of those that a mesh axis runs over, the one named last changes fastest.
Arguments:
- tokens_in: bfloat16 [16384, 1152], P(('dp', 'tensor')), may hold values from -6 to 6
- condition: bfloat16 [16, 1152], P('dp'), may hold values from -6 to 6
- w_ada: bfloat16 [1152, 6912], P('dp', 'tensor'), may hold values from -0.1875 to 0.1875
- b_ada: bfloat16 [6912], P('tensor'), may hold values from -3 to 3
- w_qkv: bfloat16 [1152, 3456], P('dp', 'tensor'), may hold values from -0.1875 to 0.1875
- b_qv: bfloat16 [2304], P('tensor'), may hold values from -3 to 3
- w_proj: bfloat16 [1152, 1152], P('tensor', 'dp'), may hold values from -2 to 2
- b_proj: bfloat16 [1152], replicated, may hold values from -3 to 3
- w_fc1: bfloat16 [1152, 4608], P('dp', 'tensor'), may hold values from -0.1875 to 0.1875
- b_fc1: bfloat16 [4608], P('tensor'), may hold values from -3 to 3
- w_fc2: bfloat16 [4608, 1152], P('tensor', 'dp'), may hold values from -0.09375 to 0.09375
- b_fc2: bfloat16 [1152], replicated, may hold values from -3 to 3
- cotangent: bfloat16 [16384, 1152], P(('dp', 'tensor')), may hold values from -6 to 6
Outputs:
- block_out: bfloat16 [16384, 1152], P(('dp', 'tensor'))
- grad_tokens: float32 [16384, 1152], P(('dp', 'tensor'))
- grad_condition: float32 [16, 1152], P('dp')
- grad_w_ada: float32 [1152, 6912], P('dp', 'tensor')
- grad_b_ada: float32 [6912], P('tensor')
- grad_w_qkv: float32 [1152, 3456], P('dp', 'tensor')
- grad_b_qv: float32 [2304], P('tensor')
- grad_w_proj: float32 [1152, 1152], P('tensor', 'dp')
- grad_b_proj: float32 [1152], replicated
- grad_w_fc1: float32 [1152, 4608], P('dp', 'tensor')
- grad_b_fc1: float32 [4608], P('tensor')
- grad_w_fc2: float32 [4608, 1152], P('tensor', 'dp')
- grad_b_fc2: float32 [1152], replicated
All inputs are finite; a program needn't handle non-finite values.
Results may differ from a plain program's by a relative error of at most 0.015.
The roundings to bfloat16 on the way count: a program that leaves them out, or rounds other values in their place, can miss the bound.
Values may be sent and summed in bfloat16 or wider, within the bound.
No kernel may reach another device: no remote copies, remote signals or barrier semaphores. Data moves between devices by JAX's collectives and lax.ppermute only.
A program may use at most 192 MiB of HBM per device.

v0:
```python
import jax
import jax.numpy as jnp
from jax import lax
from jax.sharding import PartitionSpec as P

HEAD_DIM = 72
SEQ = 1024


highest = lax.Precision.HIGHEST
root_two_pi = 0.7978845608028654
cubic_term = 0.044715
epsilon = 1e-06


def normalize(values):
    centre = values - jnp.mean(values, axis=-1, keepdims=True)
    inverse = lax.rsqrt(jnp.mean(centre * centre, axis=-1, keepdims=True) + epsilon)
    return (centre * inverse, inverse)


def norm_back(normed, inverse, grad_in):
    mean_grad = jnp.mean(grad_in, axis=-1, keepdims=True)
    mean_cross = jnp.mean(grad_in * normed, axis=-1, keepdims=True)
    return inverse * (grad_in - mean_grad - normed * mean_cross)


def gelu_parts(pre_act):
    tangent = jnp.tanh(root_two_pi * (pre_act + cubic_term * pre_act * pre_act * pre_act))
    activated = 0.5 * pre_act * (1.0 + tangent)
    gelu_slope = 0.5 * (1.0 + tangent) + 0.5 * pre_act * (1.0 - tangent * tangent) * root_two_pi * (
        1.0 + 3.0 * cubic_term * pre_act * pre_act
    )
    return (activated, gelu_slope)


def fetch_weights(w_qkv, w_fc1, w_ada, w_proj, w_fc2):
    columns = (
        lax.all_gather(w_qkv, "dp", axis=0, tiled=True),
        lax.all_gather(w_fc1, "dp", axis=0, tiled=True),
        lax.all_gather(w_ada, "dp", axis=0, tiled=True),
    )
    row_parts = (
        lax.all_gather(w_proj, "dp", axis=1, tiled=True),
        lax.all_gather(w_fc2, "dp", axis=1, tiled=True),
    )
    return (columns, row_parts)


def gather_rows(values):
    return lax.all_gather(values, "tensor", axis=0, tiled=True)


def sum_back(row_term, row_count):
    return lax.psum_scatter(
        row_term(jnp.int32(0), lax.axis_size("tensor") * row_count).astype(jnp.bfloat16),
        "tensor",
        scatter_dimension=0,
        tiled=True,
    ).astype(jnp.float32)


def right_product(left_rows, right_mat):
    return jnp.dot(left_rows, right_mat, preferred_element_type=jnp.float32)


def transposed_product(left_rows, right_mat):

    def row_term(row_start, row_count):
        return lax.dot_general(
            left_rows, right_mat, (((1,), (1,)), ((), ())), preferred_element_type=jnp.float32
        )

    return row_term


def back_fold(weight_mat, kept_all, shard_rows):
    rows_in = lax.dot_general(
        shard_rows, weight_mat, (((1,), (1,)), ((), ())), preferred_element_type=jnp.float32
    )
    grad_weight = lax.dot_general(
        kept_all, shard_rows, (((0,), (0,)), ((), ())), preferred_element_type=jnp.float32
    )
    return (rows_in, grad_weight)


def attend(operands):
    queries, keys_b, values_b = operands
    score_scale = queries.shape[-1] ** (-0.5)
    scores = (
        jnp.einsum("qhd,khd->hqk", queries, keys_b, preferred_element_type=jnp.float32)
        * score_scale
    )
    row_max = jnp.max(scores, axis=-1, keepdims=True)
    exponent = jnp.exp(scores - row_max)
    row_total = jnp.sum(exponent, axis=-1, keepdims=True)
    attn_probs = (exponent / row_total).astype(jnp.bfloat16)
    mixture = jnp.einsum("hqk,khd->qhd", attn_probs, values_b, preferred_element_type=jnp.float32)
    return (mixture.astype(jnp.bfloat16), (row_max + jnp.log(row_total))[..., 0])


def attend_back(operands):
    queries, keys_b, values_b, grad_mix, logsum = operands
    score_scale = queries.shape[-1] ** (-0.5)
    scores = (
        jnp.einsum("qhd,khd->hqk", queries, keys_b, preferred_element_type=jnp.float32)
        * score_scale
    )
    attn_probs = jnp.exp(scores - logsum[..., None])
    grad_probs = jnp.einsum("qhd,khd->hqk", grad_mix, values_b, preferred_element_type=jnp.float32)
    row_inner = jnp.sum(grad_probs * attn_probs, axis=-1, keepdims=True)
    grad_scores = (attn_probs * (grad_probs - row_inner)).astype(jnp.bfloat16)
    grad_queries = (
        jnp.einsum("hqk,khd->qhd", grad_scores, keys_b, preferred_element_type=jnp.float32)
        * score_scale
    )
    grad_keys = (
        jnp.einsum("hqk,qhd->khd", grad_scores, queries, preferred_element_type=jnp.float32)
        * score_scale
    )
    grad_values = jnp.einsum(
        "hqk,qhd->khd",
        attn_probs.astype(jnp.bfloat16),
        grad_mix,
        preferred_element_type=jnp.float32,
    )
    return jnp.stack([grad_queries, grad_keys, grad_values], axis=2).astype(jnp.bfloat16)


def shards(
    tokens_in,
    condition,
    w_ada,
    b_ada,
    w_qkv,
    b_qv,
    w_proj,
    b_proj,
    w_fc1,
    b_fc1,
    w_fc2,
    b_fc2,
    cotangent,
):
    tok_rows = tokens_in.shape[0]
    latents = condition.shape[0]
    head_size = HEAD_DIM
    (qkv_full, fc1_full, ada_full), (proj_full, fc2_full) = fetch_weights(
        w_qkv, w_fc1, w_ada, w_proj, w_fc2
    )
    cond_vals = condition.astype(jnp.float32)
    cond_sigmoid = jax.nn.sigmoid(cond_vals)
    silu_cond = (cond_vals * cond_sigmoid).astype(jnp.bfloat16)
    mod_part = jnp.dot(silu_cond, ada_full, preferred_element_type=jnp.float32) + b_ada.astype(
        jnp.float32
    )
    modulation = lax.all_gather(mod_part, "tensor", axis=1, tiled=True)
    row_place = lax.axis_index("tensor") * tok_rows + jnp.arange(tok_rows, dtype=jnp.int32)
    onehot = (row_place[:, None] // SEQ == jnp.arange(latents, dtype=jnp.int32)[None, :]).astype(
        jnp.float32
    )
    mod_rows = jnp.dot(onehot, modulation, precision=highest)
    shift_attn, scale_attn, gate_attn, shift_mlp, scale_mlp, gate_mlp = jnp.split(
        mod_rows, 6, axis=1
    )
    input_vals = tokens_in.astype(jnp.float32)
    normed_one, inverse_one = normalize(input_vals)
    attn_in = (normed_one * (1.0 + scale_attn) + shift_attn).astype(jnp.bfloat16)
    attn_rows = gather_rows(attn_in)
    full_rows = attn_rows.shape[0]
    head_count = qkv_full.shape[1] // (3 * head_size)
    projected = jnp.dot(attn_rows, qkv_full, preferred_element_type=jnp.float32).reshape(
        full_rows, head_count, 3, head_size
    )
    bias_qv = b_qv.astype(jnp.float32).reshape(head_count, 2, head_size)
    block_shape = (full_rows // SEQ, SEQ, head_count, head_size)
    queries = (projected[:, :, 0] + bias_qv[:, 0]).astype(jnp.bfloat16).reshape(block_shape)
    keys_b = projected[:, :, 1].astype(jnp.bfloat16).reshape(block_shape)
    values_b = (projected[:, :, 2] + bias_qv[:, 1]).astype(jnp.bfloat16).reshape(block_shape)
    mixture, logsum = lax.map(attend, (queries, keys_b, values_b))
    mix_rows = mixture.reshape(full_rows, head_count * head_size)
    attn_out = lax.psum_scatter(
        right_product(mix_rows, proj_full).astype(jnp.bfloat16),
        "tensor",
        scatter_dimension=0,
        tiled=True,
    ).astype(jnp.float32) + b_proj.astype(jnp.float32)
    middle = input_vals + gate_attn * attn_out
    normed_two, inverse_two = normalize(middle)
    mlp_in = (normed_two * (1.0 + scale_mlp) + shift_mlp).astype(jnp.bfloat16)
    mlp_rows = gather_rows(mlp_in)
    pre_act = jnp.dot(mlp_rows, fc1_full, preferred_element_type=jnp.float32) + b_fc1.astype(
        jnp.float32
    )
    activated, gelu_slope = gelu_parts(pre_act)
    act_rows = activated.astype(jnp.bfloat16)
    mlp_out = lax.psum_scatter(
        right_product(act_rows, fc2_full).astype(jnp.bfloat16),
        "tensor",
        scatter_dimension=0,
        tiled=True,
    ).astype(jnp.float32) + b_fc2.astype(jnp.float32)
    result = middle + gate_mlp * mlp_out
    grad_out = cotangent.astype(jnp.float32)
    grad_mlp = (gate_mlp * grad_out).astype(jnp.bfloat16)
    d_gate_mlp = grad_out * mlp_out
    held_weights = lax.optimization_barrier((w_qkv, w_fc1, w_ada, w_proj, w_fc2, grad_mlp))
    (qkv_back, fc1_back, ada_back), (proj_back, fc2_back) = fetch_weights(
        held_weights[0], held_weights[1], held_weights[2], held_weights[3], held_weights[4]
    )
    grad_act, grad_fc2 = back_fold(
        fc2_back, act_rows, lax.all_gather(grad_mlp, "tensor", axis=0, tiled=True)
    )
    grad_pre = (grad_act * gelu_slope).astype(jnp.bfloat16)
    grad_fc1 = lax.dot_general(
        mlp_rows, grad_pre, (((0,), (0,)), ((), ())), preferred_element_type=jnp.float32
    )
    grad_mlp_in = sum_back(transposed_product(grad_pre, fc1_back), tok_rows)
    d_scale_mlp = grad_mlp_in * normed_two
    grad_middle = grad_out + norm_back(normed_two, inverse_two, grad_mlp_in * (1.0 + scale_mlp))
    grad_attn = (gate_attn * grad_middle).astype(jnp.bfloat16)
    d_gate_attn = grad_middle * attn_out
    grad_mixture, grad_proj = back_fold(
        proj_back, mix_rows, lax.all_gather(grad_attn, "tensor", axis=0, tiled=True)
    )
    grad_mix_b = grad_mixture.astype(jnp.bfloat16).reshape(block_shape)
    grad_qkv = lax.map(attend_back, (queries, keys_b, values_b, grad_mix_b, logsum)).reshape(
        full_rows, head_count * 3 * head_size
    )
    grad_wqkv = lax.dot_general(
        attn_rows, grad_qkv, (((0,), (0,)), ((), ())), preferred_element_type=jnp.float32
    )
    grad_attn_in = sum_back(transposed_product(grad_qkv, qkv_back), tok_rows)
    d_scale_attn = grad_attn_in * normed_one
    grad_tokens = grad_middle + norm_back(
        normed_one, inverse_one, grad_attn_in * (1.0 + scale_attn)
    )
    grad_mod_rows = jnp.concatenate(
        [grad_attn_in, d_scale_attn, d_gate_attn, grad_mlp_in, d_scale_mlp, d_gate_mlp], axis=1
    )
    grad_mod_all = jnp.dot(onehot.T, grad_mod_rows, precision=highest)
    grad_mod = lax.psum_scatter(
        grad_mod_all.astype(jnp.bfloat16), "tensor", scatter_dimension=1, tiled=True
    ).astype(jnp.float32)
    grad_ada = jnp.dot(silu_cond.astype(jnp.float32).T, grad_mod, precision=highest)
    grad_silu = jnp.dot(grad_mod, ada_back.T, precision=highest)
    grad_cond_part = grad_silu * cond_sigmoid * (1.0 + cond_vals * (1.0 - cond_sigmoid))
    qkv_sums = jnp.sum(
        grad_qkv.astype(jnp.float32).reshape(full_rows, head_count, 3, head_size), axis=0
    )
    grad_bqv_part = jnp.stack([qkv_sums[:, 0], qkv_sums[:, 2]], axis=1).reshape(-1)
    grad_b1_part = jnp.sum(grad_pre.astype(jnp.float32), axis=0)
    grad_bo_part = jnp.sum(grad_attn.astype(jnp.float32), axis=0)
    grad_b2_part = jnp.sum(grad_mlp.astype(jnp.float32), axis=0)
    grad_ba_part = jnp.sum(grad_mod, axis=0)
    grad_condition, grad_bo_mid, grad_b2_mid = lax.psum(
        (grad_cond_part, grad_bo_part, grad_b2_part), "tensor"
    )
    grad_bqv, grad_b1, grad_ba, grad_bo, grad_b2 = lax.psum(
        (grad_bqv_part, grad_b1_part, grad_ba_part, grad_bo_mid, grad_b2_mid), "dp"
    )
    owned_qkv, owned_fc1, owned_ada = (
        lax.psum_scatter(grad_wqkv, "dp", scatter_dimension=0, tiled=True),
        lax.psum_scatter(grad_fc1, "dp", scatter_dimension=0, tiled=True),
        lax.psum_scatter(grad_ada, "dp", scatter_dimension=0, tiled=True),
    )
    owned_proj, owned_fc2 = (
        lax.psum_scatter(grad_proj, "dp", scatter_dimension=1, tiled=True),
        lax.psum_scatter(grad_fc2, "dp", scatter_dimension=1, tiled=True),
    )
    return (
        result.astype(jnp.bfloat16),
        grad_tokens,
        grad_condition,
        owned_ada,
        grad_ba,
        owned_qkv,
        grad_bqv,
        owned_proj,
        grad_bo,
        owned_fc1,
        grad_b1,
        owned_fc2,
        grad_b2,
    )


def solution(mesh):
    placed = (
        P(("dp", "tensor"), None),
        P("dp", None),
        P("dp", "tensor"),
        P("tensor"),
        P("dp", "tensor"),
        P("tensor"),
        P("tensor", "dp"),
        P(),
        P("dp", "tensor"),
        P("tensor"),
        P("tensor", "dp"),
        P(),
        P(("dp", "tensor"), None),
    )
    return jax.shard_map(
        shards,
        mesh=mesh,
        in_specs=placed,
        out_specs=(
            P(("dp", "tensor"), None),
            P(("dp", "tensor"), None),
            P("dp", None),
            P("dp", "tensor"),
            P("tensor"),
            P("dp", "tensor"),
            P("tensor"),
            P("tensor", "dp"),
            P(),
            P("dp", "tensor"),
            P("tensor"),
            P("tensor", "dp"),
            P(),
        ),
        check_vma=False,
    )
```

profile of v0, /device:TPU:0, one launch (start us, length us, event | category | flops | bytes accessed | tf_op | source)
XLA Modules:
  0.0 1585.5 jit_solution(13999615193881543100)
XLA Ops:
  11.4 74.1 %all-gather.14.cloned.1.call-done = bf16[1152,1728]{1,0:T(8,128)(2,1)} async-done(((bf16[144,1728]{1,0:T(8,128)(2,1)}), bf16[1152,1728]{1,0:T(8,128)(2,1)}) %all-gather.14.cloned.1.call-update) | async-done | bytes 3981328 | tf_op jit(solution)/shard_map/all_gather | solution.py:41
  106.3 36.7 %all_gather.49 = bf16[288,1152]{0,1:T(8,128)(2,1)} all-gather(bf16[288,144]{0,1:T(8,128)(2,1)S(1)} %copy-done.24), channel_id=1, replica_groups=mesh['dp'=8,'tensor'=4] {'dp'}, dimensions={1}, use_global_device_ids=true | all-gather | bytes 746496 | tf_op jit(solution)/shard_map/all_gather | solution.py:44
  147.2 39.3 %all-gather.16.cloned.1.call-done = bf16[2048,1152]{1,0:T(8,128)(2,1)} async-done(((bf16[512,1152]{1,0:T(8,128)(2,1)}), bf16[2048,1152]{1,0:T(8,128)(2,1)}) %all-gather.16.cloned.1.call-update) | async-done | bytes 4718608 | tf_op jit(solution)/shard_map/all_gather | solution.py:51
  216.0 51.3 %while.22 = (s32[]{:T(128)}, bf16[2,1024,4,72]{1,3,2,0:T(8,128)(2,1)}, f32[2,4,1024]{2,1,0:T(4,128)S(1)}, bf16[2,1024,4,72]{1,3,2,0:T(8,128)(2,1)}, bf16[2,1024,...) while((s32[]{:T(128)}, bf16[2,1024,4,72]{1,3,2,0:T(8,128)(2,1)}, ...), condition=%wide.region_5.6_spmd, body=%wide.region_2.5_spmd.sunk | while | flops 1245999104 | bytes 66980012 | solution.py:180
  276.7 47.1 %reduce-scatter.13.cloned.1.call-done = bf16[512,1152]{1,0:T(8,128)(2,1)} async-done(((bf16[2048,1152]{1,0:T(8,128)(2,1)}), bf16[512,1152]{1,0:T(8,128)(2,1)}) %reduce-scatter.13.cloned.1.call-update) | async-done | bytes 1179664 | tf_op jit(solution)/shard_map/reduce_scatter | solution.py:182
  337.3 43.7 %all-gather.22.cloned.1.call-done = bf16[1152,1152]{1,0:T(8,128)(2,1)} async-done(((bf16[144,1152]{1,0:T(8,128)(2,1)}), bf16[1152,1152]{1,0:T(8,128)(2,1)}) %all-gather.22.cloned.1.call-update) | async-done | bytes 2654224 | tf_op jit(solution)/shard_map/all_gather | solution.py:40
  381.1 38.1 %all-gather.20.cloned.1.call-done = bf16[2048,1152]{1,0:T(8,128)(2,1)} async-done(((bf16[512,1152]{1,0:T(8,128)(2,1)}), bf16[2048,1152]{1,0:T(8,128)(2,1)}) %all-gather.20.cloned.1.call-update) | async-done | bytes 4718608 | tf_op jit(solution)/shard_map/all_gather | solution.py:51
  419.2 11.6 convolution_add_fusion
  430.8 45.9 %all-gather.28.cloned.1.call-done = bf16[1152,1152]{0,1:T(8,128)(2,1)} async-done(((bf16[1152,144]{0,1:T(8,128)(2,1)}), bf16[1152,1152]{0,1:T(8,128)(2,1)}) %all-gather.28.cloned.1.call-update) | async-done | bytes 2654224 | tf_op jit(solution)/shard_map/all_gather | solution.py:45
  476.7 38.3 %all-gather.26.cloned.1.call-done = bf16[2048,1152]{1,0:T(8,128)(2,1)} async-done(((bf16[512,1152]{1,0:T(8,128)(2,1)}), bf16[2048,1152]{1,0:T(8,128)(2,1)}) %all-gather.26.cloned.1.call-update) | async-done | bytes 4718608 | tf_op jit(solution)/shard_map/all_gather | solution.py:212
  515.0 16.0 %convert_reduce_fusion = (f32[1152]{0:T(1024)}, bf16[2048,1152]{1,0:T(8,128)(2,1)}) fusion(f32[2048,1152]{1,0:T(8,128)} %convolution_add_fusion, bf16[2048,1152]{1,0:T(8,128)(2,1)} %all-gather.26.cloned.1.call-done, bf16[1152,1152]{0,1:T(8,128)(2,1)} %all-gather.28.cloned.1.call-done), kind=kOutput, calls=%fused_computation.64 | convolution fusion | flops 5485362176 | bytes 21533184 | tf_op jit(solution)/shard_map/dot_general | solution.py:78
  530.9 41.5 %all-gather.30.cloned.1.call-done = bf16[1152,1152]{1,0:T(8,128)(2,1)} async-done(((bf16[144,1152]{1,0:T(8,128)(2,1)}), bf16[1152,1152]{1,0:T(8,128)(2,1)}) %all-gather.30.cloned.1.call-update) | async-done | bytes 2654224 | tf_op jit(solution)/shard_map/all_gather | solution.py:40
  572.4 11.0 convolution_convert_fusion.2
  583.9 44.4 %all-gather.24.cloned.1.call-done = bf16[1152,1152]{0,1:T(8,128)(2,1)} async-done(((bf16[1152,144]{0,1:T(8,128)(2,1)}), bf16[1152,1152]{0,1:T(8,128)(2,1)}) %all-gather.24.cloned.1.call-update) | async-done | bytes 2654224 | tf_op jit(solution)/shard_map/all_gather | solution.py:45
  628.3 13.0 convolution_convert_fusion.3
  642.0 35.4 %reduce-scatter.17.cloned.1.call-done = bf16[512,1152]{1,0:T(8,128)(2,1)} async-done(((bf16[2048,1152]{1,0:T(8,128)(2,1)}), bf16[512,1152]{1,0:T(8,128)(2,1)}) %reduce-scatter.17.cloned.1.call-update) | async-done | bytes 1179664 | tf_op jit(solution)/shard_map/reduce_scatter | solution.py:55
  681.0 46.8 %reduce-scatter.15.cloned.1.call-done = bf16[512,1152]{1,0:T(8,128)(2,1)} async-done(((bf16[2048,1152]{1,0:T(8,128)(2,1)}), bf16[512,1152]{1,0:T(8,128)(2,1)}) %reduce-scatter.15.cloned.1.call-update) | async-done | bytes 1179664 | tf_op jit(solution)/shard_map/reduce_scatter | solution.py:197
  735.7 32.4 %all_gather.57 = bf16[288,1152]{0,1:T(8,128)(2,1)S(1)} all-gather(bf16[288,144]{0,1:T(8,128)(2,1)S(1)} %copy-done.25), channel_id=1, replica_groups=mesh['dp'=8,'tensor'=4] {'dp'}, dimensions={1}, use_global_device_ids=true | all-gather | bytes 746496 | tf_op jit(solution)/shard_map/all_gather | solution.py:44
  785.2 75.6 %while.23 = (s32[]{:T(128)}, bf16[2,1024,4,3,72]{1,4,2,3,0:T(8,128)(2,1)}, bf16[2,1024,4,72]{1,3,2,0:T(8,128)(2,1)S(1)}, bf16[2,1024,4,72]{1,3,2,0:T(8,128)(2,1)...) while((s32[]{:T(128)}, ...), condition=%wide.region_15.16_spmd, body=%wide.region_13.15_spmd.sunk | while | flops 3077009408 | bytes 199608528 | solution.py:227
  867.7 10.1 convolution_convert_fusion.1
  877.9 48.1 %reduce-scatter.19.cloned.1.call-done = bf16[512,1152]{1,0:T(8,128)(2,1)} async-done(((bf16[2048,1152]{1,0:T(8,128)(2,1)}), bf16[512,1152]{1,0:T(8,128)(2,1)}) %reduce-scatter.19.cloned.1.call-update) | async-done | bytes 1179664 | tf_op jit(solution)/shard_map/reduce_scatter | solution.py:55
  946.2 14.2 fusion.95
  960.6 12.7 fusion.104
  980.6 9.5 fusion.102
  1000.3 49.2 %all-gather.36.cloned.1.call-done = bf16[1152,1728]{1,0:T(8,128)(2,1)} async-done(((bf16[144,1728]{1,0:T(8,128)(2,1)}), bf16[1152,1728]{1,0:T(8,128)(2,1)}) %all-gather.36.cloned.1.call-update) | async-done | bytes 3981328 | tf_op jit(solution)/shard_map/all_gather | solution.py:41
  1053.0 10.8 all-reduce.1
  1063.8 39.3 %all-reduce = (f32[1728]{0:T(1024)}, f32[576]{0:T(1024)}, f32[1152]{0:T(1024)}, f32[1152]{0:T(1024)}, f32[1152]{0:T(1024)}) all-reduce(f32[1728]{0:T(1024)S(1)} %convert_reduce_fusion.5, f32[576]{0:T(1024)S(1)} %reshape.219, f32[1152]{0:T(1024)S(1)} %get-tuple-element.178, ...), channel_id=1, replica_groups=mesh['dp'=8,'tensor'=4] {'dp'}, use_global_device_ids=true, to_apply=%region_23.24 | all-reduce | flops 5760 | bytes 46080 | tf_op jit(solution)/shard_map/psum | solution.py:259
  1103.2 54.5 %reduce-scatter.29.cloned.1.call-done = f32[1152,144]{0,1:T(8,128)} async-done(((f32[1152,1152]{0,1:T(8,128)}), f32[1152,144]{0,1:T(8,128)}) %reduce-scatter.29.cloned.1.call-update) | async-done | bytes 663568 | tf_op jit(solution)/shard_map/reduce_scatter | solution.py:269
  1157.7 108.1 %reduce-scatter.27.cloned.1.call-done = f32[144,1152]{1,0:T(8,128)} async-done(((f32[1152,1152]{1,0:T(8,128)}), f32[144,1152]{1,0:T(8,128)}) %reduce-scatter.27.cloned.1.call-update) | async-done | bytes 663568 | tf_op jit(solution)/shard_map/reduce_scatter | solution.py:264
  1265.9 70.7 %reduce-scatter.25.cloned.1.call-done = f32[288,144]{0,1:T(8,128)} async-done(((f32[288,1152]{0,1:T(8,128)}), f32[288,144]{0,1:T(8,128)}) %reduce-scatter.25.cloned.1.call-update) | async-done | bytes 165904 | tf_op jit(solution)/shard_map/reduce_scatter | solution.py:268
  1336.5 90.6 %reduce-scatter.23.cloned.1.call-done = f32[144,864]{1,0:T(8,128)} async-done(((f32[1152,864]{1,0:T(8,128)}), f32[144,864]{1,0:T(8,128)}) %reduce-scatter.23.cloned.1.call-update) | async-done | bytes 497680 | tf_op jit(solution)/shard_map/reduce_scatter | solution.py:263
  1427.1 151.3 %reduce-scatter.21.cloned.1.call-done = f32[144,1728]{1,0:T(8,128)} async-done(((f32[1152,1728]{1,0:T(8,128)}), f32[144,1728]{1,0:T(8,128)}) %reduce-scatter.21.cloned.1.call-update) | async-done | bytes 995344 | tf_op jit(solution)/shard_map/reduce_scatter | solution.py:265
  (254 shorter events, 285.3 us)
Async XLA Ops:
  7.2 78.3 %copy-start.35 = (bf16[2,1152]{1,0:T(2,128)(2,1)S(1)}, bf16[2,1152]{1,0:T(2,128)(2,1)}, u32[]{:S(2)}) copy-start(bf16[2,1152]{1,0:T(2,128)(2,1)} %param.18) | copy-start | bytes 13828
  7.2 78.3 %all-gather.14.cloned.1.call-start = ((), (), s32[]{:S(2)}) async-start(), calls=%async_computation.10 | async-start | bytes 4644864 | tf_op jit(solution)/shard_map/all_gather | solution.py:41
  7.9 139.3 %all-gather.18.cloned.1.call-start = ((), (), s32[]{:S(2)}) async-start(), calls=%async_computation.12 | async-start | bytes 2322432 | tf_op jit(solution)/shard_map/all_gather | solution.py:39
  8.7 177.8 %all-gather.16.cloned.1.call-start = ((), (), s32[]{:S(2)}) async-start(), calls=%async_computation.11 | async-start | bytes 5898240 | tf_op jit(solution)/shard_map/all_gather | solution.py:51
  9.4 84.3 %copy-start.27 = (s32[512]{0:T(512)}, s32[512]{0:T(512)S(1)}, u32[]{:S(2)}) copy-start(s32[512]{0:T(512)S(1)} %add_select_fusion) | copy-start | bytes 6148
  11.0 88.5 %copy-start.39 = (f32[512]{0:T(512)}, f32[512]{0:T(512)S(1)}, u32[]{:S(2)}) copy-start(f32[512]{0:T(512)S(1)} %broadcast_multiply_fusion.5) | copy-start | bytes 6148
  11.4 88.0 %copy-start.43 = (f32[512]{0:T(512)}, f32[512]{0:T(512)S(1)}, u32[]{:S(2)}) copy-start(f32[512]{0:T(512)S(1)} %add_rsqrt_fusion.1) | copy-start | bytes 6148
  106.1 217.7 %reduce-scatter.13.cloned.1.call-start = ((), (), s32[]{:S(2)}) async-start(), calls=%async_computation.13 | async-start | bytes 5898240 | tf_op jit(solution)/shard_map/reduce_scatter | solution.py:182
  275.8 105.3 %all-gather.22.cloned.1.call-start = ((), (), s32[]{:S(2)}) async-start(), calls=%async_computation.15 | async-start | bytes 2985984 | tf_op jit(solution)/shard_map/all_gather | solution.py:40
  276.4 142.9 %all-gather.20.cloned.1.call-start = ((), (), s32[]{:S(2)}) async-start(), calls=%async_computation.14 | async-start | bytes 5898240 | tf_op jit(solution)/shard_map/all_gather | solution.py:51
  326.7 401.0 %copy-start.33 = (f32[512]{0:T(512)}, f32[512]{0:T(512)S(1)}, u32[]{:S(2)}) copy-start(f32[512]{0:T(512)S(1)} %broadcast_multiply_fusion.4) | copy-start | bytes 6148
  328.8 398.9 %copy-start.37 = (f32[512]{0:T(512)}, f32[512]{0:T(512)S(1)}, u32[]{:S(2)}) copy-start(f32[512]{0:T(512)S(1)} %add_rsqrt_fusion) | copy-start | bytes 6148
  334.5 142.2 %all-gather.28.cloned.1.call-start = ((), (), s32[]{:S(2)}) async-start(), calls=%async_computation.19 | async-start | bytes 2985984 | tf_op jit(solution)/shard_map/all_gather | solution.py:45
  335.2 179.8 %all-gather.26.cloned.1.call-start = ((), (), s32[]{:S(2)}) async-start(), calls=%async_computation.18 | async-start | bytes 5898240 | tf_op jit(solution)/shard_map/all_gather | solution.py:212
  336.0 236.5 %all-gather.30.cloned.1.call-start = ((), (), s32[]{:S(2)}) async-start(), calls=%async_computation.20 | async-start | bytes 2985984 | tf_op jit(solution)/shard_map/all_gather | solution.py:40
  336.7 291.6 %all-gather.24.cloned.1.call-start = ((), (), s32[]{:S(2)}) async-start(), calls=%async_computation.16 | async-start | bytes 2985984 | tf_op jit(solution)/shard_map/all_gather | solution.py:45
  337.3 340.2 %reduce-scatter.17.cloned.1.call-start = ((), (), s32[]{:S(2)}) async-start(), calls=%async_computation.21 | async-start | bytes 5898240 | tf_op jit(solution)/shard_map/reduce_scatter | solution.py:55
  583.4 144.3 %reduce-scatter.15.cloned.1.call-start = ((), (), s32[]{:S(2)}) async-start(), calls=%async_computation.17 | async-start | bytes 5898240 | tf_op jit(solution)/shard_map/reduce_scatter | solution.py:197
  641.4 131.9 %all-gather.32.cloned.1.call-start = ((), (), s32[]{:S(2)}) async-start(), calls=%async_computation.22 | async-start | bytes 5898240 | tf_op jit(solution)/shard_map/all_gather | solution.py:224
  642.0 85.7 %copy-start.31 = (f32[1152]{0:T(1024)}, f32[1152]{0:T(1024)S(1)}, u32[]{:S(2)}) copy-start(f32[1152]{0:T(1024)S(1)} %convert_element_type.147) | copy-start | bytes 13828
  735.6 132.1 %all-gather.34.cloned.1.call-start = ((), (), s32[]{:S(2)}) async-start(), calls=%async_computation.23 | async-start | bytes 2322432 | tf_op jit(solution)/shard_map/all_gather | solution.py:39
  768.2 157.8 %reduce-scatter.19.cloned.1.call-start = ((), (), s32[]{:S(2)}) async-start(), calls=%async_computation.24 | async-start | bytes 5898240 | tf_op jit(solution)/shard_map/reduce_scatter | solution.py:55
  877.9 112.3 %reduce-scatter.31.cloned.1.call-start = ((), (), s32[]{:S(2)}) async-start(), calls=%async_computation.31 | async-start | bytes 2211840
  945.1 104.4 %all-gather.36.cloned.1.call-start = ((), (), s32[]{:S(2)}) async-start(), calls=%async_computation.25 | async-start | bytes 4644864 | tf_op jit(solution)/shard_map/all_gather | solution.py:41
  945.7 212.0 %reduce-scatter.29.cloned.1.call-start = ((), (), s32[]{:S(2)}) async-start(), calls=%async_computation.30 | async-start | bytes 5971968 | tf_op jit(solution)/shard_map/reduce_scatter | solution.py:269
  960.4 305.4 %reduce-scatter.27.cloned.1.call-start = ((), (), s32[]{:S(2)}) async-start(), calls=%async_computation.29 | async-start | bytes 5971968 | tf_op jit(solution)/shard_map/reduce_scatter | solution.py:264
  973.4 363.1 %reduce-scatter.25.cloned.1.call-start = ((), (), s32[]{:S(2)}) async-start(), calls=%async_computation.28 | async-start | bytes 1990656 | tf_op jit(solution)/shard_map/reduce_scatter | solution.py:268
  980.3 446.8 %reduce-scatter.23.cloned.1.call-start = ((), (), s32[]{:S(2)}) async-start(), calls=%async_computation.27 | async-start | bytes 4644864 | tf_op jit(solution)/shard_map/reduce_scatter | solution.py:263
  990.1 588.3 %reduce-scatter.21.cloned.1.call-start = ((), (), s32[]{:S(2)}) async-start(), calls=%async_computation.26 | async-start | bytes 9289728 | tf_op jit(solution)/shard_map/reduce_scatter | solution.py:265
  998.9 54.0 %copy-start.41 = (f32[1152]{0:T(1024)S(1)}, f32[1152]{0:T(1024)}, u32[]{:S(2)}) copy-start(f32[1152]{0:T(1024)} %get-tuple-element.182) | copy-start | bytes 13828
  998.9 54.0 %copy-start.42 = (f32[1152]{0:T(1024)S(1)}, f32[1152]{0:T(1024)}, u32[]{:S(2)}) copy-start(f32[1152]{0:T(1024)} %get-tuple-element.180) | copy-start | bytes 13828
  998.9 64.9 %copy-start.45 = (f32[1152]{0:T(1024)S(1)}, f32[1152]{0:T(1024)}, u32[]{:S(2)}) copy-start(f32[1152]{0:T(1024)} %get-tuple-element.202) | copy-start | bytes 13828
  (47 other events, 360.7 us)
Sparse Core Ops, SparseCore 0:
  10.2 75.2 all-gather.13
  87.7 59.4 all-gather.17
  149.3 37.0 all-gather.15
  275.9 47.8 reduce-scatter.12
  326.0 55.0 all-gather.21
  383.1 36.0 all-gather.19
  421.6 55.0 all-gather.27
  478.9 36.0 all-gather.25
  517.4 55.0 all-gather.29
  574.7 53.5 all-gather.23
  631.0 46.3 reduce-scatter.16
  679.8 47.8 reduce-scatter.14
  735.8 37.4 all-gather.31
  775.5 48.9 all-gather.33
  877.9 47.9 reduce-scatter.18
  945.2 29.3 reduce-scatter.30
  976.9 72.5 all-gather.35
  1053.9 103.7 reduce-scatter.28
  1161.9 103.9 reduce-scatter.26
  1270.1 66.3 reduce-scatter.24
  1340.7 86.3 reduce-scatter.22
  1431.8 146.5 reduce-scatter.20
where the time goes:
time: 1590 us
  waiting for transfers between devices  1080 us (68%)
  matrix products  225 us (14%)
  blocking collectives  124 us (8%)
  other arithmetic  71.7 us (5%)
  local copies, waits for them, and re-layouts  64.6 us (4%)
    reduce_scatter x1, waiting for transfers between devices, shards(): lax.psum_scatter(grad_ada, 'dp', scatter_dimension=0, tiled=True)  151 us
    all_gather x2, waiting for transfers between devices, fetch_weights(): lax.all_gather(w_ada, 'dp', axis=0, tiled=True)  123 us
    reduce_scatter x1, waiting for transfers between devices, shards(): lax.psum_scatter(grad_fc1, 'dp', scatter_dimension=0, tiled=True)  108 us
    reduce_scatter x1, waiting for transfers between devices, shards(): lax.psum_scatter(grad_wqkv, 'dp', scatter_dimension=0, tiled=True)  90.6 us
    all_gather x2, waiting for transfers between devices, fetch_weights(): lax.all_gather(w_fc2, 'dp', axis=1, tiled=True)  90.3 us
    all_gather x2, waiting for transfers between devices, fetch_weights(): lax.all_gather(w_fc1, 'dp', axis=0, tiled=True)  85.2 us
    reduce_scatter x2, waiting for transfers between devices, sum_back(): lax.psum_scatter(row_term(jnp.int32(0), lax.axis_size('tensor') * row_cou...  83.5 us
    all_gather x2, waiting for transfers between devices, gather_rows(): return lax.all_gather(values, 'tensor', axis=0, tiled=True)  77.4 us
  transfers between devices with their start and end apart: 22, of which 20 were waited for; matrix products, arithmetic and copies ran while one was open for 14% of the time, Pallas kernels for 0%

commit v1 on v0

v1 whole, which is shorter than its diff:
```python
import jax
import jax.numpy as jnp
from jax import lax
from jax.experimental import pallas as pl
from jax.experimental.pallas import tpu as pltpu
from jax.sharding import PartitionSpec as P

HEAD_DIM = 72
SEQ = 1024

highest = lax.Precision.HIGHEST
root_two_pi = 0.7978845608028654
cubic_term = 0.044715
epsilon = 1e-06
bf16 = jnp.bfloat16
f32 = jnp.float32


def normalize(values):
    centre = values - jnp.mean(values, axis=-1, keepdims=True)
    inverse = lax.rsqrt(jnp.mean(centre * centre, axis=-1, keepdims=True) + epsilon)
    return (centre * inverse, inverse)


def norm_back(normed, inverse, grad_in):
    mean_grad = jnp.mean(grad_in, axis=-1, keepdims=True)
    mean_cross = jnp.mean(grad_in * normed, axis=-1, keepdims=True)
    return inverse * (grad_in - mean_grad - normed * mean_cross)


def gelu_parts(pre_act):
    tangent = jnp.tanh(root_two_pi * (pre_act + cubic_term * pre_act * pre_act * pre_act))
    activated = 0.5 * pre_act * (1.0 + tangent)
    gelu_slope = 0.5 * (1.0 + tangent) + 0.5 * pre_act * (1.0 - tangent * tangent) * root_two_pi * (
        1.0 + 3.0 * cubic_term * pre_act * pre_act
    )
    return (activated, gelu_slope)


def swap_cores(values):
    return lax.ppermute(values, "tensor", [(i, i ^ 1) for i in range(4)])


def swap_y(values):
    return lax.ppermute(values, "tensor", [(i, i ^ 2) for i in range(4)])


def swap_dp(values, bit):
    size = lax.axis_size("dp")
    return lax.ppermute(values, "dp", [(i, i ^ (1 << bit)) for i in range(size)])


def place_blocks(pieces, order_bits):
    half, rows, _ = pieces[0][0].shape
    widths = [first.shape[2] for first, _ in pieces]
    total = sum(widths)
    dp = 2 * half

    def rel_of(j, me):
        apart = j ^ me
        rel = 0
        for place, bit in enumerate(order_bits):
            rel = rel | (((apart >> bit) & 1) << place)
        return rel

    def kernel(me_ref, *refs):
        out_ref = refs[-1]
        rel = rel_of(pl.program_id(0), me_ref[0])

        @pl.when(rel < half)
        def _():
            at = 0
            for i, n in enumerate(widths):
                out_ref[0, :, at : at + n] = refs[2 * i][0]
                at += n

        @pl.when(rel >= half)
        def _():
            at = 0
            for i, n in enumerate(widths):
                out_ref[0, :, at : at + n] = refs[2 * i + 1][0]
                at += n

    def first_map(j, me_ref):
        rel = rel_of(j, me_ref[0])
        return (jnp.where(rel < half, rel, 0), 0, 0)

    def second_map(j, me_ref):
        rel = rel_of(j, me_ref[0])
        return (jnp.where(rel >= half, rel - half, 0), 0, 0)

    in_specs = []
    operands = []
    for (first, second), n in zip(pieces, widths):
        in_specs += [pl.BlockSpec((1, rows, n), first_map), pl.BlockSpec((1, rows, n), second_map)]
        operands += [first, second]
    me = lax.axis_index("dp").astype(jnp.int32).reshape(1)
    placed = pl.pallas_call(
        kernel,
        out_shape=jax.ShapeDtypeStruct((dp, rows, total), bf16),
        grid_spec=pltpu.PrefetchScalarGridSpec(
            num_scalar_prefetch=1,
            grid=(dp,),
            in_specs=in_specs,
            out_specs=pl.BlockSpec((1, rows, total), lambda j, me_ref: (j, 0, 0)),
        ),
        cost_estimate=pl.CostEstimate(flops=0, transcendentals=0, bytes_accessed=5 * dp * rows * total),
        name="place_blocks",
    )(me, *operands)
    return placed.reshape(dp * rows, total)


def gather_group(shard, cut):
    dp = lax.axis_size("dp")
    bits = dp.bit_length() - 1
    order_bits = list(range(bits - 1, -1, -1))
    got = shard[None]
    for bit in order_bits[:-1]:
        got = jnp.concatenate([got, swap_dp(got, bit)], axis=0)
    last = order_bits[-1]
    part_a, part_b = got[:, :, :cut], got[:, :, cut:]
    a_x = swap_dp(part_a, last)
    b_y = swap_y(part_b)
    a_both = swap_y(jnp.concatenate([part_a, a_x], axis=0))
    b_both = swap_dp(jnp.concatenate([part_b, b_y], axis=0), last)
    half = dp // 2
    pieces = [
        (part_a, a_x),
        (part_b, b_both[:half]),
        (a_both[:half], a_both[half:]),
        (b_y, b_both[half:]),
    ]
    return place_blocks(pieces, order_bits)


def scatter_half(own, other, y_first):
    dp = lax.axis_size("dp")
    me = lax.axis_index("dp")
    bits = dp.bit_length() - 1
    rows = own.shape[0] // dp
    n = own.shape[1]

    own = own.astype(f32)
    if y_first:
        total = own + swap_y(other.astype(bf16)).astype(f32)
        blocks = total.reshape(dp // 2, 2, rows, n)
        keep = lax.dynamic_index_in_dim(blocks, me & 1, 1, False)
        send = lax.dynamic_index_in_dim(blocks, 1 - (me & 1), 1, False)
        total = keep + swap_dp(send.astype(bf16), 0).astype(f32)
    else:
        both = jnp.stack([own, other.astype(f32)]).reshape(2, dp // 2, 2, rows, n)
        keep = lax.dynamic_index_in_dim(both, me & 1, 2, False)
        send = lax.dynamic_index_in_dim(both, 1 - (me & 1), 2, False)
        both = keep + swap_dp(send.astype(bf16), 0).astype(f32)
        total = both[0] + swap_y(both[1].astype(bf16)).astype(f32)
    for bit in range(1, bits):
        count = total.shape[0]
        blocks = total.reshape(count // 2, 2, rows, n)
        mine = (me >> bit) & 1
        keep = lax.dynamic_index_in_dim(blocks, mine, 1, False)
        send = lax.dynamic_index_in_dim(blocks, 1 - mine, 1, False)
        total = keep + swap_dp(send.astype(bf16), bit).astype(f32)
    return total[0]


def scatter_group(left, right, cut):
    n = right.shape[1] // 2

    def term(lo, hi, kind):
        out = lax.dot_general(
            left, right[:, lo:hi], (((0,), (0,)), ((), ())), preferred_element_type=f32
        )
        return out.astype(kind)

    part_a = scatter_half(term(0, cut, f32), term(n, n + cut, bf16), True)
    part_b = scatter_half(term(cut, n, f32), term(n + cut, 2 * n, f32), False)
    return jnp.concatenate([part_a, part_b], axis=1)


def dot_nt(left_rows, right_mat):
    return lax.dot_general(
        left_rows, right_mat, (((1,), (1,)), ((), ())), preferred_element_type=f32
    )


def dot_nn(left_rows, right_mat):
    return jnp.dot(left_rows, right_mat, preferred_element_type=f32)


def flip_halves(values):
    half = values.shape[0] // 2
    return jnp.concatenate([values[half:], values[:half]], axis=0)


def sum_cores_all(partial):
    mine = partial.astype(bf16)
    theirs = flip_halves(swap_cores(mine))
    return mine.astype(f32) + theirs.astype(f32)


def sum_cores_own(partial):
    mine = partial.astype(bf16)
    half = mine.shape[0] // 2
    theirs = swap_cores(mine[half:])
    return mine[:half].astype(f32) + theirs.astype(f32)


def attend(queries, keys_b, values_b):
    score_scale = queries.shape[-1] ** (-0.5)
    scores = (
        jnp.einsum("qhd,khd->hqk", queries, keys_b, preferred_element_type=f32) * score_scale
    )
    row_max = jnp.max(scores, axis=-1, keepdims=True)
    exponent = jnp.exp(scores - row_max)
    row_total = jnp.sum(exponent, axis=-1, keepdims=True)
    attn_probs = (exponent / row_total).astype(bf16)
    mixture = jnp.einsum("hqk,khd->qhd", attn_probs, values_b, preferred_element_type=f32)
    return (mixture.astype(bf16), (row_max + jnp.log(row_total))[..., 0])


def attend_back(queries, keys_b, values_b, grad_mix, logsum):
    score_scale = queries.shape[-1] ** (-0.5)
    scores = (
        jnp.einsum("qhd,khd->hqk", queries, keys_b, preferred_element_type=f32) * score_scale
    )
    attn_probs = jnp.exp(scores - logsum[..., None])
    grad_probs = jnp.einsum("qhd,khd->hqk", grad_mix, values_b, preferred_element_type=f32)
    row_inner = jnp.sum(grad_probs * attn_probs, axis=-1, keepdims=True)
    grad_scores = (attn_probs * (grad_probs - row_inner)).astype(bf16)
    grad_queries = (
        jnp.einsum("hqk,khd->qhd", grad_scores, keys_b, preferred_element_type=f32) * score_scale
    )
    grad_keys = (
        jnp.einsum("hqk,qhd->khd", grad_scores, queries, preferred_element_type=f32) * score_scale
    )
    grad_values = jnp.einsum(
        "hqk,qhd->khd", attn_probs.astype(bf16), grad_mix, preferred_element_type=f32
    )
    return jnp.stack([grad_queries, grad_keys, grad_values], axis=2).astype(bf16)


def shards(
    tokens_in,
    condition,
    w_ada,
    b_ada,
    w_qkv,
    b_qv,
    w_proj,
    b_proj,
    w_fc1,
    b_fc1,
    w_fc2,
    b_fc2,
    cotangent,
):
    tok_rows, width = tokens_in.shape
    head_size = HEAD_DIM
    dp_at = lax.axis_index("dp")
    y_at = lax.axis_index("tensor") // 2
    t_at = lax.axis_index("tensor")
    dp_size = lax.axis_size("dp")
    ada_rows, ada_cols = w_ada.shape
    n_qkv, n_proj, n_fc1, n_fc2 = w_qkv.shape[1], w_proj.shape[0], w_fc1.shape[1], w_fc2.shape[0]

    tokens_all = jnp.concatenate([tokens_in, swap_cores(tokens_in)], axis=0)
    cot_all = jnp.concatenate([cotangent, swap_cores(cotangent)], axis=0)
    bias_mine = jnp.concatenate([b_qv, b_fc1])
    bias_theirs = swap_y(bias_mine)
    n_bqv = b_qv.shape[0]

    wqkv = gather_group(w_qkv, 384)
    group_two = gather_group(jnp.concatenate([w_proj.T, w_fc1], axis=1), 672)
    n_two = n_proj + n_fc1
    wproj_t = jnp.concatenate([group_two[:, :n_proj], group_two[:, n_two : n_two + n_proj]], axis=1)
    wfc1 = jnp.concatenate([group_two[:, n_proj:n_two], group_two[:, n_two + n_proj :]], axis=1)
    wfc2_t = gather_group(w_fc2.T, 512)

    cond_all = lax.all_gather(condition, "dp", axis=0, tiled=True).astype(f32)
    silu_all = (cond_all * jax.nn.sigmoid(cond_all)).astype(bf16)
    silu_mine = lax.dynamic_slice_in_dim(silu_all, dp_at * ada_rows, ada_rows, 1)
    mod_part = jnp.dot(silu_mine, w_ada, preferred_element_type=f32)
    mod_cols = lax.psum_scatter(mod_part, "dp", scatter_dimension=0, tiled=True) + b_ada.astype(f32)
    modulation = lax.all_gather(mod_cols, "tensor", axis=1, tiled=True)
    mod_row = lax.dynamic_slice_in_dim(modulation, y_at, 1, 0)
    shift_attn, scale_attn, gate_attn, shift_mlp, scale_mlp, gate_mlp = jnp.split(mod_row, 6, axis=1)

    input_vals = tokens_all.astype(f32)
    normed_one, inverse_one = normalize(input_vals)
    attn_in = (normed_one * (1.0 + scale_attn) + shift_attn).astype(bf16)
    heads = 2 * n_qkv // (3 * head_size)
    rows = 2 * tok_rows
    bias_qv = jnp.concatenate([bias_mine[:n_bqv], bias_theirs[:n_bqv]]).astype(f32).reshape(heads, 2, head_size)
    projected = dot_nn(attn_in, wqkv).reshape(rows, heads, 3, head_size)
    queries = (projected[:, :, 0] + bias_qv[:, 0]).astype(bf16)
    keys_b = projected[:, :, 1].astype(bf16)
    values_b = (projected[:, :, 2] + bias_qv[:, 1]).astype(bf16)
    mixture, logsum = attend(queries, keys_b, values_b)
    mix_rows = mixture.reshape(rows, heads * head_size)
    attn_out = sum_cores_all(dot_nt(mix_rows, wproj_t)) + b_proj.astype(f32)
    middle = input_vals + gate_attn * attn_out

    normed_two, inverse_two = normalize(middle)
    mlp_in = (normed_two * (1.0 + scale_mlp) + shift_mlp).astype(bf16)
    bias_one = jnp.concatenate([bias_mine[n_bqv:], bias_theirs[n_bqv:]]).astype(f32)
    pre_act = dot_nn(mlp_in, wfc1) + bias_one
    activated, gelu_slope = gelu_parts(pre_act)
    act_rows = activated.astype(bf16)
    mlp_out = sum_cores_own(dot_nt(act_rows, wfc2_t)) + b_fc2.astype(f32)
    result = middle[:tok_rows] + gate_mlp * mlp_out

    grad_out = cot_all.astype(f32)
    grad_mlp = (gate_mlp * grad_out).astype(bf16)
    d_gate_mlp = grad_out[:tok_rows] * mlp_out
    grad_act = dot_nn(grad_mlp, wfc2_t)
    grad_pre = (grad_act * gelu_slope).astype(bf16)
    owned_fc2 = scatter_group(grad_mlp, act_rows, 512).T
    owned_fc1 = scatter_group(mlp_in, grad_pre, 512)
    grad_mlp_in = sum_cores_all(dot_nt(grad_pre, wfc1))
    d_scale_mlp = grad_mlp_in * normed_two
    grad_middle = grad_out + norm_back(normed_two, inverse_two, grad_mlp_in * (1.0 + scale_mlp))

    grad_attn = (gate_attn * grad_middle).astype(bf16)
    d_gate_attn = grad_middle * attn_out
    grad_mix = dot_nn(grad_attn, wproj_t).astype(bf16).reshape(rows, heads, head_size)
    owned_proj = scatter_group(grad_attn, mix_rows, 128).T
    grad_qkv = attend_back(queries, keys_b, values_b, grad_mix, logsum).reshape(rows, 2 * n_qkv)
    owned_qkv = scatter_group(attn_in, grad_qkv, 384)
    grad_attn_in = sum_cores_own(dot_nt(grad_qkv, wqkv))
    d_scale_attn = grad_attn_in * normed_one[:tok_rows]
    grad_tokens = grad_middle[:tok_rows] + norm_back(
        normed_one[:tok_rows], inverse_one[:tok_rows], grad_attn_in * (1.0 + scale_attn)
    )

    own = [
        jnp.sum(term[:tok_rows], axis=0)
        for term in (grad_attn_in, d_scale_attn, d_gate_attn, grad_mlp_in, d_scale_mlp, d_gate_mlp)
    ]
    mod_sums = jnp.concatenate(own)
    mod_sums = mod_sums + swap_cores(mod_sums)
    by_rank = mod_sums.reshape(4, ada_cols)
    mod_keep = lax.dynamic_index_in_dim(by_rank, t_at, 0, True)
    mod_got = swap_y(lax.dynamic_index_in_dim(by_rank, t_at ^ 2, 0, True))
    first = jnp.where(y_at == 0, mod_keep, mod_got)
    second = jnp.where(y_at == 0, mod_got, mod_keep)
    grad_mod = lax.all_gather(jnp.concatenate([first, second], axis=0), "dp", axis=0, tiled=True)
    owned_ada = lax.dot_general(
        silu_mine.astype(f32), grad_mod, (((0,), (0,)), ((), ())), precision=highest
    )
    grad_ba = jnp.sum(grad_mod, axis=0)
    silu_part = lax.dot_general(
        grad_mod, w_ada.astype(f32), (((1,), (1,)), ((), ())), precision=highest
    )
    silu_place = lax.dynamic_update_slice(
        jnp.zeros((silu_part.shape[0], width), f32), silu_part, (0, dp_at * ada_rows)
    )

    qkv_sums = jnp.sum(grad_qkv.astype(f32), axis=0).reshape(2, heads // 2, 3, head_size)
    bqv_two = jnp.stack([qkv_sums[:, :, 0], qkv_sums[:, :, 2]], axis=2).reshape(2, n_bqv)
    b1_two = jnp.sum(grad_pre.astype(f32), axis=0).reshape(2, n_fc1)
    two = jnp.concatenate([bqv_two, b1_two], axis=1)
    bias_place = lax.dynamic_update_slice(jnp.zeros((4, two.shape[1]), f32), two[:1], (t_at, 0))
    bias_place = lax.dynamic_update_slice(bias_place, two[1:], (t_at ^ 2, 0))
    grad_bo = jnp.sum(grad_attn[:tok_rows].astype(f32), axis=0)
    grad_b2 = jnp.sum(grad_mlp[:tok_rows].astype(f32), axis=0)
    silu_total, bias_total, grad_bo, grad_b2 = lax.psum(
        (silu_place, bias_place, grad_bo, grad_b2), ("dp", "tensor")
    )
    bias_own = lax.dynamic_index_in_dim(bias_total, t_at, 0, False)
    cond_vals = condition.astype(f32)
    cond_sigmoid = jax.nn.sigmoid(cond_vals)
    latents = condition.shape[0]
    grad_silu = lax.dynamic_slice_in_dim(silu_total, dp_at * latents, latents, 0)
    grad_condition = grad_silu * cond_sigmoid * (1.0 + cond_vals * (1.0 - cond_sigmoid))
    return (
        result.astype(bf16),
        grad_tokens,
        grad_condition,
        owned_ada,
        grad_ba,
        owned_qkv,
        bias_own[:n_bqv],
        owned_proj,
        grad_bo,
        owned_fc1,
        bias_own[n_bqv:],
        owned_fc2,
        grad_b2,
    )


def solution(mesh):
    placed = (
        P(("dp", "tensor"), None),
        P("dp", None),
        P("dp", "tensor"),
        P("tensor"),
        P("dp", "tensor"),
        P("tensor"),
        P("tensor", "dp"),
        P(),
        P("dp", "tensor"),
        P("tensor"),
        P("tensor", "dp"),
        P(),
        P(("dp", "tensor"), None),
    )
    return jax.shard_map(
        shards,
        mesh=mesh,
        in_specs=placed,
        out_specs=(
            P(("dp", "tensor"), None),
            P(("dp", "tensor"), None),
            P("dp", None),
            P("dp", "tensor"),
            P("tensor"),
            P("dp", "tensor"),
            P("tensor"),
            P("tensor", "dp"),
            P(),
            P("dp", "tensor"),
            P("tensor"),
            P("tensor", "dp"),
            P(),
        ),
        check_vma=False,
    )
```

time: 1590 us -> 986 us (0.62)
  waiting for transfers between devices: 1080 us -> 393 us
  starting transfers between devices: 2.35 us -> 65.5 us
  other arithmetic: 71.7 us -> 118 us
  Pallas kernels: 0 us -> 26.2 us
  matrix products: 225 us -> 200 us
  local copies, waits for them, and re-layouts: 64.6 us -> 47.6 us
    reduce_scatter x9 -> x0, waiting for transfers between devices: 653 us -> none  [the longest x1 151 us: shards(): lax.psum_scatter(grad_ada, 'dp', scatter_dimension=0, tiled=True)]
    all_gather x12 -> x0, waiting for transfers between devices: 424 us -> none  [the longest x2 123 us: fetch_weights(): lax.all_gather(w_ada, 'dp', axis=0, tiled=True)]
    ppermute x0 -> x59, waiting for transfers between devices: none -> 196 us  [the longest x36 131 us: swap_dp(): return lax.ppermute(values, 'dp', [(i, i ^ 1 << bit) for i in range(size)])]
    psum x0 -> x1, waiting for transfers between devices: none -> 114 us  [shards(): lax.psum((silu_place, bias_place, grad_bo, grad_b2), ('dp', 'tensor'))]
    unnamed x23 -> x3, waiting for transfers between devices: 5.3 us -> 83.5 us
    ppermute x0 -> x59, starting transfers between devices: none -> 65.4 us  [the longest x36 41.9 us: swap_dp(): return lax.ppermute(values, 'dp', [(i, i ^ 1 << bit) for i in range(size)])]
    dot_general x31, matrix products: 225 us -> 196 us  [the longest x14 37.8 us: term(): lax.dot_general(left, right[:, lo:hi], (((0,), (0,)), ((), ())), preferre...]
    convert_element_type x9 -> x14, other arithmetic: 21.7 us -> 49.9 us  [the longest x1 28.2 us: attend_back(): grad_scores = (attn_probs * (grad_probs - row_inner)).astype(bf16)]
  transfers between devices with their start and end apart: 22 -> 61, of which waited for: 20 -> 29; matrix products, arithmetic and copies ran while one was open for 14% -> 30% of each run, Pallas kernels for 0% -> 3%
where the time goes in v1:
time: 986 us; the launch traced here: 981 us
  waiting for transfers between devices  393 us (40%)
  matrix products  200 us (20%)
  other arithmetic  118 us (12%)
  blocking collectives  114 us (12%)
  starting transfers between devices  65.5 us (7%)
  local copies, waits for them, and re-layouts  47.6 us (5%)
  Pallas kernels  26.2 us (3%)
  between operations  16.7 us (2%)
    ppermute x36, waiting for transfers between devices, swap_dp(): return lax.ppermute(values, 'dp', [(i, i ^ 1 << bit) for i in range(size)])  131 us
    psum x1, waiting for transfers between devices, shards(): lax.psum((silu_place, bias_place, grad_bo, grad_b2), ('dp', 'tensor'))  114 us
    unnamed x3, waiting for transfers between devices  83.5 us
    ppermute x16, waiting for transfers between devices, swap_y(): return lax.ppermute(values, 'tensor', [(i, i ^ 2) for i in range(4)])  64.3 us
    psum x1, blocking collectives, shards(): lax.psum((silu_place, bias_place, grad_bo, grad_b2), ('dp', 'tensor'))  46.8 us
    ppermute x36, starting transfers between devices, swap_dp(): return lax.ppermute(values, 'dp', [(i, i ^ 1 << bit) for i in range(size)])  41.9 us
    dot_general x14, matrix products, term(): lax.dot_general(left, right[:, lo:hi], (((0,), (0,)), ((), ())), preferre...  37.8 us
    dot_general x4, matrix products, dot_nn(): return jnp.dot(left_rows, right_mat, preferred_element_type=f32)  35.1 us
  transfers between devices with their start and end apart: 61, of which 29 were waited for; matrix products, arithmetic and copies ran while one was open for 30% of the time, Pallas kernels for 3%

profile of v1, /device:TPU:0, one launch (start us, length us, event | category | flops | bytes accessed | tf_op | source)
XLA Modules:
  0.0 980.5 jit_solution(13944173487136557791)
XLA Ops:
  11.1 31.2 %all-gather = bf16[8,2,1152]{2,1,0:T(2,128)(2,1)S(1)} all-gather(bf16[1,2,1152]{2,1,0:T(2,128)(2,1)} %bitcast.371), channel_id=1, replica_groups=mesh['dp'=8,'tensor'=4] {'dp'}, dimensions={0}, use_global_device_ids=true | all-gather | bytes 41472 | tf_op jit(solution)/shard_map/all_gather | solution.py:279
  54.5 83.4 %all-reduce.7.cloned.1.call-done = f32[16,1728]{1,0:T(8,128)} async-done(((f32[16,1728]{1,0:T(8,128)}), f32[16,1728]{1,0:T(8,128)}) %all-reduce.7.cloned.1.call-update) | async-done | bytes 110608
  149.4 9.5 collective-permute-done.2
  161.4 11.7 %collective-permute-done.16 = bf16[2,144,1152]{2,1,0:T(8,128)(2,1)S(1)} collective-permute-done((bf16[2,144,1152]{2,1,0:T(8,128)(2,1)S(1)}, bf16[2,144,1152]{2,1,0:T(8,128)(2,1)S(1)}, u32[]{:S(2)}, u32[]{:S(2)}) %collective-permute-start.16) | collective-permute-done | bytes 663584 | tf_op jit(solution)/shard_map/ppermute | solution.py:50
  207.9 7.9 collective-permute-done.10.refs_1_
  226.6 16.5 %collective-permute-done.11.refs_6_ = bf16[4,144,768]{2,1,0:T(8,128)(2,1)S(1)} collective-permute-done((bf16[4,144,768]{2,1,0:T(8,128)(2,1)S(1)}, bf16[4,144,768]{2,1,0:T(8,128)(2,1)S(1)}, u32[]{:S(2)}, u32[]{:S(2)}) %collective-permute-start.11) | collective-permute-done | bytes 884768 | tf_op jit(solution)/shard_map/ppermute | solution.py:45
  247.0 7.8 place_blocks.3
  268.6 13.2 %multiply_reduce_fusion.1 = (f32[8,1024]{1,0:T(8,128)S(1)}, f32[8,1024,1024]{1,2,0:T(8,128)}) fusion(f32[1024,8,3,72]{0,3,2,1:T(8,128)S(1)} %fusion.41, f32[8,72]{1,0:T(8,128)S(1)} %bitcast.360), kind=kOutput, calls=%fused_computation.6 | convolution fusion | flops 1226498048 | bytes 38309888 | tf_op jit(solution)/shard_map/qhd,khd->hqk/dot_general | solution.py:211
  281.8 13.5 %fusion = f32[8,1024]{1,0:T(8,128)S(1)} fusion(f32[8,1024,1024]{1,2,0:T(8,128)} %get-tuple-element.75, f32[8,1024]{1,0:T(8,128)S(1)} %get-tuple-element.74), kind=kLoop, calls=%fused_computation.5 | loop fusion | flops 25157632 | bytes 33619968 | tf_op jit(solution)/shard_map/reduce_sum | solution.py:215
  295.4 16.2 %fusion.49 = bf16[8,72,1024]{2,1,0:T(8,128)(2,1)} fusion(f32[8,1024,1024]{1,2,0:T(8,128)} %get-tuple-element.75, f32[8,1024]{1,0:T(8,128)S(1)} %fusion, f32[8,1024]{1,0:T(8,128)S(1)} %get-tuple-element.74, f32[1024,8,3,72]{0,3,2,1:T(8,128)} %copy-done.2, f32[8,72]{1,0:T(8,128)S(1)} %bitcast.363), kind=kOutput, calls=%fused_computation.123 | convolution fusion | flops 1243283456 | bytes 37161216 | tf_op jit(solution)/shard_map/hqk,khd->qhd/dot_general | solution.py:217
  317.1 10.1 %place_blocks.4 = bf16[8,144,2880]{2,1,0:T(8,128)(2,1)} custom-call(s32[1]{0:T(128)} %bitcast.6.me_ref, bf16[4,144,672]{2,1,0:T(8,128)(2,1)} %copy-done.11, bf16[4,144,672]{2,1,0:T(8,128)(2,1)} %copy-done.32, bf16[4,144,768]{2,1,0:T(8,128)(2,1)} %copy-done.10, bf16[4,144,768]{2,1,0:T(8,128)(2,1)} %get-tuple-element.55.refs_3_, ...), custom_call_target="tpu_custom_call" | custom-call | bytes 16588800 | tf_op jit(solution)/shard_map/place_blocks/pallas_call | solution.py:98
  339.0 8.3 place_blocks.5
  366.4 10.4 %multiply_convert_fusion.1 = (bf16[1024,2304]{1,0:T(8,128)(2,1)S(1)}, f32[1024,2304]{1,0:T(8,128)}) fusion(f32[2304]{0:T(1024)S(1)} %maximum_convert_fusion.2, bf16[1024,1152]{1,0:T(8,128)(2,1)S(1)} %get-tuple-element.34, bf16[1152,1152]{1,0:T(8,128)(2,1)S(1)} %get-tuple-element.40, bf16[1152,1152]{1,0:T(8,128)(2,1)S(1)} %get-tuple-element.39), kind=kOutput, calls=%fused_computation.20 | convolution fusion | flops 5470027776 | bytes 21832704 | tf_op jit(solution)/shard_map/dot_general | solution.py:187
  376.8 14.5 %convert_reduce_fusion = (f32[2304]{0:T(1024)S(1)}, bf16[1024,2304]{1,0:T(8,128)(2,1)S(1)}) fusion(f32[1024,2304]{1,0:T(8,128)} %get-tuple-element.77, f32[2304]{0:T(1024)S(1)} %maximum_convert_fusion.2, bf16[1024,1152]{1,0:T(8,128)(2,1)S(1)} %copy-done.15, bf16[1152,2304]{1,0:T(8,128)(2,1)S(1)} %bitcast.314), kind=kOutput, calls=%fused_computation.19 | convolution fusion | flops 5487720448 | bytes 21841920 | tf_op jit(solution)/shard_map/dot_general | solution.py:187
  401.3 7.7 convolution_convert_fusion.1
  430.8 16.8 %collective-permute-done.51 = bf16[1152,512]{1,0:T(8,128)(2,1)S(1)} collective-permute-done((bf16[1152,512]{1,0:T(8,128)(2,1)}, bf16[1152,512]{1,0:T(8,128)(2,1)S(1)}, u32[]{:S(2)}, u32[]{:S(2)}) %collective-permute-start.51) | collective-permute-done | bytes 1179680 | tf_op jit(solution)/shard_map/ppermute | solution.py:45
  451.3 21.4 %collective-permute-done.43 = bf16[1152,512]{1,0:T(8,128)(2,1)} collective-permute-done((bf16[1152,512]{1,0:T(8,128)(2,1)}, bf16[1152,512]{1,0:T(8,128)(2,1)}, u32[]{:S(2)}, u32[]{:S(2)}) %collective-permute-start.43) | collective-permute-done | bytes 1179680 | tf_op jit(solution)/shard_map/ppermute | solution.py:45
  481.8 15.1 %collective-permute-done.55 = bf16[2,4,144,640]{3,2,1,0:T(8,128)(2,1)S(1)} collective-permute-done((bf16[2,4,144,640]{3,2,1,0:T(8,128)(2,1)S(1)}, bf16[2,4,144,640]{3,2,1,0:T(8,128)(2,1)S(1)}, u32[]{:S(2)}, u32[]{:S(2)}) %collective-permute-start.55) | collective-permute-done | bytes 1474592 | tf_op jit(solution)/shard_map/ppermute | solution.py:50
  498.8 10.7 %collective-permute-done.52 = bf16[4,144,512]{2,1,0:T(8,128)(2,1)S(1)} collective-permute-done((bf16[4,144,512]{2,1,0:T(8,128)(2,1)S(1)}, bf16[4,144,512]{2,1,0:T(8,128)(2,1)S(1)}, u32[]{:S(2)}, u32[]{:S(2)}) %collective-permute-start.52) | collective-permute-done | bytes 589856 | tf_op jit(solution)/shard_map/ppermute | solution.py:50
  510.5 11.3 %collective-permute-done.44 = bf16[4,144,512]{2,1,0:T(8,128)(2,1)S(1)} collective-permute-done((bf16[4,144,512]{2,1,0:T(8,128)(2,1)S(1)}, bf16[4,144,512]{2,1,0:T(8,128)(2,1)S(1)}, u32[]{:S(2)}, u32[]{:S(2)}) %collective-permute-start.44) | collective-permute-done | bytes 589856 | tf_op jit(solution)/shard_map/ppermute | solution.py:50
  524.0 9.8 %collective-permute-done.45 = bf16[2,144,512]{2,1,0:T(8,128)(2,1)S(1)} collective-permute-done((bf16[2,144,512]{2,1,0:T(8,128)(2,1)S(1)}, bf16[2,144,512]{2,1,0:T(8,128)(2,1)S(1)}, u32[]{:S(2)}, u32[]{:S(2)}) %collective-permute-start.45) | collective-permute-done | bytes 294944 | tf_op jit(solution)/shard_map/ppermute | solution.py:50
  564.0 15.5 %fusion.46 = bf16[1024,8,1,72]{0,3,1,2:T(8,128)(2,1)} fusion(bf16[1024,8,72]{0,2,1:T(8,128)(2,1)} %bitcast.320, f32[8,1024,1024]{1,2,0:T(8,128)} %get-tuple-element.75, f32[8,1024]{1,0:T(8,128)S(1)} %log_add_fusion), kind=kOutput, calls=%fused_computation.121 | convolution fusion | flops 1233125376 | bytes 35946496 | tf_op jit(solution)/shard_map/hqk,qhd->khd/dot_general | solution.py:236
  579.5 23.7 %multiply_reduce_fusion = (f32[8,1024]{1,0:T(8,128)S(1)}, f32[8,1024,1024]{1,2,0:T(8,128)}) fusion(f32[8,1024,1024]{1,2,0:T(8,128)} %get-tuple-element.75, f32[8,1024]{1,0:T(8,128)S(1)} %log_add_fusion, bf16[1024,8,72]{0,2,1:T(8,128)(2,1)} %bitcast.321, f32[1024,8,3,72]{0,3,2,1:T(8,128)} %copy-done.2, f32[8,72]{1,0:T(8,128)S(1)} %bitcast.364), kind=kOutput, calls=%fused_computation.1 | convolution fusion | flops 1242685440 | bytes 70715648 | tf_op jit(solution)/shard_map/qhd,khd->hqk/dot_general | solution.py:227
  603.2 28.2 %multiply_convert_fusion = bf16[8,1024,1024]{1,2,0:T(8,128)(2,1)} fusion(f32[8,1024,1024]{1,2,0:T(8,128)} %get-tuple-element.79, f32[8,1024,1024]{1,2,0:T(8,128)} %get-tuple-element.75, f32[8,1024]{1,0:T(8,128)S(1)} %get-tuple-element.78, f32[8,1024]{1,0:T(8,128)S(1)} %log_add_fusion), kind=kLoop, calls=%fused_computation | loop fusion | flops 41943040 | bytes 83951616 | tf_op jit(solution)/shard_map/convert_element_type | solution.py:229
  631.5 12.7 %multiply_bitcast_fusion = bf16[1024,8,1,72]{0,3,1,2:T(8,128)(2,1)} fusion(bf16[8,1024,1024]{1,2,0:T(8,128)(2,1)} %multiply_convert_fusion, f32[1024,8,3,72]{0,3,2,1:T(8,128)} %copy-done.2, f32[8,72]{1,0:T(8,128)S(1)} %bitcast.361), kind=kOutput, calls=%fused_computation.110 | convolution fusion | flops 1210318848 | bytes 20318464 | tf_op jit(solution)/shard_map/hqk,qhd->khd/dot_general | solution.py:234
  644.2 9.7 multiply_bitcast_fusion.1
  668.9 46.8 %all-reduce.1 = (f32[4,1728]{1,0:T(4,128)S(1)}, f32[1152]{0:T(1024)}, f32[1152]{0:T(1024)}) all-reduce(f32[4,1728]{1,0:T(4,128)S(1)} %dynamic_update_slice.11, f32[1152]{0:T(1024)S(1)} %convert_reduce_fusion.4, f32[1152]{0:T(1024)S(1)} %copy-done.68), channel_id=1, replica_groups=mesh['dp'=8,'tensor'=4] {'dp','tensor'}, use_global_device_ids=true, to_apply=%region_22.23 | all-reduce | flops 9216 | bytes 73728 | tf_op jit(solution)/shard_map/psum | solution.py:366
  716.9 8.4 convolution_convert_fusion.2
  741.9 9.3 collective-permute-done.50
  755.0 8.6 collective-permute-done.36
  793.9 30.6 %all-gather.2 = f32[8,2,1728]{2,1,0:T(2,128)S(1)} all-gather(f32[1,2,1728]{2,1,0:T(2,128)S(1)} %maximum_bitcast_fusion.3), channel_id=1, replica_groups=mesh['dp'=8,'tensor'=4] {'dp'}, dimensions={0}, use_global_device_ids=true | all-gather | bytes 124416 | tf_op jit(solution)/shard_map/all_gather | solution.py:346
  830.9 113.8 %all-reduce.5.cloned.1.call-done = f32[16,1152]{1,0:T(8,128)} async-done(((f32[16,1152]{1,0:T(8,128)}), f32[16,1152]{1,0:T(8,128)}) %all-reduce.5.cloned.1.call-update) | async-done | bytes 73744 | tf_op jit(solution)/shard_map/psum | solution.py:366
  (487 shorter events, 309.6 us)
Async XLA Ops:
  7.2 130.7 %all-reduce.7.cloned.1.call-start = ((), (), s32[]{:S(2)}) async-start(), calls=%async_computation.1 | async-start | bytes 229376
  8.1 44.9 %collective-permute-start.7 = (bf16[1728]{0:T(1024)(128)(2,1)S(1)}, bf16[1728]{0:T(1024)(128)(2,1)S(1)}, u32[]{:S(2)}, u32[]{:S(2)}) collective-permute-start(bf16[1728]{0:T(1024)(128)(2,1)S(1)} %pad_maximum_fusion.27), channel_id=1, source_target_pairs={{0,2},{1,3},{2,0},{3,1},{4,6},{5,7},{6,4},{7,5},{8,10},{9,11},{10,... | collective-permute-start | bytes 10376 | tf_op jit(solution)/shard_map/ppermute | solution.py:45
  43.3 901.4 %all-reduce.5.cloned.1.call-start = ((), (), s32[]{:S(2)}) async-start(), calls=%async_computation | async-start | bytes 147456 | tf_op jit(solution)/shard_map/psum | solution.py:366
  43.3 100.8 %collective-permute-start.1 = (bf16[1,144,864]{2,1,0:T(8,128)(2,1)}, bf16[1,144,864]{2,1,0:T(8,128)(2,1)S(1)}, u32[]{:S(2)}, u32[]{:S(2)}) collective-permute-start(bf16[1,144,864]{2,1,0:T(8,128)(2,1)} %bitcast.346), channel_id=1, source_target_pairs={{0,16},{4,20},{8,24},{12,28},{16,0},{20,4},{24,8},{28,12},{1,17},{... | collective-permute-start | bytes 746504 | tf_op jit(solution)/shard_map/ppermute | solution.py:50
  43.4 102.5 %collective-permute-start.15 = (bf16[1,144,1152]{2,1,0:T(8,128)(2,1)}, bf16[1,144,1152]{2,1,0:T(8,128)(2,1)S(1)}, u32[]{:S(2)}, u32[]{:S(2)}) collective-permute-start(bf16[1,144,1152]{2,1,0:T(8,128)(2,1)} %bitcast.340), channel_id=1, source_target_pairs={{0,16},{4,20},{8,24},{12,28},{16,0},{20,4},{24,8},{28,12},{1,17},{... | collective-permute-start | bytes 995336 | tf_op jit(solution)/shard_map/ppermute | solution.py:50
  47.5 99.2 %collective-permute-start.8 = (bf16[1,144,1440]{2,1,0:T(8,128)(2,1)S(1)}, bf16[1,144,1440]{2,1,0:T(8,128)(2,1)}, u32[]{:S(2)}, u32[]{:S(2)}) collective-permute-start(bf16[1,144,1440]{2,1,0:T(8,128)(2,1)S(1)} %maximum_bitcast_fusion.1), channel_id=1, source_target_pairs={{0,16},{4,20},{8,24},{12,28},{16,0},{20,4},{24,8},{28,12},{1,17},{... | collective-permute-start | bytes 1244168 | tf_op jit(solution)/shard_map/ppermute | solution.py:50
  47.7 136.2 %collective-permute-start.22 = (bf16[512,1152]{1,0:T(8,128)(2,1)}, bf16[512,1152]{1,0:T(8,128)(2,1)}, u32[]{:S(2)}, u32[]{:S(2)}) collective-permute-start(bf16[512,1152]{1,0:T(8,128)(2,1)} %param.25), channel_id=1, source_target_pairs={{0,1},{1,0},{2,3},{3,2},{4,5},{5,4},{6,7},{7,6},{8,9},{9,8},{10,11... | collective-permute-start | bytes 3538952 | tf_op jit(solution)/shard_map/ppermute | solution.py:41
  53.1 123.8 %collective-permute-start = (bf16[512,1152]{1,0:T(8,128)(2,1)}, bf16[512,1152]{1,0:T(8,128)(2,1)S(1)}, u32[]{:S(2)}, u32[]{:S(2)}) collective-permute-start(bf16[512,1152]{1,0:T(8,128)(2,1)} %param.13), channel_id=1, source_target_pairs={{0,1},{1,0},{2,3},{3,2},{4,5},{5,4},{6,7},{7,6},{8,9},{9,8},{10,11... | collective-permute-start | bytes 3538952 | tf_op jit(solution)/shard_map/ppermute | solution.py:41
  147.8 43.7 %collective-permute-start.9 = (bf16[2,144,1440]{2,1,0:T(8,128)(2,1)S(1)}, bf16[2,144,1440]{2,1,0:T(8,128)(2,1)S(1)}, u32[]{:S(2)}, u32[]{:S(2)}) collective-permute-start(bf16[2,144,1440]{2,1,0:T(8,128)(2,1)S(1)} %pad_maximum_fusion.12), channel_id=1, source_target_pairs={{0,8},{4,12},{8,0},{12,4},{16,24},{20,28},{24,16},{28,20},{1,9},{5... | collective-permute-start | bytes 2488328 | tf_op jit(solution)/shard_map/ppermute | solution.py:50
  194.6 48.5 %collective-permute-start.11 = (bf16[4,144,768]{2,1,0:T(8,128)(2,1)S(1)}, bf16[4,144,768]{2,1,0:T(8,128)(2,1)S(1)}, u32[]{:S(2)}, u32[]{:S(2)}) collective-permute-start(bf16[4,144,768]{2,1,0:T(8,128)(2,1)S(1)} %slice.341.refs_2_), channel_id=1, source_target_pairs={{0,2},{1,3},{2,0},{3,1},{4,6},{5,7},{6,4},{7,5},{8,10},{9,11},{10,... | collective-permute-start | bytes 2654216 | tf_op jit(solution)/shard_map/ppermute | solution.py:45
  196.3 49.7 %collective-permute-start.5 = (bf16[8,144,480]{2,1,0:T(8,128)(2,1)S(1)}, bf16[8,144,480]{2,1,0:T(8,128)(2,1)S(1)}, u32[]{:S(2)}, u32[]{:S(2)}) collective-permute-start(bf16[8,144,480]{2,1,0:T(8,128)(2,1)S(1)} %pad_maximum_fusion.9), channel_id=1, source_target_pairs={{0,4},{4,0},{8,12},{12,8},{16,20},{20,16},{24,28},{28,24},{1,5},{5... | collective-permute-start | bytes 3317768 | tf_op jit(solution)/shard_map/ppermute | solution.py:50
  205.2 128.8 %collective-permute-start.20 = (bf16[8,144,512]{2,1,0:T(8,128)(2,1)}, bf16[8,144,512]{2,1,0:T(8,128)(2,1)}, u32[]{:S(2)}, u32[]{:S(2)}) collective-permute-start(bf16[8,144,512]{2,1,0:T(8,128)(2,1)} %pad_maximum_fusion.10), channel_id=1, source_target_pairs={{0,2},{1,3},{2,0},{3,1},{4,6},{5,7},{6,4},{7,5},{8,10},{9,11},{10,... | collective-permute-start | bytes 3538952 | tf_op jit(solution)/shard_map/ppermute | solution.py:45
  215.9 120.5 %collective-permute-start.19 = (bf16[8,144,640]{2,1,0:T(8,128)(2,1)}, bf16[8,144,640]{2,1,0:T(8,128)(2,1)}, u32[]{:S(2)}, u32[]{:S(2)}) collective-permute-start(bf16[8,144,640]{2,1,0:T(8,128)(2,1)} %pad_maximum_fusion.8), channel_id=1, source_target_pairs={{0,4},{4,0},{8,12},{12,8},{16,20},{20,16},{24,28},{28,24},{1,5},{5... | collective-permute-start | bytes 4423688 | tf_op jit(solution)/shard_map/ppermute | solution.py:50
  224.2 87.4 %collective-permute-start.13 = (bf16[8,144,672]{2,1,0:T(8,128)(2,1)}, bf16[8,144,672]{2,1,0:T(8,128)(2,1)}, u32[]{:S(2)}, u32[]{:S(2)}) collective-permute-start(bf16[8,144,672]{2,1,0:T(8,128)(2,1)} %pad_maximum_fusion.6), channel_id=1, source_target_pairs={{0,2},{1,3},{2,0},{3,1},{4,6},{5,7},{6,4},{7,5},{8,10},{9,11},{10,... | collective-permute-start | bytes 4644872 | tf_op jit(solution)/shard_map/ppermute | solution.py:45
  244.6 69.8 %collective-permute-start.12 = (bf16[8,144,768]{2,1,0:T(8,128)(2,1)}, bf16[8,144,768]{2,1,0:T(8,128)(2,1)}, u32[]{:S(2)}, u32[]{:S(2)}) collective-permute-start(bf16[8,144,768]{2,1,0:T(8,128)(2,1)} %pad_maximum_fusion.5), channel_id=1, source_target_pairs={{0,4},{4,0},{8,12},{12,8},{16,20},{20,16},{24,28},{28,24},{1,5},{5... | collective-permute-start | bytes 5308424 | tf_op jit(solution)/shard_map/ppermute | solution.py:50
  420.2 56.5 %collective-permute-start.21 = (bf16[512,1152]{1,0:T(8,128)(2,1)S(1)}, bf16[512,1152]{1,0:T(8,128)(2,1)S(1)}, u32[]{:S(2)}, u32[]{:S(2)}) collective-permute-start(bf16[512,1152]{1,0:T(8,128)(2,1)S(1)} %slice.359), channel_id=1, source_target_pairs={{0,1},{1,0},{2,3},{3,2},{4,5},{5,4},{6,7},{7,6},{8,9},{9,8},{10,11... | collective-permute-start | bytes 3538952 | tf_op jit(solution)/shard_map/ppermute | solution.py:41
  420.4 52.3 %collective-permute-start.43 = (bf16[1152,512]{1,0:T(8,128)(2,1)}, bf16[1152,512]{1,0:T(8,128)(2,1)}, u32[]{:S(2)}, u32[]{:S(2)}) collective-permute-start(bf16[1152,512]{1,0:T(8,128)(2,1)} %convolution_convert_fusion.5), channel_id=1, source_target_pairs={{0,2},{1,3},{2,0},{3,1},{4,6},{5,7},{6,4},{7,5},{8,10},{9,11},{10,... | collective-permute-start | bytes 3538952 | tf_op jit(solution)/shard_map/ppermute | solution.py:45
  421.0 125.4 %collective-permute-start.23 = (bf16[1024,1152]{1,0:T(8,128)(2,1)}, bf16[1024,1152]{1,0:T(8,128)(2,1)S(1)}, u32[]{:S(2)}, u32[]{:S(2)}) collective-permute-start(bf16[1024,1152]{1,0:T(8,128)(2,1)} %convolution_convert_fusion), channel_id=1, source_target_pairs={{0,1},{1,0},{2,3},{3,2},{4,5},{5,4},{6,7},{7,6},{8,9},{9,8},{10,11... | collective-permute-start | bytes 7077896 | tf_op jit(solution)/shard_map/ppermute | solution.py:41
  430.1 49.8 %collective-permute-start.47 = (bf16[2,4,144,640]{3,2,1,0:T(8,128)(2,1)S(1)}, bf16[2,4,144,640]{3,2,1,0:T(8,128)(2,1)S(1)}, u32[]{:S(2)}, u32[]{:S(2)}) collective-permute-start(bf16[2,4,144,640]{3,2,1,0:T(8,128)(2,1)S(1)} %fusion.50), channel_id=1, source_target_pairs={{0,4},{4,0},{8,12},{12,8},{16,20},{20,16},{24,28},{28,24},{1,5},{5... | collective-permute-start | bytes 4423688 | tf_op jit(solution)/shard_map/ppermute | solution.py:50
  447.7 49.2 %collective-permute-start.55 = (bf16[2,4,144,640]{3,2,1,0:T(8,128)(2,1)S(1)}, bf16[2,4,144,640]{3,2,1,0:T(8,128)(2,1)S(1)}, u32[]{:S(2)}, u32[]{:S(2)}) collective-permute-start(bf16[2,4,144,640]{3,2,1,0:T(8,128)(2,1)S(1)} %fusion.51), channel_id=1, source_target_pairs={{0,4},{4,0},{8,12},{12,8},{16,20},{20,16},{24,28},{28,24},{1,5},{5... | collective-permute-start | bytes 4423688 | tf_op jit(solution)/shard_map/ppermute | solution.py:50
  476.7 45.0 %collective-permute-start.44 = (bf16[4,144,512]{2,1,0:T(8,128)(2,1)S(1)}, bf16[4,144,512]{2,1,0:T(8,128)(2,1)S(1)}, u32[]{:S(2)}, u32[]{:S(2)}) collective-permute-start(bf16[4,144,512]{2,1,0:T(8,128)(2,1)S(1)} %fusion.91), channel_id=1, source_target_pairs={{0,4},{4,0},{8,12},{12,8},{16,20},{20,16},{24,28},{28,24},{1,5},{5... | collective-permute-start | bytes 1769480 | tf_op jit(solution)/shard_map/ppermute | solution.py:50
  480.2 62.2 %collective-permute-start.48 = (bf16[4,144,640]{2,1,0:T(8,128)(2,1)S(1)}, bf16[4,144,640]{2,1,0:T(8,128)(2,1)S(1)}, u32[]{:S(2)}, u32[]{:S(2)}) collective-permute-start(bf16[4,144,640]{2,1,0:T(8,128)(2,1)S(1)} %fusion.89), channel_id=1, source_target_pairs={{0,2},{1,3},{2,0},{3,1},{4,6},{5,7},{6,4},{7,5},{8,10},{9,11},{10,... | collective-permute-start | bytes 2211848 | tf_op jit(solution)/shard_map/ppermute | solution.py:45
  497.3 46.1 %collective-permute-start.56 = (bf16[4,144,640]{2,1,0:T(8,128)(2,1)S(1)}, bf16[4,144,640]{2,1,0:T(8,128)(2,1)S(1)}, u32[]{:S(2)}, u32[]{:S(2)}) collective-permute-start(bf16[4,144,640]{2,1,0:T(8,128)(2,1)S(1)} %fusion.90), channel_id=1, source_target_pairs={{0,2},{1,3},{2,0},{3,1},{4,6},{5,7},{6,4},{7,5},{8,10},{9,11},{10,... | collective-permute-start | bytes 2211848 | tf_op jit(solution)/shard_map/ppermute | solution.py:45
  543.4 187.5 %collective-permute-start.49 = (bf16[2,144,640]{2,1,0:T(8,128)(2,1)}, bf16[2,144,640]{2,1,0:T(8,128)(2,1)}, u32[]{:S(2)}, u32[]{:S(2)}) collective-permute-start(bf16[2,144,640]{2,1,0:T(8,128)(2,1)} %fusion.100), channel_id=1, source_target_pairs={{0,8},{4,12},{8,0},{12,4},{16,24},{20,28},{24,16},{28,20},{1,9},{5... | collective-permute-start | bytes 1105928 | tf_op jit(solution)/shard_map/ppermute | solution.py:50
  544.3 188.8 %collective-permute-start.57 = (bf16[2,144,640]{2,1,0:T(8,128)(2,1)}, bf16[2,144,640]{2,1,0:T(8,128)(2,1)}, u32[]{:S(2)}, u32[]{:S(2)}) collective-permute-start(bf16[2,144,640]{2,1,0:T(8,128)(2,1)} %fusion.101), channel_id=1, source_target_pairs={{0,8},{4,12},{8,0},{12,4},{16,24},{20,28},{24,16},{28,20},{1,9},{5... | collective-permute-start | bytes 1105928 | tf_op jit(solution)/shard_map/ppermute | solution.py:50
  665.3 70.2 %collective-permute-start.35 = (bf16[1152,128]{1,0:T(8,128)(2,1)}, bf16[1152,128]{1,0:T(8,128)(2,1)}, u32[]{:S(2)}, u32[]{:S(2)}) collective-permute-start(bf16[1152,128]{1,0:T(8,128)(2,1)} %convolution_convert_fusion.7), channel_id=1, source_target_pairs={{0,2},{1,3},{2,0},{3,1},{4,6},{5,7},{6,4},{7,5},{8,10},{9,11},{10,... | collective-permute-start | bytes 884744 | tf_op jit(solution)/shard_map/ppermute | solution.py:45
  667.7 71.4 %collective-permute-start.39 = (bf16[2,4,144,160]{3,2,1,0:T(8,128)(2,1)}, bf16[2,4,144,160]{3,2,1,0:T(8,128)(2,1)}, u32[]{:S(2)}, u32[]{:S(2)}) collective-permute-start(bf16[2,4,144,160]{3,2,1,0:T(8,128)(2,1)} %fusion.94), channel_id=1, source_target_pairs={{0,4},{4,0},{8,12},{12,8},{16,20},{20,16},{24,28},{28,24},{1,5},{5... | collective-permute-start | bytes 1105928 | tf_op jit(solution)/shard_map/ppermute | solution.py:50
  725.3 55.0 %collective-permute-start.27 = (bf16[1152,384]{1,0:T(8,128)(2,1)S(1)}, bf16[1152,384]{1,0:T(8,128)(2,1)S(1)}, u32[]{:S(2)}, u32[]{:S(2)}) collective-permute-start(bf16[1152,384]{1,0:T(8,128)(2,1)S(1)} %copy-done.72), channel_id=1, source_target_pairs={{0,2},{1,3},{2,0},{3,1},{4,6},{5,7},{6,4},{7,5},{8,10},{9,11},{10,... | collective-permute-start | bytes 2654216 | tf_op jit(solution)/shard_map/ppermute | solution.py:45
  730.8 54.5 %collective-permute-start.24 = (bf16[512,1152]{1,0:T(8,128)(2,1)S(1)}, bf16[512,1152]{1,0:T(8,128)(2,1)S(1)}, u32[]{:S(2)}, u32[]{:S(2)}) collective-permute-start(bf16[512,1152]{1,0:T(8,128)(2,1)S(1)} %slice.364), channel_id=1, source_target_pairs={{0,1},{1,0},{2,3},{3,2},{4,5},{5,4},{6,7},{7,6},{8,9},{9,8},{10,11... | collective-permute-start | bytes 3538952 | tf_op jit(solution)/shard_map/ppermute | solution.py:41
  733.1 55.8 %collective-permute-start.31 = (bf16[2,4,144,480]{3,2,1,0:T(8,128)(2,1)S(1)}, bf16[2,4,144,480]{3,2,1,0:T(8,128)(2,1)S(1)}, u32[]{:S(2)}, u32[]{:S(2)}) collective-permute-start(bf16[2,4,144,480]{3,2,1,0:T(8,128)(2,1)S(1)} %fusion.63), channel_id=1, source_target_pairs={{0,4},{4,0},{8,12},{12,8},{16,20},{20,16},{24,28},{28,24},{1,5},{5... | collective-permute-start | bytes 3317768 | tf_op jit(solution)/shard_map/ppermute | solution.py:50
  784.0 162.1 %collective-permute-start.28 = (bf16[4,144,384]{2,1,0:T(8,128)(2,1)}, bf16[4,144,384]{2,1,0:T(8,128)(2,1)S(1)}, u32[]{:S(2)}, u32[]{:S(2)}) collective-permute-start(bf16[4,144,384]{2,1,0:T(8,128)(2,1)} %fusion.99), channel_id=1, source_target_pairs={{0,4},{4,0},{8,12},{12,8},{16,20},{20,16},{24,28},{28,24},{1,5},{5... | collective-permute-start | bytes 1327112 | tf_op jit(solution)/shard_map/ppermute | solution.py:50
  792.0 159.8 %collective-permute-start.32 = (bf16[4,144,480]{2,1,0:T(8,128)(2,1)}, bf16[4,144,480]{2,1,0:T(8,128)(2,1)}, u32[]{:S(2)}, u32[]{:S(2)}) collective-permute-start(bf16[4,144,480]{2,1,0:T(8,128)(2,1)} %fusion.93), channel_id=1, source_target_pairs={{0,2},{1,3},{2,0},{3,1},{4,6},{5,7},{6,4},{7,5},{8,10},{9,11},{10,... | collective-permute-start | bytes 1658888 | tf_op jit(solution)/shard_map/ppermute | solution.py:45
  (121 other events, 2770.8 us)
Sparse Core Ops, SparseCore 0:
  43.4 94.4 all-reduce.6
  827.9 116.6 all-reduce.4

commit v2 on v1

v2 whole, which is shorter than its diff:
```python
import jax
import jax.numpy as jnp
from jax import lax
from jax.experimental import pallas as pl
from jax.experimental.pallas import tpu as pltpu
from jax.sharding import PartitionSpec as P

HEAD_DIM = 72
SEQ = 1024

highest = lax.Precision.HIGHEST
root_two_pi = 0.7978845608028654
cubic_term = 0.044715
epsilon = 1e-06
log2_e = 1.4426950408889634
bf16 = jnp.bfloat16
f32 = jnp.float32


def normalize(values):
    centre = values - jnp.mean(values, axis=-1, keepdims=True)
    inverse = lax.rsqrt(jnp.mean(centre * centre, axis=-1, keepdims=True) + epsilon)
    return (centre * inverse, inverse)


def norm_back(normed, inverse, grad_in):
    mean_grad = jnp.mean(grad_in, axis=-1, keepdims=True)
    mean_cross = jnp.mean(grad_in * normed, axis=-1, keepdims=True)
    return inverse * (grad_in - mean_grad - normed * mean_cross)


def gelu_parts(pre_act):
    tangent = jnp.tanh(root_two_pi * (pre_act + cubic_term * pre_act * pre_act * pre_act))
    activated = 0.5 * pre_act * (1.0 + tangent)
    gelu_slope = 0.5 * (1.0 + tangent) + 0.5 * pre_act * (1.0 - tangent * tangent) * root_two_pi * (
        1.0 + 3.0 * cubic_term * pre_act * pre_act
    )
    return (activated, gelu_slope)


def swap_cores(values):
    return lax.ppermute(values, "tensor", [(i, i ^ 1) for i in range(4)])


def swap_y(values):
    return lax.ppermute(values, "tensor", [(i, i ^ 2) for i in range(4)])


def swap_dp(values, bit):
    size = lax.axis_size("dp")
    return lax.ppermute(values, "dp", [(i, i ^ (1 << bit)) for i in range(size)])


def after(values, *deps):
    return lax.optimization_barrier((values, deps))[0]


def dp_bits():
    return lax.axis_size("dp").bit_length() - 1


def own_bit(bit):
    return (lax.axis_index("dp") >> bit) & 1


def ordered(flag, mine, theirs, axis):
    first = jnp.where(flag == 0, mine, theirs)
    second = jnp.where(flag == 0, theirs, mine)
    return jnp.concatenate([first, second], axis=axis)


def gather_small(values):
    for bit in range(dp_bits()):
        values = ordered(own_bit(bit), values, swap_dp(values, bit), 0)
    return values


def scatter_small(values):
    for bit in reversed(range(dp_bits())):
        halves = values.reshape((2, values.shape[0] // 2) + values.shape[1:])
        mine = own_bit(bit)
        keep = lax.dynamic_index_in_dim(halves, mine, 0, False)
        send = lax.dynamic_index_in_dim(halves, 1 - mine, 0, False)
        values = keep + swap_dp(send, bit)
    return values


def exchange_small(values):
    dp, k, n = values.shape
    values = values[:, :, None]
    for bit in range(dp_bits()):
        pairs = values.reshape((values.shape[0] // 2, 2) + values.shape[1:])
        mine = own_bit(bit)
        keep = lax.dynamic_index_in_dim(pairs, mine, 1, False)
        send = lax.dynamic_index_in_dim(pairs, 1 - mine, 1, False)
        values = ordered(mine, keep, swap_dp(send, bit), 2)
    return values.reshape(k, dp * n)


def place_blocks(pieces, outputs, order_bits):
    half, rows, _ = pieces[0][0].shape
    widths = [first.shape[2] for first, _ in pieces]
    totals = [sum(hi - lo for _, lo, hi in spec) for spec in outputs]
    dp = 2 * half

    def rel_of(j, me):
        apart = j ^ me
        rel = 0
        for place, bit in enumerate(order_bits):
            rel = rel | (((apart >> bit) & 1) << place)
        return rel

    def kernel(me_ref, *refs):
        rel = rel_of(pl.program_id(0), me_ref[0])
        out_refs = refs[2 * len(pieces) :]

        def write(which):
            for out_ref, spec in zip(out_refs, outputs):
                at = 0
                for i, lo, hi in spec:
                    out_ref[0, :, at : at + hi - lo] = refs[2 * i + which][0, :, lo:hi]
                    at += hi - lo

        @pl.when(rel < half)
        def _():
            write(0)

        @pl.when(rel >= half)
        def _():
            write(1)

    def first_map(j, me_ref):
        rel = rel_of(j, me_ref[0])
        return (jnp.where(rel < half, rel, 0), 0, 0)

    def second_map(j, me_ref):
        rel = rel_of(j, me_ref[0])
        return (jnp.where(rel >= half, rel - half, 0), 0, 0)

    in_specs = []
    operands = []
    for (first, second), n in zip(pieces, widths):
        in_specs += [pl.BlockSpec((1, rows, n), first_map), pl.BlockSpec((1, rows, n), second_map)]
        operands += [first, second]
    me = lax.axis_index("dp").astype(jnp.int32).reshape(1)
    placed = pl.pallas_call(
        kernel,
        out_shape=[jax.ShapeDtypeStruct((dp, rows, total), bf16) for total in totals],
        grid_spec=pltpu.PrefetchScalarGridSpec(
            num_scalar_prefetch=1,
            grid=(dp,),
            in_specs=in_specs,
            out_specs=[
                pl.BlockSpec((1, rows, total), lambda j, me_ref: (j, 0, 0)) for total in totals
            ],
        ),
        cost_estimate=pl.CostEstimate(
            flops=0, transcendentals=0, bytes_accessed=5 * dp * rows * sum(totals)
        ),
        name="place_blocks",
    )(me, *operands)
    return [array.reshape(dp * rows, total) for array, total in zip(placed, totals)]


def gather_start(shard):
    got = shard[None]
    for bit in range(dp_bits() - 1, 0, -1):
        got = jnp.concatenate([got, swap_dp(got, bit)], axis=0)
    return got


def gather_end(got, cut, outputs):
    half = got.shape[0]
    part_a, part_b = got[:, :, :cut], got[:, :, cut:]
    a_x = swap_dp(part_a, 0)
    b_y = swap_y(part_b)
    a_both = swap_y(jnp.concatenate([part_a, a_x], axis=0))
    b_both = swap_dp(jnp.concatenate([part_b, b_y], axis=0), 0)
    pieces = [
        (part_a, a_x),
        (part_b, b_both[:half]),
        (a_both[:half], a_both[half:]),
        (b_y, b_both[half:]),
    ]
    columns = []
    for spec in outputs:
        split = []
        for far, lo, hi in spec:
            if lo < cut:
                split.append((2 * far, lo, min(hi, cut)))
            if hi > cut:
                split.append((2 * far + 1, max(lo, cut) - cut, hi - cut))
        columns.append(split)
    return place_blocks(pieces, columns, list(range(dp_bits() - 1, -1, -1)))


def split_bit(blocks, axis, bit):
    mine = own_bit(bit)
    keep = lax.dynamic_index_in_dim(blocks, mine, axis, False)
    send = lax.dynamic_index_in_dim(blocks, 1 - mine, axis, False)
    return keep, send.astype(bf16)


def weight_term(left, right, kind):
    out = lax.dot_general(left, right, (((0,), (0,)), ((), ())), preferred_element_type=f32)
    dp = lax.axis_size("dp")
    return out.astype(kind).reshape(dp // 2, 2, out.shape[0] // dp, out.shape[1])


def low_stages(total, deps):
    for bit in range(1, dp_bits()):
        blocks = total.reshape((total.shape[0] // 2, 2) + total.shape[1:])
        keep, send = split_bit(blocks, 1, bit)
        got = swap_dp(send, bit)
        if deps:
            got = after(got, deps.pop(0))
        total = keep + got.astype(f32)
    return total[0]


def y_first_send(far):
    return swap_y(far)


def y_first_mid(near, got):
    keep, send = split_bit(near + got.astype(f32), 1, 0)
    return keep, swap_dp(send, 0)


def x_first_send(near, far):
    keep_near, send_near = split_bit(near, 1, 0)
    keep_far, send_far = split_bit(far, 1, 0)
    return keep_near, keep_far, swap_dp(jnp.stack([send_near, send_far]), 0)


def x_first_mid(keep_near, keep_far, got):
    far = (keep_far + got[1].astype(f32)).astype(bf16)
    return keep_near + got[0].astype(f32), swap_y(far)


def dot_nt(left_rows, right_mat):
    return lax.dot_general(
        left_rows, right_mat, (((1,), (1,)), ((), ())), preferred_element_type=f32
    )


def dot_nn(left_rows, right_mat):
    return jnp.dot(left_rows, right_mat, preferred_element_type=f32)


def flip_halves(values):
    half = values.shape[0] // 2
    return jnp.concatenate([values[half:], values[:half]], axis=0)


def sum_cores_all(partial):
    mine = partial.astype(bf16)
    theirs = flip_halves(swap_cores(mine))
    return mine.astype(f32) + theirs.astype(f32)


def sum_cores_own(partial):
    mine = partial.astype(bf16)
    half = mine.shape[0] // 2
    theirs = swap_cores(mine[half:])
    return mine[:half].astype(f32) + theirs.astype(f32)


def attend(qkv, block=512, unroll=2):
    rows, cols = qkv.shape
    size = HEAD_DIM
    heads = cols // (3 * size)
    factor = size ** (-0.5) * log2_e

    def kernel(x_ref, mix_ref, lse_ref, q_s, k_s, v_s, o_s, l_s):
        i = pl.program_id(0)

        @pl.when(i == 0)
        def _():
            for h in range(heads):
                b = h * 3 * size
                q_s[h] = x_ref[:, b : b + size]
                k_s[h] = x_ref[:, b + size : b + 2 * size]
                v_s[h] = x_ref[:, b + 2 * size : b + 3 * size]

        def one(h):
            q = q_s[h, pl.ds(pl.multiple_of(i * block, block), block), :]
            scores = lax.dot_general(
                q, k_s[h], (((1,), (1,)), ((), ())), preferred_element_type=f32
            )
            top = jnp.max(scores, axis=-1, keepdims=True)
            probs = jnp.exp2((scores - top) * factor)
            total = jnp.sum(probs, axis=-1, keepdims=True)
            out = jnp.dot(probs.astype(bf16), v_s[h], preferred_element_type=f32)
            o_s[h] = (out / total).astype(bf16)
            l_s[h] = top * factor + jnp.log2(total)

        def body(g, _):
            for u in range(unroll):
                one(g * unroll + u)
            return 0

        lax.fori_loop(0, heads // unroll, body, 0)
        for h in range(heads):
            mix_ref[:, h * size : (h + 1) * size] = o_s[h]
            lse_ref[:, h : h + 1] = l_s[h]

    return pl.pallas_call(
        kernel,
        out_shape=(
            jax.ShapeDtypeStruct((rows, heads * size), bf16),
            jax.ShapeDtypeStruct((rows, heads), f32),
        ),
        grid=(rows // block,),
        in_specs=[pl.BlockSpec((rows, cols), lambda i: (0, 0))],
        out_specs=(
            pl.BlockSpec((block, heads * size), lambda i: (i, 0)),
            pl.BlockSpec((block, heads), lambda i: (i, 0)),
        ),
        scratch_shapes=[pltpu.VMEM((heads, rows, size), bf16)] * 3
        + [pltpu.VMEM((heads, block, size), bf16), pltpu.VMEM((heads, block, 1), f32)],
        compiler_params=pltpu.CompilerParams(vmem_limit_bytes=48 << 20),
        cost_estimate=pl.CostEstimate(
            flops=16 * heads * rows * rows * size,
            transcendentals=heads * rows * rows,
            bytes_accessed=rows * cols * 2 + rows * heads * size * 2,
        ),
        name="attend",
    )(qkv)


def attend_back(qkv, grad_mix, lse, first, heads, block=512, unroll=2):
    rows, cols = qkv.shape
    size = HEAD_DIM
    all_heads = cols // (3 * size)
    factor = size ** (-0.5) * log2_e
    scale = size ** (-0.5)
    steps = rows // block

    def kernel(x_ref, g_ref, lse_ref, out_ref, q_s, k_s, v_s, g_s, dq_s, dk_s, dv_s):
        i = pl.program_id(0)

        @pl.when(i == 0)
        def _():
            for h in range(heads):
                b = (first + h) * 3 * size
                q_s[h] = x_ref[:, b : b + size]
                k_s[h] = x_ref[:, b + size : b + 2 * size]
                v_s[h] = x_ref[:, b + 2 * size : b + 3 * size]
                g_s[h] = g_ref[:, (first + h) * size : (first + h + 1) * size]
            dk_s[...] = jnp.zeros_like(dk_s)
            dv_s[...] = jnp.zeros_like(dv_s)

        at = pl.ds(pl.multiple_of(i * block, block), block)

        def one(h):
            q = q_s[h, at, :]
            g = g_s[h, at, :]
            k = k_s[h]
            scores = lax.dot_general(k, q, (((1,), (1,)), ((), ())), preferred_element_type=f32)
            probs = jnp.exp2(scores * factor - lse_ref[first + h, :, at])
            grad_probs = lax.dot_general(
                v_s[h], g, (((1,), (1,)), ((), ())), preferred_element_type=f32
            )
            inner = jnp.sum(probs * grad_probs, axis=0, keepdims=True)
            grad_scores = (probs * (grad_probs - inner)).astype(bf16)
            dv_s[h] += jnp.dot(probs.astype(bf16), g, preferred_element_type=f32)
            dk_s[h] += jnp.dot(grad_scores, q, preferred_element_type=f32)
            grad_q = lax.dot_general(
                grad_scores, k, (((0,), (0,)), ((), ())), preferred_element_type=f32
            )
            dq_s[h, at, :] = (grad_q * scale).astype(bf16)

        def body(g, _):
            for u in range(unroll):
                one(g * unroll + u)
            return 0

        lax.fori_loop(0, heads // unroll, body, 0)

        @pl.when(i == steps - 1)
        def _():
            for h in range(heads):
                b = h * 3 * size
                out_ref[:, b : b + size] = dq_s[h]
                out_ref[:, b + size : b + 2 * size] = (dk_s[h] * scale).astype(bf16)
                out_ref[:, b + 2 * size : b + 3 * size] = dv_s[h].astype(bf16)

    return pl.pallas_call(
        kernel,
        out_shape=jax.ShapeDtypeStruct((rows, heads * 3 * size), bf16),
        grid=(steps,),
        in_specs=[
            pl.BlockSpec((rows, cols), lambda i: (0, 0)),
            pl.BlockSpec((rows, all_heads * size), lambda i: (0, 0)),
            pl.BlockSpec((all_heads, 1, rows), lambda i: (0, 0, 0)),
        ],
        out_specs=pl.BlockSpec((rows, heads * 3 * size), lambda i: (0, 0)),
        scratch_shapes=[pltpu.VMEM((heads, rows, size), bf16)] * 5
        + [pltpu.VMEM((heads, rows, size), f32)] * 2,
        compiler_params=pltpu.CompilerParams(vmem_limit_bytes=56 << 20),
        cost_estimate=pl.CostEstimate(
            flops=40 * heads * rows * rows * size,
            transcendentals=heads * rows * rows,
            bytes_accessed=rows * cols * 4,
        ),
        name="attend_back",
    )(qkv, grad_mix, lse)


def shards(
    tokens_in,
    condition,
    w_ada,
    b_ada,
    w_qkv,
    b_qv,
    w_proj,
    b_proj,
    w_fc1,
    b_fc1,
    w_fc2,
    b_fc2,
    cotangent,
):
    tok_rows, width = tokens_in.shape
    head_size = HEAD_DIM
    dp_at = lax.axis_index("dp")
    y_at = lax.axis_index("tensor") // 2
    t_at = lax.axis_index("tensor")
    dp_size = lax.axis_size("dp")
    ada_rows, ada_cols = w_ada.shape
    n_qkv, n_proj, n_fc1, n_fc2 = w_qkv.shape[1], w_proj.shape[0], w_fc1.shape[1], w_fc2.shape[0]

    tokens_all = jnp.concatenate([tokens_in, swap_cores(tokens_in)], axis=0)
    cot_all = jnp.concatenate([cotangent, swap_cores(cotangent)], axis=0)
    bias_mine = jnp.concatenate([b_qv, b_fc1])
    bias_theirs = swap_y(bias_mine)
    n_bqv = b_qv.shape[0]

    got_qkv = gather_start(w_qkv)
    got_two = gather_start(after(jnp.concatenate([w_fc1[:, :384], w_proj.T, w_fc1[:, 384:]], axis=1), got_qkv))
    got_fc2 = gather_start(after(w_fc2.T, got_two))
    (wqkv,) = gather_end(got_qkv, 384, [[(0, 0, n_qkv), (1, 0, n_qkv)]])
    fc1_at = 384 + n_proj
    end_two = n_fc1 + n_proj
    wproj_t, wfc1 = gather_end(
        got_two,
        fc1_at,
        [
            [(0, 384, fc1_at), (1, 384, fc1_at)],
            [(0, 0, 384), (0, fc1_at, end_two), (1, 0, 384), (1, fc1_at, end_two)],
        ],
    )
    (wfc2_t,) = gather_end(got_fc2, 512, [[(0, 0, n_fc2), (1, 0, n_fc2)]])

    cond_all = gather_small(condition).astype(f32)
    silu_all = (cond_all * jax.nn.sigmoid(cond_all)).astype(bf16)
    silu_mine = lax.dynamic_slice_in_dim(silu_all, dp_at * ada_rows, ada_rows, 1)
    mod_part = jnp.dot(silu_mine, w_ada, preferred_element_type=f32)
    mod_cols = scatter_small(mod_part) + b_ada.astype(f32)
    mod_mine = lax.dynamic_slice_in_dim(mod_cols, y_at, 1, 0)
    mod_near = swap_y(lax.dynamic_slice_in_dim(mod_cols, 1 - y_at, 1, 0))
    core_at = t_at % 2
    mod_two = ordered(y_at, mod_mine, mod_near, 0)
    mod_row = ordered(core_at, mod_two[:, None], swap_cores(mod_two)[:, None], 1).reshape(1, 4 * ada_cols)
    shift_attn, scale_attn, gate_attn, shift_mlp, scale_mlp, gate_mlp = jnp.split(mod_row, 6, axis=1)

    input_vals = tokens_all.astype(f32)
    normed_one, inverse_one = normalize(input_vals)
    attn_in = (normed_one * (1.0 + scale_attn) + shift_attn).astype(bf16)
    heads = 2 * n_qkv // (3 * head_size)
    bias_qv = jnp.concatenate([bias_mine[:n_bqv], bias_theirs[:n_bqv]]).reshape(heads, 2, head_size)
    bias_qkv = jnp.stack([bias_qv[:, 0], jnp.zeros_like(bias_qv[:, 0]), bias_qv[:, 1]], axis=1)
    qkv = (dot_nn(attn_in, wqkv) + bias_qkv.astype(f32).reshape(1, 2 * n_qkv)).astype(bf16)
    mix_rows, lse = attend(qkv)
    attn_out = sum_cores_all(dot_nt(mix_rows, wproj_t)) + b_proj.astype(f32)
    middle = input_vals + gate_attn * attn_out

    normed_two, inverse_two = normalize(middle)
    mlp_in = (normed_two * (1.0 + scale_mlp) + shift_mlp).astype(bf16)
    bias_one = jnp.concatenate([bias_mine[n_bqv:], bias_theirs[n_bqv:]]).astype(f32)
    pre_act = dot_nn(mlp_in, wfc1) + bias_one
    activated, gelu_slope = gelu_parts(pre_act)
    act_rows = activated.astype(bf16)

    grad_out = cot_all.astype(f32)
    grad_mlp = (gate_mlp * grad_out).astype(bf16)
    grad_pre = (dot_nn(grad_mlp, wfc2_t) * gelu_slope).astype(bf16)
    cut = 512
    fc2_a_near = weight_term(grad_mlp, act_rows[:, :cut], f32)
    fc2_a_far = weight_term(grad_mlp, act_rows[:, n_fc2 : n_fc2 + cut], bf16)
    fc2_b_near = weight_term(grad_mlp, act_rows[:, cut:n_fc2], f32)
    fc2_b_far = weight_term(grad_mlp, act_rows[:, n_fc2 + cut :], f32)
    fc2_a_got = y_first_send(fc2_a_far)
    fc2_b_near, fc2_b_far, fc2_b_got = x_first_send(fc2_b_near, fc2_b_far)
    mlp_part = dot_nt(act_rows, wfc2_t)
    grad_mlp_part = dot_nt(grad_pre, wfc1)
    mlp_out = sum_cores_own(mlp_part) + b_fc2.astype(f32)
    result = middle[:tok_rows] + gate_mlp * mlp_out
    d_gate_mlp = grad_out[:tok_rows] * mlp_out
    fc1_a_far = weight_term(mlp_in, grad_pre[:, n_fc1 : n_fc1 + cut], bf16)
    fc1_a_near = weight_term(mlp_in, grad_pre[:, :cut], f32)
    fc1_b_near = weight_term(mlp_in, grad_pre[:, cut:n_fc1], f32)
    fc1_b_far = weight_term(mlp_in, grad_pre[:, n_fc1 + cut :], f32)
    fc2_a_got = after(fc2_a_got, fc1_b_far, fc1_a_near)
    fc2_b_got = after(fc2_b_got, fc1_b_far, fc1_a_near)
    fc2_a_keep, fc2_a_got = y_first_mid(fc2_a_near, fc2_a_got)
    fc2_b_keep, fc2_b_got = x_first_mid(fc2_b_near, fc2_b_far, fc2_b_got)
    fc1_a_got = y_first_send(fc1_a_far)
    fc1_b_near, fc1_b_far, fc1_b_got = x_first_send(fc1_b_near, fc1_b_far)
    grad_mlp_in = sum_cores_all(grad_mlp_part)
    d_scale_mlp = grad_mlp_in * normed_two
    grad_middle = grad_out + norm_back(normed_two, inverse_two, grad_mlp_in * (1.0 + scale_mlp))

    grad_attn = (gate_attn * grad_middle).astype(bf16)
    d_gate_attn = grad_middle * attn_out
    grad_mix = dot_nn(grad_attn, wproj_t).astype(bf16)
    proj_far = weight_term(grad_attn, mix_rows[:, n_proj:], bf16)
    proj_near = weight_term(grad_attn, mix_rows[:, :n_proj], f32)
    lse_rows = lse.T.reshape(heads, 1, 2 * tok_rows)
    fc2_a_got = after(fc2_a_got, grad_mix, proj_near)
    fc2_b_got = after(fc2_b_got, grad_mix, proj_near)
    fc2_sum = jnp.concatenate(
        [fc2_a_keep + fc2_a_got.astype(f32), fc2_b_keep + fc2_b_got.astype(f32)], axis=2
    )
    grad_far = attend_back(qkv, grad_mix, lse_rows, heads // 2, heads // 2)
    qkv_far = weight_term(attn_in, grad_far, bf16)
    fc1_a_got = after(fc1_a_got, grad_far)
    fc1_b_got = after(fc1_b_got, grad_far)
    fc1_a_keep, fc1_a_got = y_first_mid(fc1_a_near, fc1_a_got)
    fc1_b_keep, fc1_b_got = x_first_mid(fc1_b_near, fc1_b_far, fc1_b_got)
    proj_got = y_first_send(proj_far)
    qkv_got = y_first_send(qkv_far)
    grad_near = attend_back(qkv, after(grad_mix, grad_far), lse_rows, 0, heads // 2)
    proj_got = after(proj_got, grad_near)
    qkv_near = weight_term(attn_in, grad_near, f32)
    owned_fc2 = low_stages(fc2_sum, [grad_far, grad_near]).T
    fc1_a_got = after(fc1_a_got, grad_near)
    fc1_b_got = after(fc1_b_got, grad_near)
    fc1_sum = jnp.concatenate(
        [fc1_a_keep + fc1_a_got.astype(f32), fc1_b_keep + fc1_b_got.astype(f32)], axis=2
    )
    grad_attn_part = dot_nt(grad_near, wqkv[:, :n_qkv]) + dot_nt(grad_far, wqkv[:, n_qkv:])
    qkv_keep, qkv_got = y_first_mid(qkv_near, qkv_got)
    proj_keep, proj_got = y_first_mid(proj_near, proj_got)
    owned_fc1 = low_stages(fc1_sum, [grad_attn_part])
    grad_attn_in = sum_cores_own(grad_attn_part)
    d_scale_attn = grad_attn_in * normed_one[:tok_rows]
    grad_tokens = grad_middle[:tok_rows] + norm_back(
        normed_one[:tok_rows], inverse_one[:tok_rows], grad_attn_in * (1.0 + scale_attn)
    )
    owned_qkv = low_stages(qkv_keep + qkv_got.astype(f32), [])
    owned_proj = low_stages(proj_keep + proj_got.astype(f32), []).T

    own = [
        jnp.sum(term[:tok_rows], axis=0)
        for term in (grad_attn_in, d_scale_attn, d_gate_attn, grad_mlp_in, d_scale_mlp, d_gate_mlp)
    ]
    mod_sums = jnp.concatenate(own)
    mod_sums = mod_sums + swap_cores(mod_sums)
    by_rank = mod_sums.reshape(4, ada_cols)
    mod_keep = lax.dynamic_index_in_dim(by_rank, t_at, 0, False)
    mod_send = lax.dynamic_index_in_dim(by_rank, t_at ^ 2, 0, False)

    def value_sums(grads):
        sums = jnp.sum(grads.astype(f32), axis=0).reshape(heads // 2, 3, head_size)
        return jnp.concatenate([sums[:, :1], sums[:, 2:]], axis=1).reshape(n_bqv)

    b1_sums = jnp.sum(grad_pre.astype(f32), axis=0)
    bias_near = jnp.concatenate([value_sums(grad_near), b1_sums[:n_fc1]])
    bias_far = jnp.concatenate([value_sums(grad_far), b1_sums[n_fc1:]])
    out_sums = jnp.concatenate(
        [jnp.sum(grad_attn.astype(f32), axis=0), jnp.sum(grad_mlp.astype(f32), axis=0)]
    )
    got = swap_y(jnp.concatenate([mod_send, bias_far, out_sums]))
    mod_got, rest = got[:ada_cols], got[ada_cols:]
    sums = jnp.concatenate([bias_near, out_sums]) + rest
    grad_mod = ordered(y_at, mod_keep[None], mod_got[None], 0)
    for bit in range(dp_bits()):
        size = grad_mod.size
        got = swap_dp(jnp.concatenate([grad_mod.reshape(size), sums]), bit)
        grad_mod = ordered(own_bit(bit), grad_mod, got[:size].reshape(grad_mod.shape), 0)
        sums = sums + got[size:]
    owned_ada = lax.dot_general(
        silu_mine.astype(f32), grad_mod, (((0,), (0,)), ((), ())), precision=highest
    )
    grad_ba = jnp.sum(grad_mod, axis=0)
    silu_part = lax.dot_general(
        grad_mod, w_ada.astype(f32), (((1,), (1,)), ((), ())), precision=highest
    )
    silu_part = silu_part + swap_cores(silu_part)
    silu_part = silu_part + swap_y(silu_part)
    latents = condition.shape[0]
    grad_silu = exchange_small(silu_part.reshape(dp_size, latents, ada_rows))
    cond_vals = condition.astype(f32)
    cond_sigmoid = jax.nn.sigmoid(cond_vals)
    grad_condition = grad_silu * cond_sigmoid * (1.0 + cond_vals * (1.0 - cond_sigmoid))
    n_bias = n_bqv + n_fc1
    return (
        result.astype(bf16),
        grad_tokens,
        grad_condition,
        owned_ada,
        grad_ba,
        owned_qkv,
        sums[:n_bqv],
        owned_proj,
        sums[n_bias : n_bias + width],
        owned_fc1,
        sums[n_bqv:n_bias],
        owned_fc2,
        sums[n_bias + width :],
    )


def solution(mesh):
    placed = (
        P(("dp", "tensor"), None),
        P("dp", None),
        P("dp", "tensor"),
        P("tensor"),
        P("dp", "tensor"),
        P("tensor"),
        P("tensor", "dp"),
        P(),
        P("dp", "tensor"),
        P("tensor"),
        P("tensor", "dp"),
        P(),
        P(("dp", "tensor"), None),
    )
    return jax.shard_map(
        shards,
        mesh=mesh,
        in_specs=placed,
        out_specs=(
            P(("dp", "tensor"), None),
            P(("dp", "tensor"), None),
            P("dp", None),
            P("dp", "tensor"),
            P("tensor"),
            P("dp", "tensor"),
            P("tensor"),
            P("tensor", "dp"),
            P(),
            P("dp", "tensor"),
            P("tensor"),
            P("tensor", "dp"),
            P(),
        ),
        check_vma=False,
    )
```

time: 986 us -> 617 us (0.63)
  waiting for transfers between devices: 393 us -> 180 us
  blocking collectives: 114 us -> 0 us
  matrix products: 200 us -> 119 us
  Pallas kernels: 26.2 us -> 91 us
  other arithmetic: 118 us -> 95.1 us
  between operations: 16.7 us -> 2.41 us
    psum x1 -> x0, waiting for transfers between devices: 114 us -> none  [shards(): lax.psum((silu_place, bias_place, grad_bo, grad_b2), ('dp', 'tensor'))]
    dot_general x20 -> x12, matrix products: 129 us -> 43 us  [weight_term(): lax.dot_general(left, right, (((0,), (0,)), ((), ())), preferred_element_...]
    unnamed x3 -> x0, waiting for transfers between devices: 83.5 us -> none
    all_gather x3 -> x0, blocking collectives: 67.1 us -> none  [the longest x1 31.2 us: shards(): cond_all = lax.all_gather(condition, 'dp', axis=0, tiled=True).astype(f32)]
    pallas_call x3 -> x6, Pallas kernels: 26.2 us -> 91 us  [the longest x2 43.1 us: attend_back(): pl.pallas_call(kernel, out_shape=jax.ShapeDtypeStruct((rows, heads * 3 *...]
    psum x1 -> x0, blocking collectives: 46.8 us -> none  [shards(): lax.psum((silu_place, bias_place, grad_bo, grad_b2), ('dp', 'tensor'))]
    convert_element_type x10 -> x6, other arithmetic: 41.8 us -> 3.27 us  [the longest x1 1.29 us: shards(): mlp_out = sum_cores_own(mlp_part) + b_fc2.astype(f32)]
    ppermute x16, waiting for transfers between devices: 64.3 us -> 29.4 us  [swap_y(): return lax.ppermute(values, 'tensor', [(i, i ^ 2) for i in range(4)])]
  transfers between devices with their start and end apart: 61 -> 63, of which waited for: 29 -> 30; matrix products, arithmetic and copies ran while one was open for 30% -> 32% of each run, Pallas kernels for 3% -> 15%
where the time goes in v2:
time: 617 us; the launch traced here: 610 us
  waiting for transfers between devices  180 us (29%)
  matrix products  119 us (19%)
  other arithmetic  95.1 us (15%)
  Pallas kernels  91 us (15%)
  starting transfers between devices  68 us (11%)
  local copies, waits for them, and re-layouts  54.1 us (9%)
    ppermute x38, waiting for transfers between devices, swap_dp(): return lax.ppermute(values, 'dp', [(i, i ^ 1 << bit) for i in range(size)])  150 us
    ppermute x38, starting transfers between devices, swap_dp(): return lax.ppermute(values, 'dp', [(i, i ^ 1 << bit) for i in range(size)])  46.6 us
    pallas_call x2, Pallas kernels, attend_back(): pl.pallas_call(kernel, out_shape=jax.ShapeDtypeStruct((rows, heads * 3 *...  43.1 us
    dot_general x12, matrix products, weight_term(): lax.dot_general(left, right, (((0,), (0,)), ((), ())), preferred_element_...  43 us
    dot_general x5, matrix products, dot_nt(): lax.dot_general(left_rows, right_mat, (((1,), (1,)), ((), ())), preferred...  37.6 us
    dot_general x4, matrix products, dot_nn(): return jnp.dot(left_rows, right_mat, preferred_element_type=f32)  35.7 us
    ppermute x16, waiting for transfers between devices, swap_y(): return lax.ppermute(values, 'tensor', [(i, i ^ 2) for i in range(4)])  29.4 us
    pallas_call x3, Pallas kernels, place_blocks(): pl.pallas_call(kernel, out_shape=[jax.ShapeDtypeStruct((dp, rows, total),...  25.9 us
  transfers between devices with their start and end apart: 63, of which 30 were waited for; matrix products, arithmetic and copies ran while one was open for 32% of the time, Pallas kernels for 15%

profile of v2, /device:TPU:0, one launch (start us, length us, event | category | flops | bytes accessed | tf_op | source)
XLA Modules:
  0.0 609.6 jit_solution(13157777733379287899)
XLA Ops:
  18.4 5.9 collective-permute-done.3
  25.0 5.0 collective-permute-done.4
  41.7 6.9 %collective-permute-done.10 = bf16[2,144,864]{2,1,0:T(8,128)(2,1)S(1)} collective-permute-done((bf16[2,144,864]{2,1,0:T(8,128)(2,1)S(1)}, bf16[2,144,864]{2,1,0:T(8,128)(2,1)S(1)}, u32[]{:S(2)}, u32[]{:S(2)}) %collective-permute-start.10) | collective-permute-done | bytes 497696 | tf_op jit(solution)/shard_map/ppermute | solution.py:51
  57.8 9.2 %collective-permute-done.16 = bf16[1,144,1440]{2,1,0:T(8,128)(2,1)} collective-permute-done((bf16[1,144,1440]{2,1,0:T(8,128)(2,1)S(1)}, bf16[1,144,1440]{2,1,0:T(8,128)(2,1)}, u32[]{:S(2)}, u32[]{:S(2)}) %collective-permute-start.16) | collective-permute-done | bytes 414752 | tf_op jit(solution)/shard_map/ppermute | solution.py:51
  73.5 15.1 %collective-permute-done.17 = bf16[2,144,1440]{2,1,0:T(8,128)(2,1)S(1)} collective-permute-done((bf16[2,144,1440]{2,1,0:T(8,128)(2,1)S(1)}, bf16[2,144,1440]{2,1,0:T(8,128)(2,1)S(1)}, u32[]{:S(2)}, u32[]{:S(2)}) %collective-permute-start.17) | collective-permute-done | bytes 829472 | tf_op jit(solution)/shard_map/ppermute | solution.py:51
  97.6 8.1 %collective-permute-done.23 = bf16[1,144,1152]{2,1,0:T(8,128)(2,1)S(1)} collective-permute-done((bf16[1,144,1152]{2,1,0:T(8,128)(2,1)S(1)}, bf16[1,144,1152]{2,1,0:T(8,128)(2,1)S(1)}, u32[]{:S(2)}, u32[]{:S(2)}) %collective-permute-start.23) | collective-permute-done | bytes 331808 | tf_op jit(solution)/shard_map/ppermute | solution.py:51
  107.8 7.9 %place_blocks.3 = bf16[8,144,1728]{2,1,0:T(8,128)(2,1)} custom-call(s32[1]{0:T(128)} %bitcast.8.me_ref, bf16[4,144,384]{2,1,0:T(8,128)(2,1)} %copy-done.16, bf16[4,144,384]{2,1,0:T(8,128)(2,1)} %copy-done.25, bf16[4,144,480]{2,1,0:T(8,128)(2,1)} %copy-done.11, bf16[4,144,480]{2,1,0:T(8,128)(2,1)} %get-tuple-element.97.refs_3_, ...), custom_call_target="tpu_custom_call" | custom-call | bytes 9953280 | tf_op jit(solution)/shard_map/place_blocks/pallas_call | solution.py:146
  123.5 6.8 %add_convert_fusion.x_ref = bf16[1024,1728]{1,0:T(8,128)(2,1)S(1)} fusion(bf16[1152,1728]{1,0:T(8,128)(2,1)S(1)} %bitcast.192, f32[1728]{0:T(1024)S(1)} %reshape.370, f32[1152]{0:T(1024)S(1)} %get-tuple-element.62, f32[1152]{0:T(1024)S(1)} %get-tuple-element.63, f32[1024]{0:T(1024)S(1)} %add_rsqrt_fusion.1, f32[1024]{0:T(1024)S(1)} %broadcast_multiply_fusion.3, ...), kind=kOutput, calls=%fused_computation.11 | convolution fusion | flops 4091019264 | bytes 9903872 | tf_op jit(solution)/shard_map/dot_general | solution.py:248
  130.3 22.0 %attend.1 = (bf16[1024,576]{1,0:T(8,128)(2,1)S(1)}, f32[1024,8]{1,0:T(8,128)S(1)}) custom-call(bf16[1024,1728]{1,0:T(8,128)(2,1)S(1)} %add_convert_fusion.x_ref), custom_call_target="tpu_custom_call" | custom-call | flops 9663676416 | bytes 4718592 | tf_op jit(solution)/shard_map/attend/pallas_call | solution.py:308
  165.1 9.8 %place_blocks.4 = (bf16[8,144,576]{2,1,0:T(8,128)(2,1)}, bf16[8,144,2304]{2,1,0:T(8,128)(2,1)}) custom-call(s32[1]{0:T(128)} %bitcast.8.me_ref, bf16[4,144,672]{2,1,0:T(8,128)(2,1)} %slice.314.refs_0_, bf16[4,144,672]{2,1,0:T(8,128)(2,1)} %collective-permute-done.18.refs_1_, bf16[4,144,768]{2,1,0:T(8,128)(2,1)} %slice.315.refs_2_, ...), custom_call_target="tpu_custom_call" | custom-call | bytes 16588800 | tf_op jit(solution)/shard_map/place_blocks/pallas_call | solution.py:146
  199.3 15.5 %collective-permute-done.28 = bf16[8,144,512]{2,1,0:T(8,128)(2,1)} collective-permute-done((bf16[8,144,512]{2,1,0:T(8,128)(2,1)}, bf16[8,144,512]{2,1,0:T(8,128)(2,1)}, u32[]{:S(2)}, u32[]{:S(2)}) %collective-permute-start.28) | collective-permute-done | bytes 1179680 | tf_op jit(solution)/shard_map/ppermute | solution.py:46
  220.1 8.3 %place_blocks.5 = bf16[8,144,2304]{2,1,0:T(8,128)(2,1)} custom-call(s32[1]{0:T(128)} %bitcast.8.me_ref, bf16[4,144,512]{2,1,0:T(8,128)(2,1)} %pad_maximum_fusion.17.refs_0_, bf16[4,144,512]{2,1,0:T(8,128)(2,1)} %collective-permute-done.25.refs_1_, bf16[4,144,640]{2,1,0:T(8,128)(2,1)} %pad_maximum_fusion.14.refs_2_, ...), custom_call_target="tpu_custom_call" | custom-call | bytes 13271040 | tf_op jit(solution)/shard_map/place_blocks/pallas_call | solution.py:146
  230.3 7.3 %fusion.73 = (f32[1024]{0:T(1024)S(1)}, f32[1024,1152]{1,0:T(8,128)S(1)}, f32[1024,1152]{1,0:T(8,128)}, f32[1024,1152]{1,0:T(8,128)}) fusion(f32[1152]{0:T(1024)S(1)} %get-tuple-element.64, bf16[512,1152]{1,0:T(8,128)(2,1)S(1)} %copy-done.6, bf16[512,1152]{1,0:T(8,128)(2,1)S(1)} %copy-done.3, f32[1152]{0:T(1024)S(1)} %copy-done.47, ...), kind=kLoop, calls=%fused_computation.262 | loop fusion | flops 18873344 | bytes 21255168 | tf_op jit(solution)/shard_map/reduce_sum | solution.py:21
  240.4 10.2 %multiply_convert_fusion = (bf16[1024,2304]{1,0:T(8,128)(2,1)}, f32[1024,2304]{1,0:T(8,128)}) fusion(f32[2304]{0:T(1024)S(1)} %copy-done.53, bf16[1024,1152]{1,0:T(8,128)(2,1)S(1)} %get-tuple-element.72, bf16[1152,2304]{1,0:T(8,128)(2,1)S(1)} %bitcast.227), kind=kOutput, calls=%fused_computation.10 | convolution fusion | flops 5459410944 | bytes 21832704 | tf_op jit(solution)/shard_map/dot_general | solution.py:248
  250.6 15.4 %convert_reduce_fusion = (f32[2304]{0:T(1024)S(1)}, bf16[1024,2304]{1,0:T(8,128)(2,1)}) fusion(f32[1024,2304]{1,0:T(8,128)} %get-tuple-element.138, f32[2304]{0:T(1024)S(1)} %copy-done.53, bf16[1152,2304]{1,0:T(8,128)(2,1)S(1)} %bitcast.188, f32[1152]{0:T(1024)S(1)} %get-tuple-element.59, bf16[512,1152]{1,0:T(8,128)(2,1)} %collective-permute-done.30, ...), kind=kOutput, calls=%fused_computation.9 | convolution fusion | flops 5494798336 | bytes 21846528 | tf_op jit(solution)/shard_map/dot_general | solution.py:248
  266.0 9.7 %convolution_convert_fusion = bf16[1024,1152]{1,0:T(8,128)(2,1)S(1)} fusion(bf16[1024,2304]{1,0:T(8,128)(2,1)} %get-tuple-element.140, bf16[1152,2304]{1,0:T(8,128)(2,1)} %bitcast.224), kind=kOutput, calls=%fused_computation.33 | convolution fusion | flops 5436997632 | bytes 12386304 | tf_op jit(solution)/shard_map/dot_general | solution.py:242
  285.1 8.3 %convolution_convert_fusion.1 = bf16[1024,1152]{1,0:T(8,128)(2,1)S(1)} fusion(bf16[1024,2304]{1,0:T(8,128)(2,1)} %get-tuple-element.137, bf16[1152,2304]{1,0:T(8,128)(2,1)S(1)} %bitcast.189), kind=kOutput, calls=%fused_computation.34 | convolution fusion | flops 5436997632 | bytes 12386304 | tf_op jit(solution)/shard_map/dot_general | solution.py:242
  332.2 13.2 %collective-permute-done.59 = bf16[2,4,144,640]{3,2,1,0:T(8,128)(2,1)S(1)} collective-permute-done((bf16[2,4,144,640]{3,2,1,0:T(8,128)(2,1)S(1)}, bf16[2,4,144,640]{3,2,1,0:T(8,128)(2,1)S(1)}, u32[]{:S(2)}, u32[]{:S(2)}) %collective-permute-start.59) | collective-permute-done | bytes 1474592 | tf_op jit(solution)/shard_map/ppermute | solution.py:51
  350.8 6.9 %convert_reduce_fusion.3 = (f32[1152]{0:T(1024)S(1)}, bf16[1024,1152]{1,0:T(8,128)(2,1)S(1)}, f32[1024,1152]{1,0:T(8,128)}, f32[1152]{0:T(1024)S(1)}) fusion(f32[1152]{0:T(1024)S(1)} %get-tuple-element.64, f32[1024,1152]{1,0:T(8,128)S(1)} %get-tuple-element.73, f32[1024]{0:T(1024)S(1)} %get-tuple-element.145, f32[1024]{0:T(1024)S(1)} %get-tuple-element.146, ...), kind=kLoop, calls=%fused_computation.19 | loop fusion | flops 28309248 | bytes 18909696 | tf_op jit(solution)/shard_map/reduce_sum | solution.py:574
  368.5 20.6 %collective-permute-done.58 = bf16[4,144,512]{2,1,0:T(8,128)(2,1)} collective-permute-done((bf16[4,144,512]{2,1,0:T(8,128)(2,1)}, bf16[4,144,512]{2,1,0:T(8,128)(2,1)}, u32[]{:S(2)}, u32[]{:S(2)}) %collective-permute-start.58) | collective-permute-done | bytes 589856 | tf_op jit(solution)/shard_map/ppermute | solution.py:51
  401.1 21.8 %attend_back.2 = bf16[1024,864]{1,0:T(8,128)(2,1)} custom-call(bf16[1024,1728]{1,0:T(8,128)(2,1)} %copy-done.1, bf16[1024,576]{1,0:T(8,128)(2,1)} %convolution_convert_fusion.7.g_ref, f32[8,1,1024]{2,1,0:T(1,128)} %reshape.340.lse_ref), custom_call_target="tpu_custom_call" | custom-call | flops 12079595520 | bytes 7077888 | tf_op jit(solution)/shard_map/attend_back/pallas_call | solution.py:389
  426.4 6.8 %fusion.16 = f32[1024,1152]{1,0:T(8,128)} fusion(bf16[1024,864]{1,0:T(8,128)(2,1)} %attend_back.2, bf16[1152,1728]{1,0:T(8,128)(2,1)S(1)} %bitcast.193), kind=kOutput, calls=%fused_computation.65 | convolution fusion | flops 2038431744 | bytes 8552448 | tf_op jit(solution)/shard_map/dot_general | solution.py:242
  436.3 21.2 %attend_back.3 = bf16[1024,864]{1,0:T(8,128)(2,1)} custom-call(bf16[1024,1728]{1,0:T(8,128)(2,1)} %copy-done.1, bf16[1024,576]{1,0:T(8,128)(2,1)} %convolution_convert_fusion.7.g_ref, f32[8,1,1024]{2,1,0:T(1,128)} %reshape.340.lse_ref), custom_call_target="tpu_custom_call" | custom-call | flops 12079595520 | bytes 7077888 | tf_op jit(solution)/shard_map/attend_back/pallas_call | solution.py:389
  463.3 5.6 convolution_convert_fusion.3
  474.8 7.8 %convolution_add_fusion = bf16[1024,1152]{1,0:T(8,128)(2,1)} fusion(f32[1024,1152]{1,0:T(8,128)} %fusion.16, bf16[1024,864]{1,0:T(8,128)(2,1)} %attend_back.3, bf16[1152,1728]{1,0:T(8,128)(2,1)} %bitcast.191), kind=kOutput, calls=%fused_computation.29 | convolution fusion | flops 2040791040 | bytes 10977280 | tf_op jit(solution)/shard_map/dot_general | solution.py:242
  482.6 5.0 fusion.70
  504.8 9.5 %collective-permute-done.62 = bf16[1,144,1152]{2,1,0:T(8,128)(2,1)S(1)} collective-permute-done((bf16[1,144,1152]{2,1,0:T(8,128)(2,1)S(1)}, bf16[1,144,1152]{2,1,0:T(8,128)(2,1)S(1)}, u32[]{:S(2)}, u32[]{:S(2)}) %collective-permute-start.62) | collective-permute-done | bytes 331808 | tf_op jit(solution)/shard_map/ppermute | solution.py:51
  525.5 5.1 collective-permute-done.49
  565.9 8.4 %collective-permute-done.42 = f32[1,2,4,144]{3,2,1,0:T(4,128)S(1)} collective-permute-done((f32[1,2,4,144]{3,2,1,0:T(4,128)S(1)}, f32[1,2,4,144]{3,2,1,0:T(4,128)S(1)}, u32[]{:S(2)}, u32[]{:S(2)}) %collective-permute-start.42) | collective-permute-done | bytes 4640 | tf_op jit(solution)/shard_map/ppermute | solution.py:51
  574.3 9.5 %collective-permute-done.44 = bf16[4,144,864]{2,1,0:T(8,128)(2,1)S(1)} collective-permute-done((bf16[4,144,864]{2,1,0:T(8,128)(2,1)S(1)}, bf16[4,144,864]{2,1,0:T(8,128)(2,1)S(1)}, u32[]{:S(2)}, u32[]{:S(2)}) %collective-permute-start.44) | collective-permute-done | bytes 995360 | tf_op jit(solution)/shard_map/ppermute | solution.py:51
  586.4 9.1 %collective-permute-done.45 = bf16[2,144,864]{2,1,0:T(8,128)(2,1)} collective-permute-done((bf16[2,144,864]{2,1,0:T(8,128)(2,1)S(1)}, bf16[2,144,864]{2,1,0:T(8,128)(2,1)}, u32[]{:S(2)}, u32[]{:S(2)}) %collective-permute-start.45) | collective-permute-done | bytes 497696 | tf_op jit(solution)/shard_map/ppermute | solution.py:51
  602.2 6.4 %collective-permute-done.46 = bf16[1,144,864]{2,1,0:T(8,128)(2,1)S(1)} collective-permute-done((bf16[1,144,864]{2,1,0:T(8,128)(2,1)S(1)}, bf16[1,144,864]{2,1,0:T(8,128)(2,1)S(1)}, u32[]{:S(2)}, u32[]{:S(2)}) %collective-permute-start.46) | collective-permute-done | bytes 248864 | tf_op jit(solution)/shard_map/ppermute | solution.py:51
  (469 shorter events, 278.7 us)
Async XLA Ops:
  10.7 27.8 %collective-permute-start.9 = (bf16[1,144,864]{2,1,0:T(8,128)(2,1)}, bf16[1,144,864]{2,1,0:T(8,128)(2,1)S(1)}, u32[]{:S(2)}, u32[]{:S(2)}) collective-permute-start(bf16[1,144,864]{2,1,0:T(8,128)(2,1)} %bitcast.217), channel_id=1, source_target_pairs={{0,16},{4,20},{8,24},{12,28},{16,0},{20,4},{24,8},{28,12},{1,17},{... | collective-permute-start | bytes 746504 | tf_op jit(solution)/shard_map/ppermute | solution.py:51
  13.3 54.9 %collective-permute-start = (bf16[512,1152]{1,0:T(8,128)(2,1)}, bf16[512,1152]{1,0:T(8,128)(2,1)S(1)}, u32[]{:S(2)}, u32[]{:S(2)}) collective-permute-start(bf16[512,1152]{1,0:T(8,128)(2,1)} %param.13), channel_id=1, source_target_pairs={{0,1},{1,0},{2,3},{3,2},{4,5},{5,4},{6,7},{7,6},{8,9},{9,8},{10,11... | collective-permute-start | bytes 3538952 | tf_op jit(solution)/shard_map/ppermute | solution.py:42
  68.1 20.6 %collective-permute-start.17 = (bf16[2,144,1440]{2,1,0:T(8,128)(2,1)S(1)}, bf16[2,144,1440]{2,1,0:T(8,128)(2,1)S(1)}, u32[]{:S(2)}, u32[]{:S(2)}) collective-permute-start(bf16[2,144,1440]{2,1,0:T(8,128)(2,1)S(1)} %pad_maximum_fusion.13), channel_id=1, source_target_pairs={{0,8},{4,12},{8,0},{12,4},{16,24},{20,28},{24,16},{28,20},{1,9},{5... | collective-permute-start | bytes 2488328 | tf_op jit(solution)/shard_map/ppermute | solution.py:51
  68.7 27.9 %collective-permute-start.14 = (bf16[8,144,384]{2,1,0:T(8,128)(2,1)S(1)}, bf16[8,144,384]{2,1,0:T(8,128)(2,1)S(1)}, u32[]{:S(2)}, u32[]{:S(2)}) collective-permute-start(bf16[8,144,384]{2,1,0:T(8,128)(2,1)S(1)} %pad_maximum_fusion.12), channel_id=1, source_target_pairs={{0,2},{1,3},{2,0},{3,1},{4,6},{5,7},{6,4},{7,5},{8,10},{9,11},{10,... | collective-permute-start | bytes 2654216 | tf_op jit(solution)/shard_map/ppermute | solution.py:46
  71.3 35.4 %collective-permute-start.13 = (bf16[8,144,480]{2,1,0:T(8,128)(2,1)S(1)}, bf16[8,144,480]{2,1,0:T(8,128)(2,1)S(1)}, u32[]{:S(2)}, u32[]{:S(2)}) collective-permute-start(bf16[8,144,480]{2,1,0:T(8,128)(2,1)S(1)} %pad_maximum_fusion.9), channel_id=1, source_target_pairs={{0,4},{4,0},{8,12},{12,8},{16,20},{20,16},{24,28},{28,24},{1,5},{5... | collective-permute-start | bytes 3317768 | tf_op jit(solution)/shard_map/ppermute | solution.py:51
  93.4 23.5 %collective-permute-start.18 = (bf16[4,144,672]{2,1,0:T(8,128)(2,1)}, bf16[4,144,672]{2,1,0:T(8,128)(2,1)}, u32[]{:S(2)}, u32[]{:S(2)}) collective-permute-start(bf16[4,144,672]{2,1,0:T(8,128)(2,1)} %slice.314.refs_0_), channel_id=1, source_target_pairs={{0,4},{4,0},{8,12},{12,8},{16,20},{20,16},{24,28},{28,24},{1,5},{5... | collective-permute-start | bytes 2322440 | tf_op jit(solution)/shard_map/ppermute | solution.py:51
  95.1 24.1 %collective-permute-start.19 = (bf16[4,144,768]{2,1,0:T(8,128)(2,1)}, bf16[4,144,768]{2,1,0:T(8,128)(2,1)}, u32[]{:S(2)}, u32[]{:S(2)}) collective-permute-start(bf16[4,144,768]{2,1,0:T(8,128)(2,1)} %slice.315.refs_2_), channel_id=1, source_target_pairs={{0,2},{1,3},{2,0},{3,1},{4,6},{5,7},{6,4},{7,5},{8,10},{9,11},{10,... | collective-permute-start | bytes 2654216 | tf_op jit(solution)/shard_map/ppermute | solution.py:46
  106.7 45.7 %collective-permute-start.24 = (bf16[2,144,1152]{2,1,0:T(8,128)(2,1)}, bf16[2,144,1152]{2,1,0:T(8,128)(2,1)}, u32[]{:S(2)}, u32[]{:S(2)}) collective-permute-start(bf16[2,144,1152]{2,1,0:T(8,128)(2,1)} %pad_maximum_fusion.16), channel_id=1, source_target_pairs={{0,8},{4,12},{8,0},{12,4},{16,24},{20,28},{24,16},{28,20},{1,9},{5... | collective-permute-start | bytes 1990664 | tf_op jit(solution)/shard_map/ppermute | solution.py:51
  118.6 39.7 %collective-permute-start.21 = (bf16[8,144,672]{2,1,0:T(8,128)(2,1)S(1)}, bf16[8,144,672]{2,1,0:T(8,128)(2,1)S(1)}, u32[]{:S(2)}, u32[]{:S(2)}) collective-permute-start(bf16[8,144,672]{2,1,0:T(8,128)(2,1)S(1)} %pad_maximum_fusion.5), channel_id=1, source_target_pairs={{0,2},{1,3},{2,0},{3,1},{4,6},{5,7},{6,4},{7,5},{8,10},{9,11},{10,... | collective-permute-start | bytes 4644872 | tf_op jit(solution)/shard_map/ppermute | solution.py:46
  122.0 41.7 %collective-permute-start.20 = (bf16[8,144,768]{2,1,0:T(8,128)(2,1)}, bf16[8,144,768]{2,1,0:T(8,128)(2,1)S(1)}, u32[]{:S(2)}, u32[]{:S(2)}) collective-permute-start(bf16[8,144,768]{2,1,0:T(8,128)(2,1)} %pad_maximum_fusion.4), channel_id=1, source_target_pairs={{0,4},{4,0},{8,12},{12,8},{16,20},{20,16},{24,28},{28,24},{1,5},{5... | collective-permute-start | bytes 5308424 | tf_op jit(solution)/shard_map/ppermute | solution.py:51
  154.3 30.2 %collective-permute-start.25 = (bf16[4,144,512]{2,1,0:T(8,128)(2,1)}, bf16[4,144,512]{2,1,0:T(8,128)(2,1)}, u32[]{:S(2)}, u32[]{:S(2)}) collective-permute-start(bf16[4,144,512]{2,1,0:T(8,128)(2,1)} %pad_maximum_fusion.17.refs_0_), channel_id=1, source_target_pairs={{0,4},{4,0},{8,12},{12,8},{16,20},{20,16},{24,28},{28,24},{1,5},{5... | collective-permute-start | bytes 1769480 | tf_op jit(solution)/shard_map/ppermute | solution.py:51
  156.7 23.6 %collective-permute-start.26 = (bf16[4,144,640]{2,1,0:T(8,128)(2,1)}, bf16[4,144,640]{2,1,0:T(8,128)(2,1)}, u32[]{:S(2)}, u32[]{:S(2)}) collective-permute-start(bf16[4,144,640]{2,1,0:T(8,128)(2,1)} %pad_maximum_fusion.14.refs_2_), channel_id=1, source_target_pairs={{0,2},{1,3},{2,0},{3,1},{4,6},{5,7},{6,4},{7,5},{8,10},{9,11},{10,... | collective-permute-start | bytes 2211848 | tf_op jit(solution)/shard_map/ppermute | solution.py:46
  179.8 48.6 %collective-permute-start.22 = (bf16[1024,1152]{1,0:T(8,128)(2,1)}, bf16[1024,1152]{1,0:T(8,128)(2,1)}, u32[]{:S(2)}, u32[]{:S(2)}) collective-permute-start(bf16[1024,1152]{1,0:T(8,128)(2,1)} %convolution_convert_fusion.2), channel_id=1, source_target_pairs={{0,1},{1,0},{2,3},{3,2},{4,5},{5,4},{6,7},{7,6},{8,9},{9,8},{10,11... | collective-permute-start | bytes 7077896 | tf_op jit(solution)/shard_map/ppermute | solution.py:42
  183.0 34.5 %collective-permute-start.27 = (bf16[8,144,640]{2,1,0:T(8,128)(2,1)}, bf16[8,144,640]{2,1,0:T(8,128)(2,1)}, u32[]{:S(2)}, u32[]{:S(2)}) collective-permute-start(bf16[8,144,640]{2,1,0:T(8,128)(2,1)} %pad_maximum_fusion.6), channel_id=1, source_target_pairs={{0,4},{4,0},{8,12},{12,8},{16,20},{20,16},{24,28},{28,24},{1,5},{5... | collective-permute-start | bytes 4423688 | tf_op jit(solution)/shard_map/ppermute | solution.py:51
  186.9 27.9 %collective-permute-start.28 = (bf16[8,144,512]{2,1,0:T(8,128)(2,1)}, bf16[8,144,512]{2,1,0:T(8,128)(2,1)}, u32[]{:S(2)}, u32[]{:S(2)}) collective-permute-start(bf16[8,144,512]{2,1,0:T(8,128)(2,1)} %pad_maximum_fusion.10), channel_id=1, source_target_pairs={{0,2},{1,3},{2,0},{3,1},{4,6},{5,7},{6,4},{7,5},{8,10},{9,11},{10,... | collective-permute-start | bytes 3538952 | tf_op jit(solution)/shard_map/ppermute | solution.py:46
  298.1 29.0 %collective-permute-start.57 = (bf16[4,2,144,512]{3,2,0,1:T(8,128)(2,1)S(1)}, bf16[4,2,144,512]{3,2,0,1:T(8,128)(2,1)S(1)}, u32[]{:S(2)}, u32[]{:S(2)}) collective-permute-start(bf16[4,2,144,512]{3,2,0,1:T(8,128)(2,1)S(1)} %copy.43), channel_id=1, source_target_pairs={{0,2},{1,3},{2,0},{3,1},{4,6},{5,7},{6,4},{7,5},{8,10},{9,11},{10,... | collective-permute-start | bytes 3538952 | tf_op jit(solution)/shard_map/ppermute | solution.py:46
  299.8 30.1 %collective-permute-start.29 = (bf16[512,1152]{1,0:T(8,128)(2,1)S(1)}, bf16[512,1152]{1,0:T(8,128)(2,1)S(1)}, u32[]{:S(2)}, u32[]{:S(2)}) collective-permute-start(bf16[512,1152]{1,0:T(8,128)(2,1)S(1)} %slice.329), channel_id=1, source_target_pairs={{0,1},{1,0},{2,3},{3,2},{4,5},{5,4},{6,7},{7,6},{8,9},{9,8},{10,11... | collective-permute-start | bytes 3538952 | tf_op jit(solution)/shard_map/ppermute | solution.py:42
  299.8 133.5 %collective-permute-start.51 = (bf16[4,2,144,512]{3,2,0,1:T(8,128)(2,1)}, bf16[4,2,144,512]{3,2,0,1:T(8,128)(2,1)}, u32[]{:S(2)}, u32[]{:S(2)}) collective-permute-start(bf16[4,2,144,512]{3,2,0,1:T(8,128)(2,1)} %copy.39), channel_id=1, source_target_pairs={{0,2},{1,3},{2,0},{3,1},{4,6},{5,7},{6,4},{7,5},{8,10},{9,11},{10,... | collective-permute-start | bytes 3538952 | tf_op jit(solution)/shard_map/ppermute | solution.py:46
  300.2 47.0 %collective-permute-start.31 = (bf16[1024,1152]{1,0:T(8,128)(2,1)S(1)}, bf16[1024,1152]{1,0:T(8,128)(2,1)S(1)}, u32[]{:S(2)}, u32[]{:S(2)}) collective-permute-start(bf16[1024,1152]{1,0:T(8,128)(2,1)S(1)} %convolution_convert_fusion), channel_id=1, source_target_pairs={{0,1},{1,0},{2,3},{3,2},{4,5},{5,4},{6,7},{7,6},{8,9},{9,8},{10,11... | collective-permute-start | bytes 7077896 | tf_op jit(solution)/shard_map/ppermute | solution.py:42
  310.3 35.1 %collective-permute-start.59 = (bf16[2,4,144,640]{3,2,1,0:T(8,128)(2,1)S(1)}, bf16[2,4,144,640]{3,2,1,0:T(8,128)(2,1)S(1)}, u32[]{:S(2)}, u32[]{:S(2)}) collective-permute-start(bf16[2,4,144,640]{3,2,1,0:T(8,128)(2,1)S(1)} %pad_maximum_fusion.8), channel_id=1, source_target_pairs={{0,4},{4,0},{8,12},{12,8},{16,20},{20,16},{24,28},{28,24},{1,5},{5... | collective-permute-start | bytes 4423688 | tf_op jit(solution)/shard_map/ppermute | solution.py:51
  327.1 95.8 %collective-permute-start.53 = (bf16[2,4,144,640]{3,2,1,0:T(8,128)(2,1)}, bf16[2,4,144,640]{3,2,1,0:T(8,128)(2,1)S(1)}, u32[]{:S(2)}, u32[]{:S(2)}) collective-permute-start(bf16[2,4,144,640]{3,2,1,0:T(8,128)(2,1)} %pad_maximum_fusion.7), channel_id=1, source_target_pairs={{0,4},{4,0},{8,12},{12,8},{16,20},{20,16},{24,28},{28,24},{1,5},{5... | collective-permute-start | bytes 4423688 | tf_op jit(solution)/shard_map/ppermute | solution.py:51
  329.9 59.2 %collective-permute-start.58 = (bf16[4,144,512]{2,1,0:T(8,128)(2,1)}, bf16[4,144,512]{2,1,0:T(8,128)(2,1)}, u32[]{:S(2)}, u32[]{:S(2)}) collective-permute-start(bf16[4,144,512]{2,1,0:T(8,128)(2,1)} %fusion.49), channel_id=1, source_target_pairs={{0,4},{4,0},{8,12},{12,8},{16,20},{20,16},{24,28},{28,24},{1,5},{5... | collective-permute-start | bytes 1769480 | tf_op jit(solution)/shard_map/ppermute | solution.py:51
  345.6 20.7 %collective-permute-start.60 = (bf16[4,144,640]{2,1,0:T(8,128)(2,1)S(1)}, bf16[4,144,640]{2,1,0:T(8,128)(2,1)S(1)}, u32[]{:S(2)}, u32[]{:S(2)}) collective-permute-start(bf16[4,144,640]{2,1,0:T(8,128)(2,1)S(1)} %fusion.20), channel_id=1, source_target_pairs={{0,2},{1,3},{2,0},{3,1},{4,6},{5,7},{6,4},{7,5},{8,10},{9,11},{10,... | collective-permute-start | bytes 2211848 | tf_op jit(solution)/shard_map/ppermute | solution.py:46
  398.7 95.9 %collective-permute-start.61 = (bf16[2,144,1152]{2,1,0:T(8,128)(2,1)}, bf16[2,144,1152]{2,1,0:T(8,128)(2,1)}, u32[]{:S(2)}, u32[]{:S(2)}) collective-permute-start(bf16[2,144,1152]{2,1,0:T(8,128)(2,1)} %fusion.47), channel_id=1, source_target_pairs={{0,8},{4,12},{8,0},{12,4},{16,24},{20,28},{24,16},{28,20},{1,9},{5... | collective-permute-start | bytes 1990664 | tf_op jit(solution)/shard_map/ppermute | solution.py:51
  399.6 96.7 %collective-permute-start.47 = (bf16[4,2,144,288]{3,2,1,0:T(8,128)(2,1)}, bf16[4,2,144,288]{3,2,1,0:T(8,128)(2,1)}, u32[]{:S(2)}, u32[]{:S(2)}) collective-permute-start(bf16[4,2,144,288]{3,2,1,0:T(8,128)(2,1)} %bitcast.31), channel_id=1, source_target_pairs={{0,2},{1,3},{2,0},{3,1},{4,6},{5,7},{6,4},{7,5},{8,10},{9,11},{10,... | collective-permute-start | bytes 1990664 | tf_op jit(solution)/shard_map/ppermute | solution.py:46
  461.2 31.8 %collective-permute-start.52 = (bf16[4,144,512]{2,1,0:T(8,128)(2,1)S(1)}, bf16[4,144,512]{2,1,0:T(8,128)(2,1)}, u32[]{:S(2)}, u32[]{:S(2)}) collective-permute-start(bf16[4,144,512]{2,1,0:T(8,128)(2,1)S(1)} %fusion.48), channel_id=1, source_target_pairs={{0,4},{4,0},{8,12},{12,8},{16,20},{20,16},{24,28},{28,24},{1,5},{5... | collective-permute-start | bytes 1769480 | tf_op jit(solution)/shard_map/ppermute | solution.py:51
  462.7 37.4 %collective-permute-start.54 = (bf16[4,144,640]{2,1,0:T(8,128)(2,1)}, bf16[4,144,640]{2,1,0:T(8,128)(2,1)}, u32[]{:S(2)}, u32[]{:S(2)}) collective-permute-start(bf16[4,144,640]{2,1,0:T(8,128)(2,1)} %fusion.22), channel_id=1, source_target_pairs={{0,2},{1,3},{2,0},{3,1},{4,6},{5,7},{6,4},{7,5},{8,10},{9,11},{10,... | collective-permute-start | bytes 2211848 | tf_op jit(solution)/shard_map/ppermute | solution.py:46
  473.2 84.0 %collective-permute-start.43 = (bf16[4,2,144,864]{3,2,1,0:T(8,128)(2,1)}, bf16[4,2,144,864]{3,2,1,0:T(8,128)(2,1)}, u32[]{:S(2)}, u32[]{:S(2)}) collective-permute-start(bf16[4,2,144,864]{3,2,1,0:T(8,128)(2,1)} %bitcast.205), channel_id=1, source_target_pairs={{0,2},{1,3},{2,0},{3,1},{4,6},{5,7},{6,4},{7,5},{8,10},{9,11},{10,... | collective-permute-start | bytes 5971976 | tf_op jit(solution)/shard_map/ppermute | solution.py:46
  493.0 22.2 %collective-permute-start.32 = (bf16[512,1152]{1,0:T(8,128)(2,1)}, bf16[512,1152]{1,0:T(8,128)(2,1)S(1)}, u32[]{:S(2)}, u32[]{:S(2)}) collective-permute-start(bf16[512,1152]{1,0:T(8,128)(2,1)} %slice.336), channel_id=1, source_target_pairs={{0,1},{1,0},{2,3},{3,2},{4,5},{5,4},{6,7},{7,6},{8,9},{9,8},{10,11... | collective-permute-start | bytes 3538952 | tf_op jit(solution)/shard_map/ppermute | solution.py:42
  502.8 54.5 %collective-permute-start.55 = (bf16[2,144,1152]{2,1,0:T(8,128)(2,1)}, bf16[2,144,1152]{2,1,0:T(8,128)(2,1)}, u32[]{:S(2)}, u32[]{:S(2)}) collective-permute-start(bf16[2,144,1152]{2,1,0:T(8,128)(2,1)} %fusion.46), channel_id=1, source_target_pairs={{0,8},{4,12},{8,0},{12,4},{16,24},{20,28},{24,16},{28,20},{1,9},{5... | collective-permute-start | bytes 1990664 | tf_op jit(solution)/shard_map/ppermute | solution.py:51
  560.6 23.2 %collective-permute-start.44 = (bf16[4,144,864]{2,1,0:T(8,128)(2,1)S(1)}, bf16[4,144,864]{2,1,0:T(8,128)(2,1)S(1)}, u32[]{:S(2)}, u32[]{:S(2)}) collective-permute-start(bf16[4,144,864]{2,1,0:T(8,128)(2,1)S(1)} %fusion.38), channel_id=1, source_target_pairs={{0,4},{4,0},{8,12},{12,8},{16,20},{20,16},{24,28},{28,24},{1,5},{5... | collective-permute-start | bytes 2985992 | tf_op jit(solution)/shard_map/ppermute | solution.py:51
  565.8 34.5 %collective-permute-start.56 = (bf16[1,144,1152]{2,1,0:T(8,128)(2,1)S(1)}, bf16[1,144,1152]{2,1,0:T(8,128)(2,1)}, u32[]{:S(2)}, u32[]{:S(2)}) collective-permute-start(bf16[1,144,1152]{2,1,0:T(8,128)(2,1)S(1)} %dynamic-slice_convert_fusion.8), channel_id=1, source_target_pairs={{0,16},{4,20},{8,24},{12,28},{16,0},{20,4},{24,8},{28,12},{1,17},{... | collective-permute-start | bytes 995336 | tf_op jit(solution)/shard_map/ppermute | solution.py:51
  (103 other events, 1238.2 us)

commit v3 on v2

v3 whole, which is shorter than its diff:
```python
import jax
import jax.numpy as jnp
from jax import lax
from jax.experimental import pallas as pl
from jax.experimental.pallas import tpu as pltpu
from jax.sharding import PartitionSpec as P

HEAD_DIM = 72
SEQ = 1024

highest = lax.Precision.HIGHEST
root_two_pi = 0.7978845608028654
cubic_term = 0.044715
epsilon = 1e-06
log2_e = 1.4426950408889634
bf16 = jnp.bfloat16
f32 = jnp.float32


def swap_cores(values):
    return lax.ppermute(values, "tensor", [(i, i ^ 1) for i in range(4)])


def swap_y(values):
    return lax.ppermute(values, "tensor", [(i, i ^ 2) for i in range(4)])


def swap_apart(values, apart):
    size = lax.axis_size("dp")
    return lax.ppermute(values, "dp", [(i, i ^ apart) for i in range(size)])


def swap_dp(values, bit):
    return swap_apart(values, 1 << bit)


def swap_diagonal(values):
    size = 4 * lax.axis_size("dp")
    return lax.ppermute(values, ("dp", "tensor"), [(i, i ^ 6) for i in range(size)])


def after(values, *deps):
    return lax.optimization_barrier((values, deps))[0]


def dp_bits():
    return lax.axis_size("dp").bit_length() - 1


def own_bit(bit):
    return (lax.axis_index("dp") >> bit) & 1


def ordered(flag, mine, theirs, axis):
    first = jnp.where(flag == 0, mine, theirs)
    second = jnp.where(flag == 0, theirs, mine)
    return jnp.concatenate([first, second], axis=axis)


def gather_small(values):
    for bit in range(dp_bits()):
        values = ordered(own_bit(bit), values, swap_dp(values, bit), 0)
    return values


def scatter_small(values):
    for bit in reversed(range(dp_bits())):
        halves = values.reshape((2, values.shape[0] // 2) + values.shape[1:])
        mine = own_bit(bit)
        keep = lax.dynamic_index_in_dim(halves, mine, 0, False)
        send = lax.dynamic_index_in_dim(halves, 1 - mine, 0, False)
        values = keep + swap_dp(send, bit)
    return values


def exchange_small(values):
    dp, k, n = values.shape
    values = values[:, :, None]
    for bit in range(dp_bits()):
        pairs = values.reshape((values.shape[0] // 2, 2) + values.shape[1:])
        mine = own_bit(bit)
        keep = lax.dynamic_index_in_dim(pairs, mine, 1, False)
        send = lax.dynamic_index_in_dim(pairs, 1 - mine, 1, False)
        values = ordered(mine, keep, swap_dp(send, bit), 2)
    return values.reshape(k, dp * n)


def width_of(weight):
    return weight[2] - weight[1]


def height_of(weight):
    return sum(piece.shape[0] for piece in weight[0])


def row_step(
    body, rows, block, row_inputs, flat_inputs, weights, row_outputs, sum_outputs, name, flops=0
):
    steps = rows // block
    arrays, specs = [], []
    for entry in row_inputs:
        array, index = entry if isinstance(entry, tuple) else (entry, lambda i: i)
        arrays.append(array)
        specs.append(pl.BlockSpec((block, array.shape[1]), lambda i, index=index: (index(i), 0)))
    for array in flat_inputs:
        arrays.append(array)
        specs.append(pl.BlockSpec(array.shape, lambda i, nd=array.ndim: (0,) * nd))
    spans = [
        (lo // 128 * 128, min(-(-hi // 128) * 128, pieces[0].shape[1])) for pieces, lo, hi in weights
    ]
    counts = [len(pieces) for pieces, _, _ in weights]
    for pieces, _, _ in weights:
        arrays += pieces
        specs += [pl.BlockSpec(memory_space=pl.ANY)] * len(pieces)
    outs, out_specs = [], []
    for columns, kind in row_outputs:
        outs.append(jax.ShapeDtypeStruct((rows, columns), kind))
        out_specs.append(pl.BlockSpec((block, columns), lambda i: (i, 0)))
    for count, columns in sum_outputs:
        outs.append(jax.ShapeDtypeStruct((count, columns), f32))
        out_specs.append(pl.BlockSpec((count, columns), lambda i: (0, 0)))
    scratch = []
    for weight, (lo, hi) in zip(weights, spans):
        scratch += [pltpu.VMEM((height_of(weight), hi - lo), bf16), pltpu.SemaphoreType.DMA((len(weight[0]),))]
    n_row, n_flat = len(row_inputs), len(flat_inputs)

    def kernel(*refs):
        refs = list(refs)

        def take(count):
            part = refs[:count]
            del refs[:count]
            return part

        row_refs, flat_refs = take(n_row), take(n_flat)
        weight_refs = [take(count) for count in counts]
        out_refs, sum_refs = take(len(row_outputs)), take(len(sum_outputs))
        targets = [take(2) for _ in weights]
        step = pl.program_id(0)

        @pl.when(step == 0)
        def _():
            copies = []
            for refs, (target, sems), (lo, hi) in zip(weight_refs, targets, spans):
                at = 0
                for i, ref in enumerate(refs):
                    rows = ref.shape[0]
                    copies.append(
                        pltpu.make_async_copy(
                            ref.at[:, lo:hi], target.at[at : at + rows], sems.at[i]
                        )
                    )
                    at += rows
            for copy in copies:
                copy.start()
            for ref in sum_refs:
                ref[...] = jnp.zeros_like(ref)
            for copy in copies:
                copy.wait()

        views = [
            target.at[:, lo - at : hi - at]
            for (target, _), (_, lo, hi), (at, _) in zip(targets, weights, spans)
        ]
        body(step, row_refs, flat_refs, views, out_refs, sum_refs)

    moved = sum(a.size * a.dtype.itemsize for a in arrays) + sum(
        o.size * o.dtype.itemsize for o in outs
    )
    return pl.pallas_call(
        kernel,
        out_shape=outs,
        grid=(steps,),
        in_specs=specs,
        out_specs=out_specs,
        scratch_shapes=scratch,
        compiler_params=pltpu.CompilerParams(vmem_limit_bytes=58 << 20),
        cost_estimate=pl.CostEstimate(flops=flops, transcendentals=0, bytes_accessed=moved),
        name=name,
    )(*arrays)


def dot_nt(left_rows, right_mat):
    return lax.dot_general(
        left_rows, right_mat, (((1,), (1,)), ((), ())), preferred_element_type=f32
    )


def dot_nn(left_rows, right_mat):
    return jnp.dot(left_rows, right_mat, preferred_element_type=f32)


def normed_of(values):
    centre = values - jnp.mean(values, axis=-1, keepdims=True)
    inverse = lax.rsqrt(jnp.mean(centre * centre, axis=-1, keepdims=True) + epsilon)
    return centre * inverse, inverse


def norm_back(normed, inverse, grad_in):
    mean_grad = jnp.mean(grad_in, axis=-1, keepdims=True)
    mean_cross = jnp.mean(grad_in * normed, axis=-1, keepdims=True)
    return inverse * (grad_in - mean_grad - normed * mean_cross)


def rows_sum(values):
    return jnp.sum(values, axis=0, keepdims=True)


def norm_project(tokens, scale, shift, bias, weight):
    rows, width = tokens.shape
    n = width_of(weight)

    def body(step, ins, flat, w, outs, sums):
        normed, _ = normed_of(ins[0][...].astype(f32))
        attn_in = (normed * (1.0 + flat[0][...]) + flat[1][...]).astype(bf16)
        outs[0][...] = attn_in
        outs[1][...] = (dot_nn(attn_in, w[0][...]) + flat[2][...]).astype(bf16)

    return row_step(
        body, rows, 256, [tokens], [scale, shift, bias], [weight],
        [(width, bf16), (n, bf16)], [], "norm_project",
    )


def project(values, bias, weight):
    n = width_of(weight)

    def body(step, ins, flat, w, outs, sums):
        outs[0][...] = (dot_nn(ins[0][...], w[0][...]) + flat[0][...]).astype(bf16)

    return row_step(body, values.shape[0], 256, [values], [bias], [weight], [(n, bf16)], [], "project")[0]


def project_out(mix_near, mix_far, near, far):
    def body(step, ins, flat, w, outs, sums):
        total = dot_nt(ins[0][...], w[0][...]) + dot_nt(ins[1][...], w[1][...])
        outs[0][...] = total.astype(bf16)

    width = height_of(near)
    rows = mix_near.shape[0]
    return row_step(
        body, rows, 256, [mix_near, mix_far], [], [near, far], [(width, bf16)], [], "project_out"
    )[0]


def other_half(steps):
    return lambda i: jnp.where(i < steps // 2, i + steps // 2, i - steps // 2)


def middle_norm(mine, theirs, tokens, cotangent, b_proj, gate_attn, scale_mlp, shift_mlp, gate_mlp):
    rows, width = tokens.shape
    block = 256

    def body(step, ins, flat, w, outs, sums):
        attn_out = ins[0][...].astype(f32) + ins[1][...].astype(f32) + flat[0][...]
        middle = ins[2][...].astype(f32) + flat[1][...] * attn_out
        outs[0][...] = middle
        normed, _ = normed_of(middle)
        outs[1][...] = (normed * (1.0 + flat[2][...]) + flat[3][...]).astype(bf16)
        grad_mlp = (flat[4][...] * ins[3][...].astype(f32)).astype(bf16)
        outs[2][...] = grad_mlp
        sums[0][...] += rows_sum(grad_mlp.astype(f32))

    return row_step(
        body, rows, block, [mine, (theirs, other_half(rows // block)), tokens, cotangent],
        [b_proj, gate_attn, scale_mlp, shift_mlp, gate_mlp], [],
        [(width, f32), (width, bf16), (width, bf16)], [(1, width)], "middle_norm",
    )


def gelu_parts(pre_act):
    tangent = jnp.tanh(root_two_pi * (pre_act + cubic_term * pre_act * pre_act * pre_act))
    activated = 0.5 * pre_act * (1.0 + tangent)
    gelu_slope = 0.5 * (1.0 + tangent) + 0.5 * pre_act * (1.0 - tangent * tangent) * root_two_pi * (
        1.0 + 3.0 * cubic_term * pre_act * pre_act
    )
    return activated, gelu_slope


def feed_forward(mlp_in, bias, weight):
    n = width_of(weight)

    def body(step, ins, flat, w, outs, sums):
        activated, slope = gelu_parts(dot_nn(ins[0][...], w[0][...]) + flat[0][...])
        outs[0][...] = activated.astype(bf16)
        outs[1][...] = slope

    return row_step(
        body, mlp_in.shape[0], 256, [mlp_in], [bias], [weight], [(n, bf16), (n, f32)], [], "feed_forward"
    )


def feed_back(grad_mlp, act, slope, added, fc1, fc2, kind):
    rows, width = grad_mlp.shape
    n = act.shape[1]

    def body(step, ins, flat, w, outs, sums):
        grad_pre = (dot_nn(ins[0][...], w[1][...]) * ins[2][...]).astype(bf16)
        outs[0][...] = grad_pre
        sums[0][...] += rows_sum(grad_pre.astype(f32))
        grad_in = dot_nt(grad_pre, w[0][...])
        out = dot_nt(ins[1][...], w[1][...])
        if added is not None:
            grad_in = grad_in + ins[3][...]
            out = out + ins[4][...]
        outs[1][...] = grad_in.astype(kind)
        outs[2][...] = out.astype(kind)

    return row_step(
        body, rows, 256, [grad_mlp, act, slope] + ([] if added is None else list(added)), [], [fc1, fc2],
        [(n, bf16), (width, kind), (width, kind)], [(1, n)], "feed_back",
    )


def middle_back(
    grad_mine, grad_theirs, middle, cotangent, mine, theirs, b_proj, gate_attn, scale_mlp, near, far
):
    rows, width = middle.shape
    block = 256
    steps = rows // block
    n = width_of(near)

    def body(step, ins, flat, w, outs, sums):
        grad_in = ins[0][...].astype(f32) + ins[1][...].astype(f32)
        normed, inverse = normed_of(ins[2][...])
        grad_middle = ins[3][...].astype(f32) + norm_back(
            normed, inverse, grad_in * (1.0 + flat[2][...])
        )
        outs[0][...] = grad_middle
        grad_attn = (flat[1][...] * grad_middle).astype(bf16)
        outs[1][...] = grad_attn
        outs[2][...] = dot_nn(grad_attn, w[0][...]).astype(bf16)
        outs[3][...] = dot_nn(grad_attn, w[1][...]).astype(bf16)
        sums[0][3:4] += rows_sum(grad_attn.astype(f32))

        @pl.when(step < steps // 2)
        def _():
            attn_out = ins[4][...].astype(f32) + ins[5][...].astype(f32) + flat[0][...]
            sums[0][0:1] += rows_sum(grad_in)
            sums[0][1:2] += rows_sum(grad_in * normed)
            sums[0][2:3] += rows_sum(grad_middle * attn_out)

    flip = other_half(steps)
    return row_step(
        body, rows, block,
        [grad_mine, (grad_theirs, flip), middle, cotangent, mine, (theirs, flip)],
        [b_proj, gate_attn, scale_mlp], [near, far],
        [(width, f32), (width, bf16), (n, bf16), (n, bf16)], [(8, width)], "middle_back",
    )


def project_back(grads, weight, added, kind):
    width = height_of(weight)

    def body(step, ins, flat, w, outs, sums):
        total = dot_nt(ins[0][...], w[0][...])
        if added is not None:
            total = total + ins[1][...]
        outs[0][...] = total.astype(kind)

    inputs = [grads] if added is None else [grads, added]
    return row_step(
        body, grads.shape[0], 256, inputs, [], [weight], [(width, kind)], [], "project_back"
    )[0]


def first_back(mine, theirs, tokens, grad_middle, scale_attn):
    rows, width = tokens.shape

    def body(step, ins, flat, w, outs, sums):
        grad_in = ins[0][...].astype(f32) + ins[1][...].astype(f32)
        normed, inverse = normed_of(ins[2][...].astype(f32))
        outs[0][...] = ins[3][...] + norm_back(normed, inverse, grad_in * (1.0 + flat[0][...]))
        sums[0][0:1] += rows_sum(grad_in)
        sums[0][1:2] += rows_sum(grad_in * normed)

    return row_step(
        body, rows, 256, [mine, theirs, tokens, grad_middle], [scale_attn], [],
        [(width, f32)], [(8, width)], "first_back",
    )


def finish(mine, theirs, middle, cotangent, b_fc2, gate_mlp):
    rows, width = cotangent.shape

    def body(step, ins, flat, w, outs, sums):
        mlp_out = ins[0][...].astype(f32) + ins[1][...].astype(f32) + flat[0][...]
        outs[0][...] = (ins[2][...] + flat[1][...] * mlp_out).astype(bf16)
        sums[0][...] += rows_sum(ins[3][...].astype(f32) * mlp_out)

    return row_step(
        body, rows, 256, [mine, theirs, middle, cotangent], [b_fc2, gate_mlp], [],
        [(width, bf16)], [(1, width)], "finish",
    )


def gather_start(shard):
    half = lax.axis_size("dp") // 2
    if half <= 4:
        return [shard] + [swap_apart(shard, 2 * r) for r in range(1, half)]
    blocks = shard[None]
    for bit in range(1, dp_bits()):
        blocks = jnp.concatenate([blocks, swap_dp(blocks, bit)], axis=0)
    return list(blocks)


def gather_end(mine, theirs):
    half, rows, n = mine.shape
    blocks = jnp.stack([mine, theirs], axis=1).reshape(2 * half, rows, n)
    for bit in range(dp_bits()):
        pairs = blocks.reshape(half >> bit, 2, 1 << bit, rows, n)
        blocks = jnp.where(own_bit(bit) == 0, pairs, pairs[:, ::-1]).reshape(blocks.shape)
    return blocks.reshape(2 * half * rows, n)


def split_bit(blocks, axis, bit):
    mine = own_bit(bit)
    keep = lax.dynamic_index_in_dim(blocks, mine, axis, False)
    send = lax.dynamic_index_in_dim(blocks, 1 - mine, axis, False)
    return keep, send.astype(bf16)


def weight_term(left, right, kind):
    out = lax.dot_general(left, right, (((0,), (0,)), ((), ())), preferred_element_type=f32)
    dp = lax.axis_size("dp")
    return out.astype(kind).reshape(dp // 2, 2, out.shape[0] // dp, out.shape[1])


def relay_first(far):
    keep, other = split_bit(far, 1, 0)
    half = other.shape[0] // 2
    return keep, other[:half], other[half:]


def relay_sends(near, far_keep, by_x, by_y):
    near_keep, near_other = split_bit(near, 1, 0)
    half = by_x.shape[0]
    to_x = jnp.concatenate([near_other[:half], near_other[half:] + by_y], axis=0)
    to_y = jnp.concatenate([far_keep[:half] + by_x, far_keep[half:]], axis=0)
    return near_keep, to_x, to_y


def scatter_z_sends(total):
    half = total.shape[0]
    if half > 4:
        for bit in range(dp_bits() - 1, 1, -1):
            blocks = total.reshape((2, total.shape[0] // 2) + total.shape[1:])
            keep, send = split_bit(blocks, 0, bit)
            total = keep + swap_dp(send, bit).astype(f32)
        keep, send = split_bit(total, 0, 1)
        return keep, [send]
    here = lax.axis_index("dp") >> 1
    sends = [
        lax.dynamic_index_in_dim(total, here ^ r, 0, False).astype(bf16) for r in range(1, half)
    ]
    return lax.dynamic_index_in_dim(total, here, 0, False), sends


def scatter_z(sends):
    return [swap_apart(send, 2 * (r + 1)) for r, send in enumerate(sends)]


def add_all(keep, got):
    for part in got:
        keep = keep + part.astype(f32)
    return keep


def attend(qkv, block=512, unroll=2):
    rows, cols = qkv.shape
    size = HEAD_DIM
    heads = cols // (3 * size)
    factor = size ** (-0.5) * log2_e

    def kernel(x_ref, mix_ref, lse_ref, q_s, k_s, v_s, o_s, l_s):
        i = pl.program_id(0)

        @pl.when(i == 0)
        def _():
            for h in range(heads):
                b = h * 3 * size
                q_s[h] = x_ref[:, b : b + size]
                k_s[h] = x_ref[:, b + size : b + 2 * size]
                v_s[h] = x_ref[:, b + 2 * size : b + 3 * size]

        def one(h):
            q = q_s[h, pl.ds(pl.multiple_of(i * block, block), block), :]
            scores = lax.dot_general(
                q, k_s[h], (((1,), (1,)), ((), ())), preferred_element_type=f32
            )
            top = jnp.max(scores, axis=-1, keepdims=True)
            probs = jnp.exp2((scores - top) * factor)
            total = jnp.sum(probs, axis=-1, keepdims=True)
            out = jnp.dot(probs.astype(bf16), v_s[h], preferred_element_type=f32)
            o_s[h] = (out / total).astype(bf16)
            l_s[h] = top * factor + jnp.log2(total)

        def body(g, _):
            for u in range(unroll):
                one(g * unroll + u)
            return 0

        lax.fori_loop(0, heads // unroll, body, 0)
        for h in range(heads):
            mix_ref[:, h * size : (h + 1) * size] = o_s[h]
            lse_ref[:, h : h + 1] = l_s[h]

    return pl.pallas_call(
        kernel,
        out_shape=(
            jax.ShapeDtypeStruct((rows, heads * size), bf16),
            jax.ShapeDtypeStruct((rows, heads), f32),
        ),
        grid=(rows // block,),
        in_specs=[pl.BlockSpec((rows, cols), lambda i: (0, 0))],
        out_specs=(
            pl.BlockSpec((block, heads * size), lambda i: (i, 0)),
            pl.BlockSpec((block, heads), lambda i: (i, 0)),
        ),
        scratch_shapes=[pltpu.VMEM((heads, rows, size), bf16)] * 3
        + [pltpu.VMEM((heads, block, size), bf16), pltpu.VMEM((heads, block, 1), f32)],
        compiler_params=pltpu.CompilerParams(vmem_limit_bytes=48 << 20),
        cost_estimate=pl.CostEstimate(
            flops=16 * heads * rows * rows * size,
            transcendentals=heads * rows * rows,
            bytes_accessed=rows * cols * 2 + rows * heads * size * 2,
        ),
        name="attend",
    )(qkv)


def attend_back(qkv, grad_mix, lse, first, heads, block=512, unroll=2):
    rows, cols = qkv.shape
    size = HEAD_DIM
    all_heads = cols // (3 * size)
    factor = size ** (-0.5) * log2_e
    scale = size ** (-0.5)
    steps = rows // block

    def kernel(x_ref, g_ref, lse_ref, out_ref, q_s, k_s, v_s, g_s, dq_s, dk_s, dv_s):
        i = pl.program_id(0)

        @pl.when(i == 0)
        def _():
            for h in range(heads):
                b = (first + h) * 3 * size
                q_s[h] = x_ref[:, b : b + size]
                k_s[h] = x_ref[:, b + size : b + 2 * size]
                v_s[h] = x_ref[:, b + 2 * size : b + 3 * size]
                g_s[h] = g_ref[:, (first + h) * size : (first + h + 1) * size]
            dk_s[...] = jnp.zeros_like(dk_s)
            dv_s[...] = jnp.zeros_like(dv_s)

        at = pl.ds(pl.multiple_of(i * block, block), block)

        def one(h):
            q = q_s[h, at, :]
            g = g_s[h, at, :]
            k = k_s[h]
            scores = lax.dot_general(k, q, (((1,), (1,)), ((), ())), preferred_element_type=f32)
            probs = jnp.exp2(scores * factor - lse_ref[first + h, :, at])
            grad_probs = lax.dot_general(
                v_s[h], g, (((1,), (1,)), ((), ())), preferred_element_type=f32
            )
            inner = jnp.sum(probs * grad_probs, axis=0, keepdims=True)
            grad_scores = (probs * (grad_probs - inner)).astype(bf16)
            dv_s[h] += jnp.dot(probs.astype(bf16), g, preferred_element_type=f32)
            dk_s[h] += jnp.dot(grad_scores, q, preferred_element_type=f32)
            grad_q = lax.dot_general(
                grad_scores, k, (((0,), (0,)), ((), ())), preferred_element_type=f32
            )
            dq_s[h, at, :] = (grad_q * scale).astype(bf16)

        def body(g, _):
            for u in range(unroll):
                one(g * unroll + u)
            return 0

        lax.fori_loop(0, heads // unroll, body, 0)

        @pl.when(i == steps - 1)
        def _():
            for h in range(heads):
                b = h * 3 * size
                out_ref[:, b : b + size] = dq_s[h]
                out_ref[:, b + size : b + 2 * size] = (dk_s[h] * scale).astype(bf16)
                out_ref[:, b + 2 * size : b + 3 * size] = dv_s[h].astype(bf16)

    return pl.pallas_call(
        kernel,
        out_shape=jax.ShapeDtypeStruct((rows, heads * 3 * size), bf16),
        grid=(steps,),
        in_specs=[
            pl.BlockSpec((rows, cols), lambda i: (0, 0)),
            pl.BlockSpec((rows, all_heads * size), lambda i: (0, 0)),
            pl.BlockSpec((all_heads, 1, rows), lambda i: (0, 0, 0)),
        ],
        out_specs=pl.BlockSpec((rows, heads * 3 * size), lambda i: (0, 0)),
        scratch_shapes=[pltpu.VMEM((heads, rows, size), bf16)] * 5
        + [pltpu.VMEM((heads, rows, size), f32)] * 2,
        compiler_params=pltpu.CompilerParams(vmem_limit_bytes=56 << 20),
        cost_estimate=pl.CostEstimate(
            flops=40 * heads * rows * rows * size,
            transcendentals=heads * rows * rows,
            bytes_accessed=rows * cols * 4,
        ),
        name="attend_back",
    )(qkv, grad_mix, lse)


def shards(
    tokens_in,
    condition,
    w_ada,
    b_ada,
    w_qkv,
    b_qv,
    w_proj,
    b_proj,
    w_fc1,
    b_fc1,
    w_fc2,
    b_fc2,
    cotangent,
):
    tok_rows, width = tokens_in.shape
    head_size = HEAD_DIM
    dp_at = lax.axis_index("dp")
    t_at = lax.axis_index("tensor")
    y_at = t_at // 2
    core_at = t_at % 2
    dp_size = lax.axis_size("dp")
    ada_rows, ada_cols = w_ada.shape
    n_qkv, n_proj, n_fc1, n_fc2 = w_qkv.shape[1], w_proj.shape[0], w_fc1.shape[1], w_fc2.shape[0]
    n_bqv = b_qv.shape[0]
    heads = n_qkv // (3 * head_size)

    latents = condition.shape[0]
    cond_all = gather_small(condition)

    gather = lambda shard: lax.all_gather(shard, "dp", axis=0, tiled=True)
    qkv_all = gather(jnp.pad(w_qkv, ((0, 0), (0, -n_qkv % 128))))
    fc1_all = gather(w_fc1)
    fc2_mine, proj_mine = w_fc2.T, w_proj.T
    theirs = swap_y(jnp.concatenate([fc2_mine, proj_mine], axis=1))
    fc2_all = gather(jnp.concatenate([fc2_mine, theirs[:, :n_fc2]], axis=1))
    proj_z = gather_start(jnp.concatenate([proj_mine, theirs[:, n_fc2:]], axis=1))
    qkv_theirs = swap_y(qkv_all)
    qkv_near, qkv_far = ((qkv_all,), 0, n_qkv), ((qkv_theirs,), 0, n_qkv)
    fc2_near, fc2_far = ((fc2_all,), 0, n_fc2), ((fc2_all,), n_fc2, 2 * n_fc2)
    fc1_theirs = swap_y(after(fc1_all, qkv_theirs))
    fc1_near, fc1_far = ((fc1_all,), 0, n_fc1), ((fc1_theirs,), 0, n_fc1)

    inputs_theirs = swap_cores(jnp.concatenate([tokens_in, cotangent], axis=0))
    tokens_all = jnp.concatenate([tokens_in, inputs_theirs[:tok_rows]], axis=0)
    cot_all = jnp.concatenate([cotangent, inputs_theirs[tok_rows:]], axis=0)

    cond_vals = cond_all.astype(f32)
    silu_all = (cond_vals * jax.nn.sigmoid(cond_vals)).astype(bf16)
    silu_mine = lax.dynamic_slice_in_dim(silu_all, dp_at * ada_rows, ada_rows, 1)
    mod_part = jnp.dot(silu_mine, w_ada, preferred_element_type=f32)
    mod_part = mod_part + jnp.where(dp_at == 0, b_ada.astype(f32), 0.0)
    by_y = mod_part.reshape(dp_size, 2, ada_cols)
    mod_keep = lax.dynamic_index_in_dim(by_y, y_at, 1, True)
    mod_send = lax.dynamic_index_in_dim(by_y, 1 - y_at, 1, False)
    bias_mine = jnp.concatenate([b_qv, b_fc1]).astype(f32)[None]
    mod_got = swap_y(jnp.concatenate([mod_send, bias_mine], axis=0))
    bias_theirs = mod_got[dp_size:]
    mod_two = ordered(y_at, mod_keep, mod_got[:dp_size, None], 1)
    mod_all = ordered(core_at, mod_two[:, :, None], swap_cores(mod_two)[:, :, None], 2)
    mod_all = mod_all.reshape(dp_size, 4 * ada_cols)
    for bit in range(dp_bits()):
        pairs = mod_all.reshape(mod_all.shape[0] // 2, 2, 4 * ada_cols)
        keep = lax.dynamic_index_in_dim(pairs, own_bit(bit), 1, False)
        send = lax.dynamic_index_in_dim(pairs, 1 - own_bit(bit), 1, False)
        mod_all = keep + swap_dp(send, bit)
    mod_row = after(mod_all, tokens_all, cot_all)

    shift_attn, scale_attn, gate_attn, shift_mlp, scale_mlp, gate_mlp = jnp.split(mod_row, 6, axis=1)

    def qkv_bias(values):
        pair = values[0, :n_bqv].reshape(heads, 2, head_size)
        return jnp.stack([pair[:, 0], jnp.zeros_like(pair[:, 0]), pair[:, 1]], axis=1).reshape(1, n_qkv)

    attn_in, qkv_n = norm_project(tokens_all, scale_attn, shift_attn, qkv_bias(bias_mine), qkv_near)
    mix_n, lse_n = attend(qkv_n)
    proj_own = jnp.stack(after(proj_z, mix_n))
    proj_theirs = swap_dp(proj_own, 0)
    qkv_f = project(after(attn_in, mix_n, proj_own), qkv_bias(bias_theirs), qkv_far)
    mix_f, lse_f = attend(qkv_f)
    proj_all = gather_end(proj_own, after(proj_theirs, mix_f))
    proj_near, proj_far = ((proj_all,), 0, n_proj), ((proj_all,), n_proj, 2 * n_proj)
    proj_row = b_proj.astype(f32)[None]
    out_mine = project_out(mix_n, mix_f, proj_near, proj_far)
    out_theirs = swap_cores(out_mine)
    middle, mlp_in, grad_mlp, grad_b2 = middle_norm(
        out_mine, out_theirs, tokens_all, cot_all, proj_row,
        gate_attn, scale_mlp, shift_mlp, gate_mlp,
    )

    act_n, slope_n = feed_forward(mlp_in, bias_mine[:, n_bqv:], fc1_near)
    act_f, slope_f = feed_forward(after(mlp_in, act_n), bias_theirs[:, n_bqv:], fc1_far)

    fc2_term_f = weight_term(grad_mlp, act_f, bf16)
    fc2_far_keep, *sends = relay_first(fc2_term_f)
    by_x, by_y = swap_dp(sends[0], 0), swap_y(sends[1])
    fc2_term_n = weight_term(grad_mlp, act_n, f32)
    pre_n, grad_in_near, mlp_near, b1_n = feed_back(
        after(grad_mlp, fc2_term_n, fc2_far_keep, sends), act_n, slope_n, None, fc1_near, fc2_near, f32
    )
    by_x, by_y = after((by_x, by_y), grad_in_near)
    fc2_keep, *sends = relay_sends(fc2_term_n, fc2_far_keep, by_x, by_y)
    fc2_got = swap_dp(sends[0], 0), swap_y(sends[1])
    pre_f, grad_in_mine, mlp_part, b1_f = feed_back(
        after(grad_mlp, sends), act_f, slope_f, (grad_in_near, mlp_near), fc1_far, fc2_far, bf16
    )
    grad_in_theirs = swap_cores(grad_in_mine)
    fc1_term_f = weight_term(mlp_in, after(pre_f, grad_in_mine), bf16)
    fc1_far_keep, *sends = relay_first(fc1_term_f)
    by_x, by_y = swap_dp(sends[0], 0), swap_y(sends[1])
    fc1_term_n = weight_term(mlp_in, pre_n, f32)
    fc2_got = after(fc2_got, fc1_term_n)
    fc2_keep, z_sends = scatter_z_sends(add_all(fc2_keep, fc2_got))
    grad_middle, grad_attn, gmix_n, gmix_f, mid_sums = middle_back(
        after(grad_in_mine, fc1_term_n, fc1_far_keep, sends, z_sends), grad_in_theirs, middle, cot_all,
        out_mine, out_theirs, proj_row, gate_attn, scale_mlp, proj_near, proj_far,
    )
    fc2_got = scatter_z(z_sends)

    proj_term_f = weight_term(grad_attn, mix_f, bf16)
    proj_term_n = weight_term(grad_attn, mix_n, f32)
    by_x, by_y = after((by_x, by_y), proj_term_n, fc2_got)
    fc1_keep, *sends = relay_sends(fc1_term_n, fc1_far_keep, by_x, by_y)
    fc1_got = swap_dp(sends[0], 0), swap_y(sends[1])
    rows_of = lambda lse: lse.T.reshape(heads, 1, 2 * tok_rows)
    grad_f = attend_back(
        qkv_f, after(gmix_f, proj_term_f, proj_term_n, sends), rows_of(lse_f), 0, heads
    )
    one_term_f = jnp.concatenate([weight_term(attn_in, grad_f, bf16), proj_term_f], axis=3)
    one_far_keep, *sends = relay_first(one_term_f)
    by_x, by_y = swap_dp(sends[0], 0), swap_y(sends[1])
    part_f = project_back(after(grad_f, sends), qkv_far, None, f32)
    fc1_got = after(fc1_got, part_f)
    fc1_keep, z_sends = scatter_z_sends(add_all(fc1_keep, fc1_got))
    fc1_got = scatter_z(z_sends)
    grad_n = attend_back(
        qkv_n, after(gmix_n, part_f, one_far_keep, z_sends), rows_of(lse_n), 0, heads
    )
    attn_part = project_back(after(grad_n, by_x, by_y), qkv_near, part_f, bf16)
    attn_theirs = swap_cores(attn_part[tok_rows:])
    one_term_n = jnp.concatenate(
        [weight_term(after(attn_in, attn_part, fc1_got), grad_n, f32), proj_term_n], axis=3
    )
    one_keep, *sends = relay_sends(one_term_n, one_far_keep, by_x, by_y)
    one_got = swap_dp(sends[0], 0), swap_y(sends[1])
    grad_tokens, one_sums = first_back(
        after(attn_part, sends), attn_theirs, tokens_in, grad_middle, scale_attn
    )
    mlp_theirs = swap_cores(after(mlp_part[tok_rows:], grad_n))
    result, gate_sums = finish(mlp_part, mlp_theirs, middle, cotangent, b_fc2.astype(f32)[None], gate_mlp)

    def value_sums(grads):
        sums = jnp.sum(grads.astype(f32), axis=0).reshape(heads, 3, head_size)
        return jnp.concatenate([sums[:, :1], sums[:, 2:]], axis=1).reshape(n_bqv)

    mod_sums = jnp.concatenate([one_sums[:2].reshape(-1), mid_sums[2], mid_sums[0], mid_sums[1], gate_sums[0]])
    mod_sums = mod_sums + swap_cores(mod_sums)
    sums = jnp.concatenate(
        [value_sums(grad_n), b1_n[0], mid_sums[3], grad_b2[0], value_sums(grad_f), b1_f[0]]
    )
    grad_mod = mod_sums[None]
    for bit in list(range(1, dp_bits())) + [0]:
        size = grad_mod.size
        if bit == 1:
            grad_mod = after(grad_mod, one_got)
        if bit == 0:
            one_keep, one_sends = scatter_z_sends(add_all(one_keep, after(one_got, grad_mod)))
            grad_mod = after(grad_mod, one_sends)
        got = swap_dp(jnp.concatenate([grad_mod.reshape(size), sums]), bit)
        theirs = got[:size].reshape(grad_mod.shape)
        if bit == 0:
            both = jnp.where(own_bit(0) == 0, jnp.stack([grad_mod, theirs], 1), jnp.stack([theirs, grad_mod], 1))
            grad_mod = both.reshape(dp_size, 4, ada_cols)
        else:
            grad_mod = ordered(own_bit(bit), grad_mod, theirs, 0)
        sums = sums + got[size:]
    mod_keep = lax.dynamic_index_in_dim(grad_mod, t_at, 1, False)
    mod_send = lax.dynamic_index_in_dim(grad_mod, t_at ^ 2, 1, False)
    n_bias = n_bqv + n_fc1
    shared = n_bias + 2 * width
    got = swap_y(jnp.concatenate([mod_send.reshape(-1), sums[n_bias:shared], sums[shared:]]))
    mod_got, rest = got[: mod_send.size].reshape(mod_send.shape), got[mod_send.size :]
    bias_sums = sums[:n_bias] + rest[2 * width :]
    out_sums = sums[n_bias:shared] + rest[: 2 * width]
    grad_mod = ordered(y_at, mod_keep[:, None], mod_got[:, None], 1).reshape(2 * dp_size, ada_cols)
    one_got = scatter_z(one_sends)
    owned_ada = lax.dot_general(
        silu_mine.astype(f32), after(grad_mod, one_sends), (((0,), (0,)), ((), ())), precision=highest
    )
    grad_ba = jnp.sum(grad_mod, axis=0)
    silu_part = lax.dot_general(
        after(grad_mod, one_sends), w_ada.astype(f32), (((1,), (1,)), ((), ())), precision=highest
    )
    silu_part = silu_part + swap_cores(silu_part)
    silu_part = silu_part + swap_y(silu_part)
    owned_one = add_all(one_keep, one_got)
    grad_silu = exchange_small(silu_part.reshape(dp_size, latents, ada_rows))
    cond_vals = condition.astype(f32)
    cond_sigmoid = jax.nn.sigmoid(cond_vals)
    grad_condition = grad_silu * cond_sigmoid * (1.0 + cond_vals * (1.0 - cond_sigmoid))
    return (
        result,
        grad_tokens,
        grad_condition,
        owned_ada,
        grad_ba,
        owned_one[:, :n_qkv],
        bias_sums[:n_bqv],
        owned_one[:, n_qkv:].T,
        out_sums[:width],
        add_all(fc1_keep, fc1_got),
        bias_sums[n_bqv:],
        add_all(fc2_keep, fc2_got).T,
        out_sums[width:],
    )


def solution(mesh):
    placed = (
        P(("dp", "tensor"), None),
        P("dp", None),
        P("dp", "tensor"),
        P("tensor"),
        P("dp", "tensor"),
        P("tensor"),
        P("tensor", "dp"),
        P(),
        P("dp", "tensor"),
        P("tensor"),
        P("tensor", "dp"),
        P(),
        P(("dp", "tensor"), None),
    )
    return jax.shard_map(
        shards,
        mesh=mesh,
        in_specs=placed,
        out_specs=(
            P(("dp", "tensor"), None),
            P(("dp", "tensor"), None),
            P("dp", None),
            P("dp", "tensor"),
            P("tensor"),
            P("dp", "tensor"),
            P("tensor"),
            P("tensor", "dp"),
            P(),
            P("dp", "tensor"),
            P("tensor"),
            P("tensor", "dp"),
            P(),
        ),
        check_vma=False,
    )
```

time: 617 us -> 547 us (0.89)
  Pallas kernels: 91 us -> 190 us
  matrix products: 119 us -> 39.8 us
  waiting for transfers between devices: 180 us -> 128 us
  other arithmetic: 95.1 us -> 50.3 us
  between operations: 2.41 us -> 15.5 us
    pallas_call x3 -> x13, Pallas kernels: 25.9 us -> 127 us  [row_step(): pl.pallas_call(kernel, out_shape=outs, grid=(steps,), in_specs=specs, out...]
    ppermute x38 -> x31, waiting for transfers between devices: 150 us -> 65.8 us  [swap_apart(): return lax.ppermute(values, 'dp', [(i, i ^ apart) for i in range(size)])]
    dot_general x11 -> x2, matrix products: 76.2 us -> 2.85 us  [the longest x1 2.38 us: shards(): lax.dot_general(silu_mine.astype(f32), after(grad_mod, one_sends), (((0,)...]
    reduce_sum x12 -> x2, other arithmetic: 31.7 us -> 1.25 us  [value_sums(): sums = jnp.sum(grads.astype(f32), axis=0).reshape(heads, 3, head_size)]
    ppermute x16 -> x12, waiting for transfers between devices: 29.4 us -> 47.8 us  [swap_y(): return lax.ppermute(values, 'tensor', [(i, i ^ 2) for i in range(4)])]
    all_gather x0 -> x3, waiting for transfers between devices: none -> 12.3 us  [shards(): gather = lambda shard: lax.all_gather(shard, 'dp', axis=0, tiled=True)]
    convert_element_type x10 -> x3, other arithmetic: 10.8 us -> 0.35 us  [the longest x1 0.26 us: split_bit(): return (keep, send.astype(bf16))]
    convert_element_type x14 -> x2, local copies, waits for them, and re-layouts: 11.3 us -> 2.03 us  [split_bit(): return (keep, send.astype(bf16))]
  transfers between devices with their start and end apart: 63 -> 54, of which waited for: 30 -> 23; matrix products, arithmetic and copies ran while one was open for 32% -> 20% of each run, Pallas kernels for 15% -> 35%
where the time goes in v3:
time: 547 us; the launch traced here: 541 us
  Pallas kernels  190 us (35%)
  waiting for transfers between devices  128 us (23%)
  starting transfers between devices  67.8 us (12%)
  other arithmetic  50.3 us (9%)
  local copies, waits for them, and re-layouts  49.2 us (9%)
  matrix products  39.8 us (7%)
  between operations  15.5 us (3%)
    pallas_call x13, Pallas kernels, row_step(): pl.pallas_call(kernel, out_shape=outs, grid=(steps,), in_specs=specs, out...  127 us
    ppermute x31, waiting for transfers between devices, swap_apart(): return lax.ppermute(values, 'dp', [(i, i ^ apart) for i in range(size)])  65.8 us
    ppermute x12, waiting for transfers between devices, swap_y(): return lax.ppermute(values, 'tensor', [(i, i ^ 2) for i in range(4)])  47.8 us
    ppermute x31, starting transfers between devices, swap_apart(): return lax.ppermute(values, 'dp', [(i, i ^ apart) for i in range(size)])  46.8 us
    pallas_call x2, Pallas kernels, attend_back(): pl.pallas_call(kernel, out_shape=jax.ShapeDtypeStruct((rows, heads * 3 *...  40.9 us
    dot_general x8, matrix products, weight_term(): lax.dot_general(left, right, (((0,), (0,)), ((), ())), preferred_element_...  36.7 us
    pallas_call x2, Pallas kernels, attend(): pl.pallas_call(kernel, out_shape=(jax.ShapeDtypeStruct((rows, heads * siz...  21.9 us
    ppermute x12, starting transfers between devices, swap_y(): return lax.ppermute(values, 'tensor', [(i, i ^ 2) for i in range(4)])  20 us
  transfers between devices with their start and end apart: 54, of which 23 were waited for; matrix products, arithmetic and copies ran while one was open for 20% of the time, Pallas kernels for 35%

profile of v3, /device:TPU:0, one launch (start us, length us, event | category | flops | bytes accessed | tf_op | source)
XLA Modules:
  0.0 541.0 jit_solution(15195858439757646850)
XLA Ops:
  34.3 4.7 collective-permute-done.6
  41.7 5.0 collective-permute-done.7
  57.9 9.6 %all-gather.4.cloned.1.call-done.refs_4_.refs_2_ = bf16[1152,896]{1,0:T(8,128)(2,1)} async-done(((bf16[144,896]{1,0:T(8,128)(2,1)}), bf16[1152,896]{1,0:T(8,128)(2,1)}) %all-gather.4.cloned.1.call-update) | async-done | bytes 2064400 | tf_op jit(solution)/shard_map/all_gather | solution.py:641
  67.6 8.0 %collective-permute-start.13 = (bf16[1152,896]{1,0:T(8,128)(2,1)}, bf16[1152,896]{1,0:T(8,128)(2,1)}, u32[]{:S(2)}, u32[]{:S(2)}) collective-permute-start(bf16[1152,896]{1,0:T(8,128)(2,1)} %all-gather.4.cloned.1.call-done.refs_4_.refs_2_), channel_id=1, source_target_pairs={{0,2},{1,3},{2,0},{3,1},{4,6},{5,7},{6,4},{7,5},{8,10},{9,11},{10,... | collective-permute-start | bytes 6193160 | tf_op jit(solution)/shard_map/ppermute | solution.py:25
  81.3 8.5 %norm_project.1 = (bf16[1024,1152]{1,0:T(8,128)(2,1)}, bf16[1024,864]{1,0:T(8,128)(2,1)}) custom-call(bf16[1024,1152]{1,0:T(8,128)(2,1)} %pad_maximum_fusion.1.refs_0_.refs_2_, f32[1,1152]{1,0:T(1,128)} %get-tuple-element.197.refs_1_.refs_4_, f32[1,1152]{1,0:T(1,128)} %get-tuple-element.196.refs_2_, f32[1,864]{1,0:T(1,128)} %reshape.193.refs_3_, ...), custom_call_target="tpu_custom_call" | custom-call | bytes 8565120 | tf_op jit(solution)/shard_map/norm_project/pallas_call | solution.py:170
  91.3 11.0 %attend.2 = (bf16[1024,288]{1,0:T(8,128)(2,1)S(1)}, f32[1024,4]{1,0:T(8,128)S(1)}) custom-call(bf16[1024,864]{1,0:T(8,128)(2,1)S(1)} %copy-done.6), custom_call_target="tpu_custom_call" | custom-call | flops 4831838208 | bytes 2359296 | tf_op jit(solution)/shard_map/attend/pallas_call | solution.py:508
  105.1 12.2 %collective-permute-done.13.refs_2_.refs_1_ = bf16[1152,896]{1,0:T(8,128)(2,1)} collective-permute-done((bf16[1152,896]{1,0:T(8,128)(2,1)}, bf16[1152,896]{1,0:T(8,128)(2,1)}, u32[]{:S(2)}, u32[]{:S(2)}) %collective-permute-start.13) | collective-permute-done | bytes 2064416 | tf_op jit(solution)/shard_map/ppermute | solution.py:25
  117.3 7.2 %project.1.x_ref = bf16[1024,864]{1,0:T(8,128)(2,1)} custom-call(bf16[1024,1152]{1,0:T(8,128)(2,1)} %get-tuple-element.126.refs_0_, f32[1,864]{1,0:T(1,128)} %reshape.194.refs_1_, bf16[1152,896]{1,0:T(8,128)(2,1)} %collective-permute-done.13.refs_2_.refs_1_), custom_call_target="tpu_custom_call" | custom-call | bytes 6196608 | tf_op jit(solution)/shard_map/project/pallas_call | solution.py:170
  126.0 11.0 %attend.3 = (bf16[1024,288]{1,0:T(8,128)(2,1)S(1)}, f32[1024,4]{1,0:T(8,128)S(1)}) custom-call(bf16[1024,864]{1,0:T(8,128)(2,1)S(1)} %copy-done.1), custom_call_target="tpu_custom_call" | custom-call | flops 4831838208 | bytes 2359296 | tf_op jit(solution)/shard_map/attend/pallas_call | solution.py:508
  140.8 7.5 %project_out.1.refs_0_.refs_4_ = bf16[1024,1152]{1,0:T(8,128)(2,1)} custom-call(bf16[1024,288]{1,0:T(8,128)(2,1)} %copy-done.2, bf16[1024,288]{1,0:T(8,128)(2,1)} %copy-done.4, bf16[1152,576]{1,0:T(8,128)(2,1)} %bitcast.221, bf16[1152,576]{1,0:T(8,128)(2,1)} %bitcast.222), custom_call_target="tpu_custom_call" | custom-call | bytes 6193152 | tf_op jit(solution)/shard_map/project_out/pallas_call | solution.py:170
  154.5 8.4 %middle_norm.1 = (f32[1024,1152]{1,0:T(8,128)}, bf16[1024,1152]{1,0:T(8,128)(2,1)}, bf16[1024,1152]{1,0:T(8,128)(2,1)}, f32[1,1152]{1,0:T(1,128)}) custom-call(bf16[1024,1152]{1,0:T(8,128)(2,1)} %project_out.1.refs_0_.refs_4_, bf16[1024,1152]{1,0:T(8,128)(2,1)} %collective-permute-done.15.refs_1_.refs_5_, ...), custom_call_target="tpu_custom_call" | custom-call | bytes 18902016 | tf_op jit(solution)/shard_map/middle_norm/pallas_call | solution.py:170
  162.8 10.1 %feed_forward.2 = (bf16[1024,1152]{1,0:T(8,128)(2,1)}, f32[1024,1152]{1,0:T(8,128)}) custom-call(bf16[1024,1152]{1,0:T(8,128)(2,1)} %get-tuple-element.91.refs_0_, f32[1,1152]{1,0:T(1,128)} %slice.330.refs_1_, bf16[1152,1152]{1,0:T(8,128)(2,1)} %all-gather.6.cloned.1.call-done.refs_2_.refs_3_), custom_call_target="tpu_custom_call" | custom-call | bytes 12096000 | tf_op jit(solution)/shard_map/feed_forward/pallas_call | solution.py:170
  173.0 7.3 %fusion.53 = f32[1152,1152]{1,0:T(8,128)} fusion(bf16[1024,1152]{1,0:T(8,128)(2,1)S(1)} %copy-done.10, bf16[1024,1152]{1,0:T(8,128)(2,1)} %get-tuple-element.90.refs_1_), kind=kOutput, calls=%fused_computation.206 | convolution fusion | flops 2717908992 | bytes 10027008 | tf_op jit(solution)/shard_map/dot_general | solution.py:424
  180.3 28.4 %collective-permute-done.16.refs_2_.refs_5_ = bf16[1152,1152]{1,0:T(8,128)(2,1)} collective-permute-done((bf16[1152,1152]{1,0:T(8,128)(2,1)}, bf16[1152,1152]{1,0:T(8,128)(2,1)}, u32[]{:S(2)}, u32[]{:S(2)}) %collective-permute-start.16) | collective-permute-done | bytes 2654240 | tf_op jit(solution)/shard_map/ppermute | solution.py:25
  208.7 10.0 %feed_forward.3 = (bf16[1024,1152]{1,0:T(8,128)(2,1)}, f32[1024,1152]{1,0:T(8,128)}) custom-call(bf16[1024,1152]{1,0:T(8,128)(2,1)} %get-tuple-element.91.refs_0_, f32[1,1152]{1,0:T(1,128)} %slice.333.refs_1_, bf16[1152,1152]{1,0:T(8,128)(2,1)} %collective-permute-done.16.refs_2_.refs_5_), custom_call_target="tpu_custom_call" | custom-call | bytes 12096000 | tf_op jit(solution)/shard_map/feed_forward/pallas_call | solution.py:170
  218.7 5.0 convolution_convert_fusion.1
  232.1 16.5 %feed_back.2 = (bf16[1024,1152]{1,0:T(8,128)(2,1)}, f32[1024,1152]{1,0:T(8,128)}, f32[1024,1152]{1,0:T(8,128)}, f32[1,1152]{1,0:T(1,128)}) custom-call(bf16[1024,1152]{1,0:T(8,128)(2,1)} %get-tuple-element.99.refs_0_, bf16[1024,1152]{1,0:T(8,128)(2,1)} %get-tuple-element.90.refs_1_, f32[1024,1152]{1,0:T(8,128)} %get-tuple-element.95.refs_2_, ...), custom_call_target="tpu_custom_call" | custom-call | bytes 29200896 | tf_op jit(solution)/shard_map/feed_back/pallas_call | solution.py:170
  255.7 17.6 %feed_back.3 = (bf16[1024,1152]{1,0:T(8,128)(2,1)}, bf16[1024,1152]{1,0:T(8,128)(2,1)}, bf16[1024,1152]{1,0:T(8,128)(2,1)}, f32[1,1152]{1,0:T(1,128)}) custom-call(bf16[1024,1152]{1,0:T(8,128)(2,1)} %get-tuple-element.99.refs_0_, bf16[1024,1152]{1,0:T(8,128)(2,1)} %get-tuple-element.93.refs_1_, f32[1024,1152]{1,0:T(8,128)} %get-tuple-element.100.refs_2_, ...), custom_call_target="tpu_custom_call" | custom-call | bytes 33919488 | tf_op jit(solution)/shard_map/feed_back/pallas_call | solution.py:170
  273.4 5.0 convolution_convert_fusion
  284.8 5.1 fusion.54
  299.1 15.3 %middle_back.1 = (f32[1024,1152]{1,0:T(8,128)}, bf16[1024,1152]{1,0:T(8,128)(2,1)}, bf16[1024,288]{1,0:T(8,128)(2,1)}, bf16[1024,288]{1,0:T(8,128)(2,1)}, f32[8,1152]{1,0:T(8,128)}) custom-call(bf16[1024,1152]{1,0:T(8,128)(2,1)} %get-tuple-element.109.refs_0_, bf16[1024,1152]{1,0:T(8,128)(2,1)} %collective-permute-done.21.refs_1_, ...), custom_call_target="tpu_custom_call" | custom-call | bytes 27477504 | tf_op jit(solution)/shard_map/middle_back/pallas_call | solution.py:170
  332.1 20.6 %attend_back.2.refs_0_ = bf16[1024,864]{1,0:T(8,128)(2,1)} custom-call(bf16[1024,864]{1,0:T(8,128)(2,1)} %project.1.x_ref, bf16[1024,288]{1,0:T(8,128)(2,1)} %get-tuple-element.116.g_ref, f32[4,1,1024]{2,1,0:T(1,128)} %reshape.201.lse_ref), custom_call_target="tpu_custom_call" | custom-call | flops 12079595520 | bytes 3538944 | tf_op jit(solution)/shard_map/attend_back/pallas_call | solution.py:589
  352.6 5.4 convolution_convert_fusion.2
  366.4 7.9 %project_back.2.refs_1_ = f32[1024,1152]{1,0:T(8,128)} custom-call(bf16[1024,864]{1,0:T(8,128)(2,1)} %attend_back.2.refs_0_, bf16[1152,896]{1,0:T(8,128)(2,1)} %collective-permute-done.13.refs_2_.refs_1_), custom_call_target="tpu_custom_call" | custom-call | bytes 8552448 | tf_op jit(solution)/shard_map/project_back/pallas_call | solution.py:170
  374.4 5.5 %collective-permute-done.30 = bf16[2,144,1152]{2,1,0:T(8,128)(2,1)} collective-permute-done((bf16[2,144,1152]{2,1,0:T(8,128)(2,1)}, bf16[2,144,1152]{2,1,0:T(8,128)(2,1)}, u32[]{:S(2)}, u32[]{:S(2)}) %collective-permute-start.30) | collective-permute-done | bytes 663584 | tf_op jit(solution)/shard_map/ppermute | solution.py:30
  389.2 6.0 %collective-permute-start.32 = (bf16[144,1152]{1,0:T(8,128)(2,1)}, bf16[144,1152]{1,0:T(8,128)(2,1)}, u32[]{:S(2)}, u32[]{:S(2)}) collective-permute-start(bf16[144,1152]{1,0:T(8,128)(2,1)} %get-tuple-element.156), channel_id=1, source_target_pairs={{0,8},{4,12},{8,0},{12,4},{16,24},{20,28},{24,16},{28,20},{1,9},{5... | collective-permute-start | bytes 995336 | tf_op jit(solution)/shard_map/ppermute | solution.py:30
  397.9 20.4 %attend_back.3.refs_0_ = bf16[1024,864]{1,0:T(8,128)(2,1)} custom-call(bf16[1024,864]{1,0:T(8,128)(2,1)} %get-tuple-element.78.x_ref, bf16[1024,288]{1,0:T(8,128)(2,1)} %get-tuple-element.121.g_ref, f32[4,1,1024]{2,1,0:T(1,128)} %reshape.203.lse_ref), custom_call_target="tpu_custom_call" | custom-call | flops 12079595520 | bytes 3538944 | tf_op jit(solution)/shard_map/attend_back/pallas_call | solution.py:589
  418.3 9.6 %project_back.3.refs_0_ = bf16[1024,1152]{1,0:T(8,128)(2,1)} custom-call(bf16[1024,864]{1,0:T(8,128)(2,1)} %attend_back.3.refs_0_, f32[1024,1152]{1,0:T(8,128)} %project_back.2.refs_1_, bf16[1152,896]{1,0:T(8,128)(2,1)} %all-gather.4.cloned.1.call-done.refs_4_.refs_2_), custom_call_target="tpu_custom_call" | custom-call | bytes 10911744 | tf_op jit(solution)/shard_map/project_back/pallas_call | solution.py:170
  442.9 4.8 first_back.1
  454.8 13.5 %collective-permute-done.37 = bf16[4,144,1152]{2,1,0:T(8,128)(2,1)} collective-permute-done((bf16[4,144,1152]{2,1,0:T(8,128)(2,1)}, bf16[4,144,1152]{2,1,0:T(8,128)(2,1)}, u32[]{:S(2)}, u32[]{:S(2)}) %collective-permute-start.37) | collective-permute-done | bytes 1327136 | tf_op jit(solution)/shard_map/ppermute | solution.py:30
  510.5 9.7 %collective-permute-done.46 = f32[2,2,2,144]{3,2,1,0:T(2,128)S(1)} collective-permute-done((f32[2,2,2,144]{3,2,1,0:T(2,128)S(1)}, f32[2,2,2,144]{3,2,1,0:T(2,128)S(1)}, u32[]{:S(2)}, u32[]{:S(2)}) %collective-permute-start.46) | collective-permute-done | bytes 4640 | tf_op jit(solution)/shard_map/ppermute | solution.py:30
  525.6 5.0 collective-permute-done.47
  (401 shorter events, 203.9 us)
Async XLA Ops:
  7.2 60.4 %all-gather.4.cloned.1.call-start = ((), (), s32[]{:S(2)}) async-start(), calls=%async_computation | async-start | bytes 2322432 | tf_op jit(solution)/shard_map/all_gather | solution.py:641
  9.1 139.4 %all-gather.6.cloned.1.call-start = ((), (), s32[]{:S(2)}) async-start(), calls=%async_computation.1 | async-start | bytes 2985984 | tf_op jit(solution)/shard_map/all_gather | solution.py:641
  15.3 60.2 %collective-permute-start = (bf16[1024,1152]{1,0:T(8,128)(2,1)}, bf16[1024,1152]{1,0:T(8,128)(2,1)}, u32[]{:S(2)}, u32[]{:S(2)}) collective-permute-start(bf16[1024,1152]{1,0:T(8,128)(2,1)} %pad_maximum_fusion), channel_id=1, source_target_pairs={{0,1},{1,0},{2,3},{3,2},{4,5},{5,4},{6,7},{7,6},{8,9},{9,8},{10,11... | collective-permute-start | bytes 7077896 | tf_op jit(solution)/shard_map/ppermute | solution.py:21
  15.4 33.6 %collective-permute-start.9 = (bf16[144,1440]{1,0:T(8,128)(2,1)S(1)}, bf16[144,1440]{1,0:T(8,128)(2,1)S(1)}, u32[]{:S(2)}, u32[]{:S(2)}) collective-permute-start(bf16[144,1440]{1,0:T(8,128)(2,1)S(1)} %pad_maximum_fusion.12), channel_id=1, source_target_pairs={{0,2},{1,3},{2,0},{3,1},{4,6},{5,7},{6,4},{7,5},{8,10},{9,11},{10,... | collective-permute-start | bytes 1244168 | tf_op jit(solution)/shard_map/ppermute | solution.py:25
  17.0 215.1 %all-gather.8.cloned.1.call-start = ((), (), s32[]{:S(2)}) async-start(), calls=%async_computation.2 | async-start | bytes 5971968 | tf_op jit(solution)/shard_map/all_gather | solution.py:641
  53.1 50.1 %collective-permute-start.10 = (bf16[144,576]{1,0:T(8,128)(2,1)S(1)}, bf16[144,576]{1,0:T(8,128)(2,1)S(1)}, u32[]{:S(2)}, u32[]{:S(2)}) collective-permute-start(bf16[144,576]{1,0:T(8,128)(2,1)S(1)} %pad_maximum_fusion.14), channel_id=1, source_target_pairs={{0,8},{4,12},{8,0},{12,4},{16,24},{20,28},{24,16},{28,20},{1,9},{5... | collective-permute-start | bytes 497672 | tf_op jit(solution)/shard_map/ppermute | solution.py:30
  54.7 48.4 %collective-permute-start.11 = (bf16[144,576]{1,0:T(8,128)(2,1)S(1)}, bf16[144,576]{1,0:T(8,128)(2,1)}, u32[]{:S(2)}, u32[]{:S(2)}) collective-permute-start(bf16[144,576]{1,0:T(8,128)(2,1)S(1)} %pad_maximum_fusion.14), channel_id=1, source_target_pairs={{0,16},{4,20},{8,24},{12,28},{16,0},{20,4},{24,8},{28,12},{1,17},{... | collective-permute-start | bytes 497672 | tf_op jit(solution)/shard_map/ppermute | solution.py:30
  57.9 45.2 %collective-permute-start.12 = (bf16[144,576]{1,0:T(8,128)(2,1)S(1)}, bf16[144,576]{1,0:T(8,128)(2,1)}, u32[]{:S(2)}, u32[]{:S(2)}) collective-permute-start(bf16[144,576]{1,0:T(8,128)(2,1)S(1)} %pad_maximum_fusion.14), channel_id=1, source_target_pairs={{0,24},{4,28},{8,16},{12,20},{16,8},{20,12},{24,0},{28,4},{1,25},{... | collective-permute-start | bytes 497672 | tf_op jit(solution)/shard_map/ppermute | solution.py:30
  67.6 49.7 %collective-permute-start.13 = (bf16[1152,896]{1,0:T(8,128)(2,1)}, bf16[1152,896]{1,0:T(8,128)(2,1)}, u32[]{:S(2)}, u32[]{:S(2)}) collective-permute-start(bf16[1152,896]{1,0:T(8,128)(2,1)} %all-gather.4.cloned.1.call-done.refs_4_.refs_2_), channel_id=1, source_target_pairs={{0,2},{1,3},{2,0},{3,1},{4,6},{5,7},{6,4},{7,5},{8,10},{9,11},{10,... | collective-permute-start | bytes 6193160 | tf_op jit(solution)/shard_map/ppermute | solution.py:25
  104.3 32.7 %collective-permute-start.14 = (bf16[4,144,576]{2,1,0:T(8,128)(2,1)S(1)}, bf16[4,144,576]{2,1,0:T(8,128)(2,1)}, u32[]{:S(2)}, u32[]{:S(2)}) collective-permute-start(bf16[4,144,576]{2,1,0:T(8,128)(2,1)S(1)} %get-tuple-element.171), channel_id=1, source_target_pairs={{0,4},{4,0},{8,12},{12,8},{16,20},{20,16},{24,28},{28,24},{1,5},{5... | collective-permute-start | bytes 1990664 | tf_op jit(solution)/shard_map/ppermute | solution.py:30
  148.5 60.3 %collective-permute-start.16 = (bf16[1152,1152]{1,0:T(8,128)(2,1)}, bf16[1152,1152]{1,0:T(8,128)(2,1)}, u32[]{:S(2)}, u32[]{:S(2)}) collective-permute-start(bf16[1152,1152]{1,0:T(8,128)(2,1)} %all-gather.6.cloned.1.call-done.refs_2_.refs_3_), channel_id=1, source_target_pairs={{0,2},{1,3},{2,0},{3,1},{4,6},{5,7},{6,4},{7,5},{8,10},{9,11},{10,... | collective-permute-start | bytes 7962632 | tf_op jit(solution)/shard_map/ppermute | solution.py:25
  225.1 23.5 %collective-permute-start.17 = (bf16[2,144,1152]{2,1,0:T(8,128)(2,1)}, bf16[2,144,1152]{2,1,0:T(8,128)(2,1)}, u32[]{:S(2)}, u32[]{:S(2)}) collective-permute-start(bf16[2,144,1152]{2,1,0:T(8,128)(2,1)} %get-tuple-element.164), channel_id=1, source_target_pairs={{0,4},{4,0},{8,12},{12,8},{16,20},{20,16},{24,28},{28,24},{1,5},{5... | collective-permute-start | bytes 1990664 | tf_op jit(solution)/shard_map/ppermute | solution.py:30
  225.8 22.9 %collective-permute-start.18 = (bf16[2,144,1152]{2,1,0:T(8,128)(2,1)}, bf16[2,144,1152]{2,1,0:T(8,128)(2,1)}, u32[]{:S(2)}, u32[]{:S(2)}) collective-permute-start(bf16[2,144,1152]{2,1,0:T(8,128)(2,1)} %get-tuple-element.165), channel_id=1, source_target_pairs={{0,2},{1,3},{2,0},{3,1},{4,6},{5,7},{6,4},{7,5},{8,10},{9,11},{10,... | collective-permute-start | bytes 1990664 | tf_op jit(solution)/shard_map/ppermute | solution.py:25
  251.3 38.9 %collective-permute-start.20 = (bf16[4,144,1152]{2,1,0:T(8,128)(2,1)}, bf16[4,144,1152]{2,1,0:T(8,128)(2,1)}, u32[]{:S(2)}, u32[]{:S(2)}) collective-permute-start(bf16[4,144,1152]{2,1,0:T(8,128)(2,1)} %pad_maximum_fusion.5), channel_id=1, source_target_pairs={{0,2},{1,3},{2,0},{3,1},{4,6},{5,7},{6,4},{7,5},{8,10},{9,11},{10,... | collective-permute-start | bytes 3981320 | tf_op jit(solution)/shard_map/ppermute | solution.py:25
  255.2 37.1 %collective-permute-start.19 = (bf16[4,144,1152]{2,1,0:T(8,128)(2,1)}, bf16[4,144,1152]{2,1,0:T(8,128)(2,1)}, u32[]{:S(2)}, u32[]{:S(2)}) collective-permute-start(bf16[4,144,1152]{2,1,0:T(8,128)(2,1)} %pad_maximum_fusion.4), channel_id=1, source_target_pairs={{0,4},{4,0},{8,12},{12,8},{16,20},{20,16},{24,28},{28,24},{1,5},{5... | collective-permute-start | bytes 3981320 | tf_op jit(solution)/shard_map/ppermute | solution.py:30
  273.3 24.5 %collective-permute-start.21 = (bf16[1024,1152]{1,0:T(8,128)(2,1)}, bf16[1024,1152]{1,0:T(8,128)(2,1)}, u32[]{:S(2)}, u32[]{:S(2)}) collective-permute-start(bf16[1024,1152]{1,0:T(8,128)(2,1)} %get-tuple-element.109.refs_0_), channel_id=1, source_target_pairs={{0,1},{1,0},{2,3},{3,2},{4,5},{5,4},{6,7},{7,6},{8,9},{9,8},{10,11... | collective-permute-start | bytes 7077896 | tf_op jit(solution)/shard_map/ppermute | solution.py:21
  279.6 41.2 %collective-permute-start.22 = (bf16[2,144,1152]{2,1,0:T(8,128)(2,1)}, bf16[2,144,1152]{2,1,0:T(8,128)(2,1)}, u32[]{:S(2)}, u32[]{:S(2)}) collective-permute-start(bf16[2,144,1152]{2,1,0:T(8,128)(2,1)} %get-tuple-element.158), channel_id=1, source_target_pairs={{0,4},{4,0},{8,12},{12,8},{16,20},{20,16},{24,28},{28,24},{1,5},{5... | collective-permute-start | bytes 1990664 | tf_op jit(solution)/shard_map/ppermute | solution.py:30
  281.1 39.7 %collective-permute-start.23 = (bf16[2,144,1152]{2,1,0:T(8,128)(2,1)S(1)}, bf16[2,144,1152]{2,1,0:T(8,128)(2,1)}, u32[]{:S(2)}, u32[]{:S(2)}) collective-permute-start(bf16[2,144,1152]{2,1,0:T(8,128)(2,1)S(1)} %get-tuple-element.159), channel_id=1, source_target_pairs={{0,2},{1,3},{2,0},{3,1},{4,6},{5,7},{6,4},{7,5},{8,10},{9,11},{10,... | collective-permute-start | bytes 1990664 | tf_op jit(solution)/shard_map/ppermute | solution.py:25
  294.7 26.1 %collective-permute-start.24 = (bf16[144,1152]{1,0:T(8,128)(2,1)S(1)}, bf16[144,1152]{1,0:T(8,128)(2,1)S(1)}, u32[]{:S(2)}, u32[]{:S(2)}) collective-permute-start(bf16[144,1152]{1,0:T(8,128)(2,1)S(1)} %get-tuple-element.162), channel_id=1, source_target_pairs={{0,8},{4,12},{8,0},{12,4},{16,24},{20,28},{24,16},{28,20},{1,9},{5... | collective-permute-start | bytes 995336 | tf_op jit(solution)/shard_map/ppermute | solution.py:30
  295.1 25.8 %collective-permute-start.25 = (bf16[144,1152]{1,0:T(8,128)(2,1)S(1)}, bf16[144,1152]{1,0:T(8,128)(2,1)S(1)}, u32[]{:S(2)}, u32[]{:S(2)}) collective-permute-start(bf16[144,1152]{1,0:T(8,128)(2,1)S(1)} %get-tuple-element.161), channel_id=1, source_target_pairs={{0,16},{4,20},{8,24},{12,28},{16,0},{20,4},{24,8},{28,12},{1,17},{... | collective-permute-start | bytes 995336 | tf_op jit(solution)/shard_map/ppermute | solution.py:30
  297.8 23.1 %collective-permute-start.26 = (bf16[144,1152]{1,0:T(8,128)(2,1)S(1)}, bf16[144,1152]{1,0:T(8,128)(2,1)S(1)}, u32[]{:S(2)}, u32[]{:S(2)}) collective-permute-start(bf16[144,1152]{1,0:T(8,128)(2,1)S(1)} %get-tuple-element.160), channel_id=1, source_target_pairs={{0,24},{4,28},{8,16},{12,20},{16,8},{20,12},{24,0},{28,4},{1,25},{... | collective-permute-start | bytes 995336 | tf_op jit(solution)/shard_map/ppermute | solution.py:30
  328.9 54.8 %collective-permute-start.28 = (bf16[4,144,1152]{2,1,0:T(8,128)(2,1)}, bf16[4,144,1152]{2,1,0:T(8,128)(2,1)}, u32[]{:S(2)}, u32[]{:S(2)}) collective-permute-start(bf16[4,144,1152]{2,1,0:T(8,128)(2,1)} %pad_maximum_fusion.7), channel_id=1, source_target_pairs={{0,2},{1,3},{2,0},{3,1},{4,6},{5,7},{6,4},{7,5},{8,10},{9,11},{10,... | collective-permute-start | bytes 3981320 | tf_op jit(solution)/shard_map/ppermute | solution.py:25
  331.6 52.1 %collective-permute-start.27 = (bf16[4,144,1152]{2,1,0:T(8,128)(2,1)}, bf16[4,144,1152]{2,1,0:T(8,128)(2,1)}, u32[]{:S(2)}, u32[]{:S(2)}) collective-permute-start(bf16[4,144,1152]{2,1,0:T(8,128)(2,1)} %pad_maximum_fusion.6), channel_id=1, source_target_pairs={{0,4},{4,0},{8,12},{12,8},{16,20},{20,16},{24,28},{28,24},{1,5},{5... | collective-permute-start | bytes 3981320 | tf_op jit(solution)/shard_map/ppermute | solution.py:30
  365.4 52.9 %collective-permute-start.31 = (bf16[2,144,1152]{2,1,0:T(8,128)(2,1)}, bf16[2,144,1152]{2,1,0:T(8,128)(2,1)S(1)}, u32[]{:S(2)}, u32[]{:S(2)}) collective-permute-start(bf16[2,144,1152]{2,1,0:T(8,128)(2,1)} %get-tuple-element.168), channel_id=1, source_target_pairs={{0,2},{1,3},{2,0},{3,1},{4,6},{5,7},{6,4},{7,5},{8,10},{9,11},{10,... | collective-permute-start | bytes 1990664 | tf_op jit(solution)/shard_map/ppermute | solution.py:25
  382.3 72.5 %collective-permute-start.38 = (bf16[4,144,1152]{2,1,0:T(8,128)(2,1)}, bf16[4,144,1152]{2,1,0:T(8,128)(2,1)}, u32[]{:S(2)}, u32[]{:S(2)}) collective-permute-start(bf16[4,144,1152]{2,1,0:T(8,128)(2,1)} %pad_maximum_fusion.9), channel_id=1, source_target_pairs={{0,2},{1,3},{2,0},{3,1},{4,6},{5,7},{6,4},{7,5},{8,10},{9,11},{10,... | collective-permute-start | bytes 3981320 | tf_op jit(solution)/shard_map/ppermute | solution.py:25
  389.2 41.1 %collective-permute-start.32 = (bf16[144,1152]{1,0:T(8,128)(2,1)}, bf16[144,1152]{1,0:T(8,128)(2,1)}, u32[]{:S(2)}, u32[]{:S(2)}) collective-permute-start(bf16[144,1152]{1,0:T(8,128)(2,1)} %get-tuple-element.156), channel_id=1, source_target_pairs={{0,8},{4,12},{8,0},{12,4},{16,24},{20,28},{24,16},{28,20},{1,9},{5... | collective-permute-start | bytes 995336 | tf_op jit(solution)/shard_map/ppermute | solution.py:30
  395.2 35.6 %collective-permute-start.33 = (bf16[144,1152]{1,0:T(8,128)(2,1)}, bf16[144,1152]{1,0:T(8,128)(2,1)}, u32[]{:S(2)}, u32[]{:S(2)}) collective-permute-start(bf16[144,1152]{1,0:T(8,128)(2,1)} %get-tuple-element.155), channel_id=1, source_target_pairs={{0,16},{4,20},{8,24},{12,28},{16,0},{20,4},{24,8},{28,12},{1,17},{... | collective-permute-start | bytes 995336 | tf_op jit(solution)/shard_map/ppermute | solution.py:30
  396.4 34.4 %collective-permute-start.34 = (bf16[144,1152]{1,0:T(8,128)(2,1)}, bf16[144,1152]{1,0:T(8,128)(2,1)}, u32[]{:S(2)}, u32[]{:S(2)}) collective-permute-start(bf16[144,1152]{1,0:T(8,128)(2,1)} %get-tuple-element.154), channel_id=1, source_target_pairs={{0,24},{4,28},{8,16},{12,20},{16,8},{20,12},{24,0},{28,4},{1,25},{... | collective-permute-start | bytes 995336 | tf_op jit(solution)/shard_map/ppermute | solution.py:30
  436.9 31.4 %collective-permute-start.37 = (bf16[4,144,1152]{2,1,0:T(8,128)(2,1)}, bf16[4,144,1152]{2,1,0:T(8,128)(2,1)}, u32[]{:S(2)}, u32[]{:S(2)}) collective-permute-start(bf16[4,144,1152]{2,1,0:T(8,128)(2,1)} %pad_maximum_fusion.8), channel_id=1, source_target_pairs={{0,4},{4,0},{8,12},{12,8},{16,20},{20,16},{24,28},{28,24},{1,5},{5... | collective-permute-start | bytes 3981320 | tf_op jit(solution)/shard_map/ppermute | solution.py:30
  497.8 33.6 %collective-permute-start.48 = (bf16[144,1152]{1,0:T(8,128)(2,1)S(1)}, bf16[144,1152]{1,0:T(8,128)(2,1)S(1)}, u32[]{:S(2)}, u32[]{:S(2)}) collective-permute-start(bf16[144,1152]{1,0:T(8,128)(2,1)S(1)} %get-tuple-element.153), channel_id=1, source_target_pairs={{0,8},{4,12},{8,0},{12,4},{16,24},{20,28},{24,16},{28,20},{1,9},{5... | collective-permute-start | bytes 995336 | tf_op jit(solution)/shard_map/ppermute | solution.py:30
  497.8 33.5 %collective-permute-start.49 = (bf16[144,1152]{1,0:T(8,128)(2,1)S(1)}, bf16[144,1152]{1,0:T(8,128)(2,1)S(1)}, u32[]{:S(2)}, u32[]{:S(2)}) collective-permute-start(bf16[144,1152]{1,0:T(8,128)(2,1)S(1)} %get-tuple-element.152), channel_id=1, source_target_pairs={{0,16},{4,20},{8,24},{12,28},{16,0},{20,4},{24,8},{28,12},{1,17},{... | collective-permute-start | bytes 995336 | tf_op jit(solution)/shard_map/ppermute | solution.py:30
  500.7 30.7 %collective-permute-start.50 = (bf16[144,1152]{1,0:T(8,128)(2,1)S(1)}, bf16[144,1152]{1,0:T(8,128)(2,1)S(1)}, u32[]{:S(2)}, u32[]{:S(2)}) collective-permute-start(bf16[144,1152]{1,0:T(8,128)(2,1)S(1)} %get-tuple-element.151), channel_id=1, source_target_pairs={{0,24},{4,28},{8,16},{12,20},{16,8},{20,12},{24,0},{28,4},{1,25},{... | collective-permute-start | bytes 995336 | tf_op jit(solution)/shard_map/ppermute | solution.py:30
  (80 other events, 609.0 us)
Sparse Core Ops, SparseCore 0:
  10.8 56.7 all-gather.3
  69.7 70.9 all-gather.5
  143.5 88.5 all-gather.7

commit v4 on v3

--- a/solution.py
+++ b/solution.py
@@ -456,6 +456,41 @@
     return lax.dynamic_index_in_dim(total, here, 0, False), sends
 
 
+def sum_and_split(keep, by_x, by_y):
+    half, rows, n = keep.shape
+    if half > 4:
+        total = add_all(keep.astype(f32), (by_x, by_y))
+        for bit in range(dp_bits() - 1, 1, -1):
+            blocks = total.reshape((2, total.shape[0] // 2) + total.shape[1:])
+            keep, send = split_bit(blocks, 0, bit)
+            total = keep + swap_dp(send, bit).astype(f32)
+        keep, send = split_bit(total, 0, 1)
+        return keep, [send]
+
+    def kernel(me_ref, keep_ref, x_ref, y_ref, *out_refs):
+        total = keep_ref[0].astype(f32) + x_ref[0].astype(f32) + y_ref[0].astype(f32)
+        for r, out_ref in enumerate(out_refs):
+
+            @pl.when(pl.program_id(0) == r)
+            def _():
+                out_ref[...] = total.astype(out_ref.dtype)
+
+    spec = pl.BlockSpec((1, rows, n), lambda r, me_ref: ((me_ref[0] >> 1) ^ r, 0, 0))
+    mine, *sends = pl.pallas_call(
+        kernel,
+        out_shape=[jax.ShapeDtypeStruct((rows, n), bf16 if r else f32) for r in range(half)],
+        grid_spec=pltpu.PrefetchScalarGridSpec(
+            num_scalar_prefetch=1,
+            grid=(half,),
+            in_specs=[spec] * 3,
+            out_specs=[pl.BlockSpec((rows, n), lambda r, me_ref: (0, 0))] * half,
+        ),
+        cost_estimate=pl.CostEstimate(flops=0, transcendentals=0, bytes_accessed=8 * keep.size),
+        name="sum_and_split",
+    )(lax.axis_index("dp").astype(jnp.int32).reshape(1), keep, by_x, by_y)
+    return mine, sends
+
+
 def scatter_z(sends):
     return [swap_apart(send, 2 * (r + 1)) for r, send in enumerate(sends)]
 
@@ -466,7 +501,7 @@
     return keep
 
 
-def attend(qkv, block=512, unroll=2):
+def attend(qkv, block=512, unroll=4):
     rows, cols = qkv.shape
     size = HEAD_DIM
     heads = cols // (3 * size)
@@ -481,7 +516,8 @@
                 b = h * 3 * size
                 q_s[h] = x_ref[:, b : b + size]
                 k_s[h] = x_ref[:, b + size : b + 2 * size]
-                v_s[h] = x_ref[:, b + 2 * size : b + 3 * size]
+                v_s[h, :, :size] = x_ref[:, b + 2 * size : b + 3 * size]
+                v_s[h, :, size:] = jnp.ones((rows, 8), bf16)
 
         def one(h):
             q = q_s[h, pl.ds(pl.multiple_of(i * block, block), block), :]
@@ -490,9 +526,9 @@
             )
             top = jnp.max(scores, axis=-1, keepdims=True)
             probs = jnp.exp2((scores - top) * factor)
-            total = jnp.sum(probs, axis=-1, keepdims=True)
             out = jnp.dot(probs.astype(bf16), v_s[h], preferred_element_type=f32)
-            o_s[h] = (out / total).astype(bf16)
+            total = out[:, size : size + 1]
+            o_s[h] = (out[:, :size] / total).astype(bf16)
             l_s[h] = top * factor + jnp.log2(total)
 
         def body(g, _):
@@ -517,8 +553,12 @@
             pl.BlockSpec((block, heads * size), lambda i: (i, 0)),
             pl.BlockSpec((block, heads), lambda i: (i, 0)),
         ),
-        scratch_shapes=[pltpu.VMEM((heads, rows, size), bf16)] * 3
-        + [pltpu.VMEM((heads, block, size), bf16), pltpu.VMEM((heads, block, 1), f32)],
+        scratch_shapes=[pltpu.VMEM((heads, rows, size), bf16)] * 2
+        + [
+            pltpu.VMEM((heads, rows, size + 8), bf16),
+            pltpu.VMEM((heads, block, size), bf16),
+            pltpu.VMEM((heads, block, 1), f32),
+        ],
         compiler_params=pltpu.CompilerParams(vmem_limit_bytes=48 << 20),
         cost_estimate=pl.CostEstimate(
             flops=16 * heads * rows * rows * size,
@@ -529,7 +569,7 @@
     )(qkv)
 
 
-def attend_back(qkv, grad_mix, lse, first, heads, block=512, unroll=2):
+def attend_back(qkv, grad_mix, lse, first, heads, block=1024, unroll=2):
     rows, cols = qkv.shape
     size = HEAD_DIM
     all_heads = cols // (3 * size)
@@ -720,7 +760,7 @@
     by_x, by_y = swap_dp(sends[0], 0), swap_y(sends[1])
     fc1_term_n = weight_term(mlp_in, pre_n, f32)
     fc2_got = after(fc2_got, fc1_term_n)
-    fc2_keep, z_sends = scatter_z_sends(add_all(fc2_keep, fc2_got))
+    fc2_keep, z_sends = sum_and_split(fc2_keep, *fc2_got)
     grad_middle, grad_attn, gmix_n, gmix_f, mid_sums = middle_back(
         after(grad_in_mine, fc1_term_n, fc1_far_keep, sends, z_sends), grad_in_theirs, middle, cot_all,
         out_mine, out_theirs, proj_row, gate_attn, scale_mlp, proj_near, proj_far,
@@ -741,7 +781,7 @@
     by_x, by_y = swap_dp(sends[0], 0), swap_y(sends[1])
     part_f = project_back(after(grad_f, sends), qkv_far, None, f32)
     fc1_got = after(fc1_got, part_f)
-    fc1_keep, z_sends = scatter_z_sends(add_all(fc1_keep, fc1_got))
+    fc1_keep, z_sends = sum_and_split(fc1_keep, *fc1_got)
     fc1_got = scatter_z(z_sends)
     grad_n = attend_back(
         qkv_n, after(gmix_n, part_f, one_far_keep, z_sends), rows_of(lse_n), 0, heads
@@ -771,10 +811,10 @@
     grad_mod = mod_sums[None]
     for bit in list(range(1, dp_bits())) + [0]:
         size = grad_mod.size
-        if bit == 1:
+        if bit == 2:
             grad_mod = after(grad_mod, one_got)
         if bit == 0:
-            one_keep, one_sends = scatter_z_sends(add_all(one_keep, after(one_got, grad_mod)))
+            one_keep, one_sends = sum_and_split(one_keep, *one_got)
             grad_mod = after(grad_mod, one_sends)
         got = swap_dp(jnp.concatenate([grad_mod.reshape(size), sums]), bit)
         theirs = got[:size].reshape(grad_mod.shape)

time: 547 us -> 530 us (0.969)
  waiting for transfers between devices: 128 us -> 102 us
  local copies, waits for them, and re-layouts: 49.2 us -> 61.8 us
  Pallas kernels: 190 us -> 199 us
  starting transfers between devices: 67.8 us -> 59.3 us
    ppermute x31, waiting for transfers between devices: 65.8 us -> 50.2 us  [swap_apart(): return lax.ppermute(values, 'dp', [(i, i ^ apart) for i in range(size)])]
    pallas_call x0 -> x3, Pallas kernels: none -> 13.9 us  [sum_and_split(): pl.pallas_call(kernel, out_shape=[jax.ShapeDtypeStruct((rows, n), bf16 if...]
    all_gather x3, waiting for transfers between devices: 12.3 us -> 1.72 us  [shards(): gather = lambda shard: lax.all_gather(shard, 'dp', axis=0, tiled=True)]
    add x5 -> x2, other arithmetic: 11.6 us -> 2.34 us  [add_all(): keep = keep + part.astype(f32)]
    ppermute x12, starting transfers between devices: 20 us -> 10.9 us  [swap_y(): return lax.ppermute(values, 'tensor', [(i, i ^ 2) for i in range(4)])]
    unnamed x123 -> x97, local copies, waits for them, and re-layouts: 13.3 us -> 14.8 us
  transfers between devices with their start and end apart: 54 -> 54, of which waited for: 23 -> 18; matrix products, arithmetic and copies ran while one was open for 20% -> 24% of each run, Pallas kernels for 35% -> 38%
where the time goes in v4:
time: 530 us; the launch traced here: 523 us
  Pallas kernels  199 us (38%)
  waiting for transfers between devices  102 us (19%)
  local copies, waits for them, and re-layouts  61.8 us (12%)
  starting transfers between devices  59.3 us (11%)
  other arithmetic  46.9 us (9%)
  matrix products  38.8 us (7%)
  between operations  15.3 us (3%)
    pallas_call x13, Pallas kernels, row_step(): pl.pallas_call(kernel, out_shape=outs, grid=(steps,), in_specs=specs, out...  127 us
    ppermute x31, waiting for transfers between devices, swap_apart(): return lax.ppermute(values, 'dp', [(i, i ^ apart) for i in range(size)])  50.2 us
    ppermute x12, waiting for transfers between devices, swap_y(): return lax.ppermute(values, 'tensor', [(i, i ^ 2) for i in range(4)])  49.4 us
    ppermute x31, starting transfers between devices, swap_apart(): return lax.ppermute(values, 'dp', [(i, i ^ apart) for i in range(size)])  47.4 us
    pallas_call x2, Pallas kernels, attend_back(): pl.pallas_call(kernel, out_shape=jax.ShapeDtypeStruct((rows, heads * 3 *...  39.5 us
    dot_general x8, matrix products, weight_term(): lax.dot_general(left, right, (((0,), (0,)), ((), ())), preferred_element_...  35.7 us
    pallas_call x2, Pallas kernels, attend(): pl.pallas_call(kernel, out_shape=(jax.ShapeDtypeStruct((rows, heads * siz...  19.1 us
    unnamed x97, local copies, waits for them, and re-layouts  14.8 us
  transfers between devices with their start and end apart: 54, of which 18 were waited for; matrix products, arithmetic and copies ran while one was open for 24% of the time, Pallas kernels for 38%

profile of v4, /device:TPU:0, one launch (start us, length us, event | category | flops | bytes accessed | tf_op | source)
XLA Modules:
  0.0 523.2 jit_solution(11997282002209835902)
XLA Ops:
  45.3 5.7 %collective-permute-done.7 = f32[2,6912]{1,0:T(2,128)S(1)} collective-permute-done((f32[2,6912]{1,0:T(2,128)S(1)}, f32[2,6912]{1,0:T(2,128)S(1)}, u32[]{:S(2)}, u32[]{:S(2)}) %collective-permute-start.7) | collective-permute-done | bytes 55328 | tf_op jit(solution)/shard_map/ppermute | solution.py:30
  71.5 8.5 %norm_project.1 = (bf16[1024,1152]{1,0:T(8,128)(2,1)}, bf16[1024,864]{1,0:T(8,128)(2,1)}) custom-call(bf16[1024,1152]{1,0:T(8,128)(2,1)} %pad_maximum_fusion.1.refs_0_.refs_2_, f32[1,1152]{1,0:T(1,128)} %get-tuple-element.208.refs_1_.refs_4_, f32[1,1152]{1,0:T(1,128)} %get-tuple-element.207.refs_2_, f32[1,864]{1,0:T(1,128)} %reshape.186.refs_3_, ...), custom_call_target="tpu_custom_call" | custom-call | bytes 8565120 | tf_op jit(solution)/shard_map/norm_project/pallas_call | solution.py:170
  81.6 9.3 %attend.2 = (bf16[1024,288]{1,0:T(8,128)(2,1)S(1)}, f32[1024,4]{1,0:T(8,128)S(1)}) custom-call(bf16[1024,864]{1,0:T(8,128)(2,1)S(1)} %copy-done.6), custom_call_target="tpu_custom_call" | custom-call | flops 4831838208 | bytes 2359296 | tf_op jit(solution)/shard_map/attend/pallas_call | solution.py:544
  94.9 15.5 %collective-permute-done.13.refs_2_.refs_1_ = bf16[1152,896]{1,0:T(8,128)(2,1)} collective-permute-done((bf16[1152,896]{1,0:T(8,128)(2,1)}, bf16[1152,896]{1,0:T(8,128)(2,1)}, u32[]{:S(2)}, u32[]{:S(2)}) %collective-permute-start.13) | collective-permute-done | bytes 2064416 | tf_op jit(solution)/shard_map/ppermute | solution.py:25
  110.3 7.3 %project.1.x_ref = bf16[1024,864]{1,0:T(8,128)(2,1)} custom-call(bf16[1024,1152]{1,0:T(8,128)(2,1)} %get-tuple-element.142.refs_0_, f32[1,864]{1,0:T(1,128)} %reshape.187.refs_1_, bf16[1152,896]{1,0:T(8,128)(2,1)} %collective-permute-done.13.refs_2_.refs_1_), custom_call_target="tpu_custom_call" | custom-call | bytes 6196608 | tf_op jit(solution)/shard_map/project/pallas_call | solution.py:170
  119.1 9.8 %attend.3 = (bf16[1024,288]{1,0:T(8,128)(2,1)S(1)}, f32[1024,4]{1,0:T(8,128)S(1)}) custom-call(bf16[1024,864]{1,0:T(8,128)(2,1)S(1)} %copy-done.1), custom_call_target="tpu_custom_call" | custom-call | flops 4831838208 | bytes 2359296 | tf_op jit(solution)/shard_map/attend/pallas_call | solution.py:544
  132.8 7.6 %project_out.1.refs_0_.refs_4_ = bf16[1024,1152]{1,0:T(8,128)(2,1)} custom-call(bf16[1024,288]{1,0:T(8,128)(2,1)} %copy-done.2, bf16[1024,288]{1,0:T(8,128)(2,1)} %copy-done.4, bf16[1152,576]{1,0:T(8,128)(2,1)} %bitcast.180, bf16[1152,576]{1,0:T(8,128)(2,1)} %bitcast.181), custom_call_target="tpu_custom_call" | custom-call | bytes 6193152 | tf_op jit(solution)/shard_map/project_out/pallas_call | solution.py:170
  145.7 8.0 %middle_norm.1 = (f32[1024,1152]{1,0:T(8,128)}, bf16[1024,1152]{1,0:T(8,128)(2,1)}, bf16[1024,1152]{1,0:T(8,128)(2,1)}, f32[1,1152]{1,0:T(1,128)}) custom-call(bf16[1024,1152]{1,0:T(8,128)(2,1)} %project_out.1.refs_0_.refs_4_, bf16[1024,1152]{1,0:T(8,128)(2,1)} %collective-permute-done.15.refs_1_.refs_5_, ...), custom_call_target="tpu_custom_call" | custom-call | bytes 18902016 | tf_op jit(solution)/shard_map/middle_norm/pallas_call | solution.py:170
  153.7 10.1 %feed_forward.2 = (bf16[1024,1152]{1,0:T(8,128)(2,1)}, f32[1024,1152]{1,0:T(8,128)}) custom-call(bf16[1024,1152]{1,0:T(8,128)(2,1)} %get-tuple-element.101.refs_0_, f32[1,1152]{1,0:T(1,128)} %slice.330.refs_1_, bf16[1152,1152]{1,0:T(8,128)(2,1)} %all-gather.6.cloned.1.call-done.refs_2_.refs_3_), custom_call_target="tpu_custom_call" | custom-call | bytes 12096000 | tf_op jit(solution)/shard_map/feed_forward/pallas_call | solution.py:170
  163.9 5.0 fusion.33
  172.0 28.7 %collective-permute-done.16.refs_2_.refs_5_ = bf16[1152,1152]{1,0:T(8,128)(2,1)} collective-permute-done((bf16[1152,1152]{1,0:T(8,128)(2,1)}, bf16[1152,1152]{1,0:T(8,128)(2,1)}, u32[]{:S(2)}, u32[]{:S(2)}) %collective-permute-start.16) | collective-permute-done | bytes 2654240 | tf_op jit(solution)/shard_map/ppermute | solution.py:25
  200.8 10.1 %feed_forward.3 = (bf16[1024,1152]{1,0:T(8,128)(2,1)}, f32[1024,1152]{1,0:T(8,128)}) custom-call(bf16[1024,1152]{1,0:T(8,128)(2,1)} %get-tuple-element.101.refs_0_, f32[1,1152]{1,0:T(1,128)} %slice.333.refs_1_, bf16[1152,1152]{1,0:T(8,128)(2,1)} %collective-permute-done.16.refs_2_.refs_5_), custom_call_target="tpu_custom_call" | custom-call | bytes 12096000 | tf_op jit(solution)/shard_map/feed_forward/pallas_call | solution.py:170
  210.9 5.0 convolution_convert_fusion.1
  223.1 16.5 %feed_back.2 = (bf16[1024,1152]{1,0:T(8,128)(2,1)}, f32[1024,1152]{1,0:T(8,128)}, f32[1024,1152]{1,0:T(8,128)}, f32[1,1152]{1,0:T(1,128)}) custom-call(bf16[1024,1152]{1,0:T(8,128)(2,1)} %get-tuple-element.109.refs_0_, bf16[1024,1152]{1,0:T(8,128)(2,1)} %get-tuple-element.100.refs_1_, f32[1024,1152]{1,0:T(8,128)} %get-tuple-element.105.refs_2_, ...), custom_call_target="tpu_custom_call" | custom-call | bytes 29200896 | tf_op jit(solution)/shard_map/feed_back/pallas_call | solution.py:170
  246.7 17.7 %feed_back.3 = (bf16[1024,1152]{1,0:T(8,128)(2,1)}, bf16[1024,1152]{1,0:T(8,128)(2,1)}, bf16[1024,1152]{1,0:T(8,128)(2,1)}, f32[1,1152]{1,0:T(1,128)}) custom-call(bf16[1024,1152]{1,0:T(8,128)(2,1)} %get-tuple-element.109.refs_0_, bf16[1024,1152]{1,0:T(8,128)(2,1)} %get-tuple-element.103.refs_1_, f32[1024,1152]{1,0:T(8,128)} %get-tuple-element.110.refs_2_, ...), custom_call_target="tpu_custom_call" | custom-call | bytes 33919488 | tf_op jit(solution)/shard_map/feed_back/pallas_call | solution.py:170
  264.5 6.6 %convolution_convert_fusion = bf16[1152,1152]{1,0:T(8,128)(2,1)} fusion(bf16[1024,1152]{1,0:T(8,128)(2,1)S(1)} %copy-done.11, bf16[1024,1152]{1,0:T(8,128)(2,1)} %get-tuple-element.116), kind=kOutput, calls=%fused_computation | convolution fusion | flops 2719236096 | bytes 7372800 | tf_op jit(solution)/shard_map/dot_general | solution.py:424
  283.1 4.7 sum_and_split.3
  292.2 15.3 %middle_back.1 = (f32[1024,1152]{1,0:T(8,128)}, bf16[1024,1152]{1,0:T(8,128)(2,1)}, bf16[1024,288]{1,0:T(8,128)(2,1)}, bf16[1024,288]{1,0:T(8,128)(2,1)}, f32[8,1152]{1,0:T(8,128)}) custom-call(bf16[1024,1152]{1,0:T(8,128)(2,1)} %get-tuple-element.122.refs_0_, bf16[1024,1152]{1,0:T(8,128)(2,1)} %collective-permute-done.21.refs_1_, ...), custom_call_target="tpu_custom_call" | custom-call | bytes 27477504 | tf_op jit(solution)/shard_map/middle_back/pallas_call | solution.py:170
  312.5 4.3 fusion.35
  324.1 19.8 %attend_back.2.refs_0_ = bf16[1024,864]{1,0:T(8,128)(2,1)} custom-call(bf16[1024,864]{1,0:T(8,128)(2,1)} %project.1.x_ref, bf16[1024,288]{1,0:T(8,128)(2,1)} %get-tuple-element.129.g_ref, f32[4,1,1024]{2,1,0:T(1,128)} %reshape.195.lse_ref), custom_call_target="tpu_custom_call" | custom-call | flops 12079595520 | bytes 3538944 | tf_op jit(solution)/shard_map/attend_back/pallas_call | solution.py:629
  345.7 5.4 %convolution_convert_fusion.2 = bf16[1152,864]{0,1:T(8,128)(2,1)} fusion(bf16[1024,1152]{1,0:T(8,128)(2,1)S(1)} %copy-done.20, bf16[1024,864]{1,0:T(8,128)(2,1)} %attend_back.2.refs_0_), kind=kOutput, calls=%fused_computation.8 | convolution fusion | flops 2039427072 | bytes 6119424 | tf_op jit(solution)/shard_map/dot_general | solution.py:424
  358.0 7.9 %project_back.2.refs_1_ = f32[1024,1152]{1,0:T(8,128)} custom-call(bf16[1024,864]{1,0:T(8,128)(2,1)} %attend_back.2.refs_0_, bf16[1152,896]{1,0:T(8,128)(2,1)} %collective-permute-done.13.refs_2_.refs_1_), custom_call_target="tpu_custom_call" | custom-call | bytes 8552448 | tf_op jit(solution)/shard_map/project_back/pallas_call | solution.py:170
  366.1 5.3 %collective-permute-done.30 = bf16[2,144,1152]{2,1,0:T(8,128)(2,1)S(1)} collective-permute-done((bf16[2,144,1152]{2,1,0:T(8,128)(2,1)S(1)}, bf16[2,144,1152]{2,1,0:T(8,128)(2,1)S(1)}, u32[]{:S(2)}, u32[]{:S(2)}) %collective-permute-start.30) | collective-permute-done | bytes 663584 | tf_op jit(solution)/shard_map/ppermute | solution.py:30
  374.1 4.6 sum_and_split.4
  384.8 19.7 %attend_back.3.refs_0_ = bf16[1024,864]{1,0:T(8,128)(2,1)} custom-call(bf16[1024,864]{1,0:T(8,128)(2,1)} %get-tuple-element.88.x_ref, bf16[1024,288]{1,0:T(8,128)(2,1)} %get-tuple-element.137.g_ref, f32[4,1,1024]{2,1,0:T(1,128)} %reshape.197.lse_ref), custom_call_target="tpu_custom_call" | custom-call | flops 12079595520 | bytes 3538944 | tf_op jit(solution)/shard_map/attend_back/pallas_call | solution.py:629
  406.6 8.6 %project_back.3.refs_0_ = bf16[1024,1152]{1,0:T(8,128)(2,1)} custom-call(bf16[1024,864]{1,0:T(8,128)(2,1)} %attend_back.3.refs_0_, f32[1024,1152]{1,0:T(8,128)} %project_back.2.refs_1_, bf16[1152,896]{1,0:T(8,128)(2,1)} %all-gather.4.cloned.1.call-done.refs_4_.refs_2_), custom_call_target="tpu_custom_call" | custom-call | bytes 10911744 | tf_op jit(solution)/shard_map/project_back/pallas_call | solution.py:170
  426.4 4.1 finish.1
  432.9 4.8 first_back.1
  451.7 4.6 collective-permute-done.38.x_ref
  461.9 4.6 sum_and_split.5
  493.1 10.3 %collective-permute-done.46 = f32[2,2,2,144]{3,2,1,0:T(2,128)S(1)} collective-permute-done((f32[2,2,2,144]{3,2,1,0:T(2,128)S(1)}, f32[2,2,2,144]{3,2,1,0:T(2,128)S(1)}, u32[]{:S(2)}, u32[]{:S(2)}) %collective-permute-start.46) | collective-permute-done | bytes 4640 | tf_op jit(solution)/shard_map/ppermute | solution.py:30
  507.9 5.9 %collective-permute-done.47 = f32[1,2,4,144]{3,2,1,0:T(4,128)S(1)} collective-permute-done((f32[1,2,4,144]{3,2,1,0:T(4,128)S(1)}, f32[1,2,4,144]{3,2,1,0:T(4,128)S(1)}, u32[]{:S(2)}, u32[]{:S(2)}) %collective-permute-start.47) | collective-permute-done | bytes 4640 | tf_op jit(solution)/shard_map/ppermute | solution.py:30
  (373 shorter events, 206.7 us)
Async XLA Ops:
  7.2 57.2 %all-gather.4.cloned.1.call-start = ((), (), s32[]{:S(2)}) async-start(), calls=%async_computation | async-start | bytes 2322432 | tf_op jit(solution)/shard_map/all_gather | solution.py:681
  12.0 128.5 %all-gather.6.cloned.1.call-start = ((), (), s32[]{:S(2)}) async-start(), calls=%async_computation.1 | async-start | bytes 2985984 | tf_op jit(solution)/shard_map/all_gather | solution.py:681
  13.8 43.2 %collective-permute-start.9 = (bf16[144,1440]{1,0:T(8,128)(2,1)}, bf16[144,1440]{1,0:T(8,128)(2,1)}, u32[]{:S(2)}, u32[]{:S(2)}) collective-permute-start(bf16[144,1440]{1,0:T(8,128)(2,1)} %pad_maximum_fusion.12), channel_id=1, source_target_pairs={{0,2},{1,3},{2,0},{3,1},{4,6},{5,7},{6,4},{7,5},{8,10},{9,11},{10,... | collective-permute-start | bytes 1244168 | tf_op jit(solution)/shard_map/ppermute | solution.py:25
  27.9 38.0 %collective-permute-start = (bf16[1024,1152]{1,0:T(8,128)(2,1)}, bf16[1024,1152]{1,0:T(8,128)(2,1)}, u32[]{:S(2)}, u32[]{:S(2)}) collective-permute-start(bf16[1024,1152]{1,0:T(8,128)(2,1)} %pad_maximum_fusion), channel_id=1, source_target_pairs={{0,1},{1,0},{2,3},{3,2},{4,5},{5,4},{6,7},{7,6},{8,9},{9,8},{10,11... | collective-permute-start | bytes 7077896 | tf_op jit(solution)/shard_map/ppermute | solution.py:21
  28.0 195.2 %all-gather.8.cloned.1.call-start = ((), (), s32[]{:S(2)}) async-start(), calls=%async_computation.2 | async-start | bytes 5971968 | tf_op jit(solution)/shard_map/all_gather | solution.py:681
  60.0 31.8 %collective-permute-start.12 = (bf16[144,576]{1,0:T(8,128)(2,1)S(1)}, bf16[144,576]{1,0:T(8,128)(2,1)S(1)}, u32[]{:S(2)}, u32[]{:S(2)}) collective-permute-start(bf16[144,576]{1,0:T(8,128)(2,1)S(1)} %pad_maximum_fusion.14), channel_id=1, source_target_pairs={{0,24},{4,28},{8,16},{12,20},{16,8},{20,12},{24,0},{28,4},{1,25},{... | collective-permute-start | bytes 497672 | tf_op jit(solution)/shard_map/ppermute | solution.py:30
  63.5 28.3 %collective-permute-start.11 = (bf16[144,576]{1,0:T(8,128)(2,1)S(1)}, bf16[144,576]{1,0:T(8,128)(2,1)}, u32[]{:S(2)}, u32[]{:S(2)}) collective-permute-start(bf16[144,576]{1,0:T(8,128)(2,1)S(1)} %pad_maximum_fusion.14), channel_id=1, source_target_pairs={{0,16},{4,20},{8,24},{12,28},{16,0},{20,4},{24,8},{28,12},{1,17},{... | collective-permute-start | bytes 497672 | tf_op jit(solution)/shard_map/ppermute | solution.py:30
  63.5 28.3 %collective-permute-start.10 = (bf16[144,576]{1,0:T(8,128)(2,1)S(1)}, bf16[144,576]{1,0:T(8,128)(2,1)}, u32[]{:S(2)}, u32[]{:S(2)}) collective-permute-start(bf16[144,576]{1,0:T(8,128)(2,1)S(1)} %pad_maximum_fusion.14), channel_id=1, source_target_pairs={{0,8},{4,12},{8,0},{12,4},{16,24},{20,28},{24,16},{28,20},{1,9},{5... | collective-permute-start | bytes 497672 | tf_op jit(solution)/shard_map/ppermute | solution.py:30
  64.4 45.9 %collective-permute-start.13 = (bf16[1152,896]{1,0:T(8,128)(2,1)}, bf16[1152,896]{1,0:T(8,128)(2,1)}, u32[]{:S(2)}, u32[]{:S(2)}) collective-permute-start(bf16[1152,896]{1,0:T(8,128)(2,1)} %all-gather.4.cloned.1.call-done.refs_4_.refs_2_), channel_id=1, source_target_pairs={{0,2},{1,3},{2,0},{3,1},{4,6},{5,7},{6,4},{7,5},{8,10},{9,11},{10,... | collective-permute-start | bytes 6193160 | tf_op jit(solution)/shard_map/ppermute | solution.py:25
  93.0 36.0 %collective-permute-start.14 = (bf16[4,144,576]{2,1,0:T(8,128)(2,1)S(1)}, bf16[4,144,576]{2,1,0:T(8,128)(2,1)}, u32[]{:S(2)}, u32[]{:S(2)}) collective-permute-start(bf16[4,144,576]{2,1,0:T(8,128)(2,1)S(1)} %get-tuple-element.182), channel_id=1, source_target_pairs={{0,4},{4,0},{8,12},{12,8},{16,20},{20,16},{24,28},{28,24},{1,5},{5... | collective-permute-start | bytes 1990664 | tf_op jit(solution)/shard_map/ppermute | solution.py:30
  140.5 60.3 %collective-permute-start.16 = (bf16[1152,1152]{1,0:T(8,128)(2,1)}, bf16[1152,1152]{1,0:T(8,128)(2,1)}, u32[]{:S(2)}, u32[]{:S(2)}) collective-permute-start(bf16[1152,1152]{1,0:T(8,128)(2,1)} %all-gather.6.cloned.1.call-done.refs_2_.refs_3_), channel_id=1, source_target_pairs={{0,2},{1,3},{2,0},{3,1},{4,6},{5,7},{6,4},{7,5},{8,10},{9,11},{10,... | collective-permute-start | bytes 7962632 | tf_op jit(solution)/shard_map/ppermute | solution.py:25
  217.3 22.4 %collective-permute-start.17 = (bf16[2,144,1152]{2,1,0:T(8,128)(2,1)}, bf16[2,144,1152]{2,1,0:T(8,128)(2,1)}, u32[]{:S(2)}, u32[]{:S(2)}) collective-permute-start(bf16[2,144,1152]{2,1,0:T(8,128)(2,1)} %get-tuple-element.175), channel_id=1, source_target_pairs={{0,4},{4,0},{8,12},{12,8},{16,20},{20,16},{24,28},{28,24},{1,5},{5... | collective-permute-start | bytes 1990664 | tf_op jit(solution)/shard_map/ppermute | solution.py:30
  219.2 20.4 %collective-permute-start.18 = (bf16[2,144,1152]{2,1,0:T(8,128)(2,1)}, bf16[2,144,1152]{2,1,0:T(8,128)(2,1)}, u32[]{:S(2)}, u32[]{:S(2)}) collective-permute-start(bf16[2,144,1152]{2,1,0:T(8,128)(2,1)} %get-tuple-element.176), channel_id=1, source_target_pairs={{0,2},{1,3},{2,0},{3,1},{4,6},{5,7},{6,4},{7,5},{8,10},{9,11},{10,... | collective-permute-start | bytes 1990664 | tf_op jit(solution)/shard_map/ppermute | solution.py:25
  243.4 39.7 %collective-permute-start.20 = (bf16[4,144,1152]{2,1,0:T(8,128)(2,1)}, bf16[4,144,1152]{2,1,0:T(8,128)(2,1)}, u32[]{:S(2)}, u32[]{:S(2)}) collective-permute-start(bf16[4,144,1152]{2,1,0:T(8,128)(2,1)} %pad_maximum_fusion.5), channel_id=1, source_target_pairs={{0,2},{1,3},{2,0},{3,1},{4,6},{5,7},{6,4},{7,5},{8,10},{9,11},{10,... | collective-permute-start | bytes 3981320 | tf_op jit(solution)/shard_map/ppermute | solution.py:25
  246.1 37.0 %collective-permute-start.19 = (bf16[4,144,1152]{2,1,0:T(8,128)(2,1)}, bf16[4,144,1152]{2,1,0:T(8,128)(2,1)}, u32[]{:S(2)}, u32[]{:S(2)}) collective-permute-start(bf16[4,144,1152]{2,1,0:T(8,128)(2,1)} %pad_maximum_fusion.4), channel_id=1, source_target_pairs={{0,4},{4,0},{8,12},{12,8},{16,20},{20,16},{24,28},{28,24},{1,5},{5... | collective-permute-start | bytes 3981320 | tf_op jit(solution)/shard_map/ppermute | solution.py:30
  264.4 25.7 %collective-permute-start.21 = (bf16[1024,1152]{1,0:T(8,128)(2,1)}, bf16[1024,1152]{1,0:T(8,128)(2,1)}, u32[]{:S(2)}, u32[]{:S(2)}) collective-permute-start(bf16[1024,1152]{1,0:T(8,128)(2,1)} %get-tuple-element.122.refs_0_), channel_id=1, source_target_pairs={{0,1},{1,0},{2,3},{3,2},{4,5},{5,4},{6,7},{7,6},{8,9},{9,8},{10,11... | collective-permute-start | bytes 7077896 | tf_op jit(solution)/shard_map/ppermute | solution.py:21
  278.3 38.5 %collective-permute-start.22 = (bf16[2,144,1152]{2,1,0:T(8,128)(2,1)}, bf16[2,144,1152]{2,1,0:T(8,128)(2,1)}, u32[]{:S(2)}, u32[]{:S(2)}) collective-permute-start(bf16[2,144,1152]{2,1,0:T(8,128)(2,1)} %get-tuple-element.172), channel_id=1, source_target_pairs={{0,4},{4,0},{8,12},{12,8},{16,20},{20,16},{24,28},{28,24},{1,5},{5... | collective-permute-start | bytes 1990664 | tf_op jit(solution)/shard_map/ppermute | solution.py:30
  279.8 37.0 %collective-permute-start.23 = (bf16[2,144,1152]{2,1,0:T(8,128)(2,1)}, bf16[2,144,1152]{2,1,0:T(8,128)(2,1)}, u32[]{:S(2)}, u32[]{:S(2)}) collective-permute-start(bf16[2,144,1152]{2,1,0:T(8,128)(2,1)} %get-tuple-element.173), channel_id=1, source_target_pairs={{0,2},{1,3},{2,0},{3,1},{4,6},{5,7},{6,4},{7,5},{8,10},{9,11},{10,... | collective-permute-start | bytes 1990664 | tf_op jit(solution)/shard_map/ppermute | solution.py:25
  287.8 29.1 %collective-permute-start.24 = (bf16[144,1152]{1,0:T(8,128)(2,1)}, bf16[144,1152]{1,0:T(8,128)(2,1)}, u32[]{:S(2)}, u32[]{:S(2)}) collective-permute-start(bf16[144,1152]{1,0:T(8,128)(2,1)} %get-tuple-element.119), channel_id=1, source_target_pairs={{0,8},{4,12},{8,0},{12,4},{16,24},{20,28},{24,16},{28,20},{1,9},{5... | collective-permute-start | bytes 995336 | tf_op jit(solution)/shard_map/ppermute | solution.py:30
  288.1 28.7 %collective-permute-start.25 = (bf16[144,1152]{1,0:T(8,128)(2,1)}, bf16[144,1152]{1,0:T(8,128)(2,1)}, u32[]{:S(2)}, u32[]{:S(2)}) collective-permute-start(bf16[144,1152]{1,0:T(8,128)(2,1)} %get-tuple-element.120), channel_id=1, source_target_pairs={{0,16},{4,20},{8,24},{12,28},{16,0},{20,4},{24,8},{28,12},{1,17},{... | collective-permute-start | bytes 995336 | tf_op jit(solution)/shard_map/ppermute | solution.py:30
  290.2 26.7 %collective-permute-start.26 = (bf16[144,1152]{1,0:T(8,128)(2,1)}, bf16[144,1152]{1,0:T(8,128)(2,1)}, u32[]{:S(2)}, u32[]{:S(2)}) collective-permute-start(bf16[144,1152]{1,0:T(8,128)(2,1)} %get-tuple-element.121), channel_id=1, source_target_pairs={{0,24},{4,28},{8,16},{12,20},{16,8},{20,12},{24,0},{28,4},{1,25},{... | collective-permute-start | bytes 995336 | tf_op jit(solution)/shard_map/ppermute | solution.py:30
  320.8 53.3 %collective-permute-start.28 = (bf16[4,144,1152]{2,1,0:T(8,128)(2,1)}, bf16[4,144,1152]{2,1,0:T(8,128)(2,1)}, u32[]{:S(2)}, u32[]{:S(2)}) collective-permute-start(bf16[4,144,1152]{2,1,0:T(8,128)(2,1)} %pad_maximum_fusion.7), channel_id=1, source_target_pairs={{0,2},{1,3},{2,0},{3,1},{4,6},{5,7},{6,4},{7,5},{8,10},{9,11},{10,... | collective-permute-start | bytes 3981320 | tf_op jit(solution)/shard_map/ppermute | solution.py:25
  323.5 50.6 %collective-permute-start.27 = (bf16[4,144,1152]{2,1,0:T(8,128)(2,1)}, bf16[4,144,1152]{2,1,0:T(8,128)(2,1)}, u32[]{:S(2)}, u32[]{:S(2)}) collective-permute-start(bf16[4,144,1152]{2,1,0:T(8,128)(2,1)} %pad_maximum_fusion.6), channel_id=1, source_target_pairs={{0,4},{4,0},{8,12},{12,8},{16,20},{20,16},{24,28},{28,24},{1,5},{5... | collective-permute-start | bytes 3981320 | tf_op jit(solution)/shard_map/ppermute | solution.py:30
  355.7 48.8 %collective-permute-start.31 = (bf16[2,144,1152]{2,1,0:T(8,128)(2,1)S(1)}, bf16[2,144,1152]{2,1,0:T(8,128)(2,1)S(1)}, u32[]{:S(2)}, u32[]{:S(2)}) collective-permute-start(bf16[2,144,1152]{2,1,0:T(8,128)(2,1)S(1)} %get-tuple-element.179), channel_id=1, source_target_pairs={{0,2},{1,3},{2,0},{3,1},{4,6},{5,7},{6,4},{7,5},{8,10},{9,11},{10,... | collective-permute-start | bytes 1990664 | tf_op jit(solution)/shard_map/ppermute | solution.py:25
  372.7 79.0 %collective-permute-start.39 = (bf16[4,144,1152]{2,1,0:T(8,128)(2,1)}, bf16[4,144,1152]{2,1,0:T(8,128)(2,1)}, u32[]{:S(2)}, u32[]{:S(2)}) collective-permute-start(bf16[4,144,1152]{2,1,0:T(8,128)(2,1)} %pad_maximum_fusion.9), channel_id=1, source_target_pairs={{0,2},{1,3},{2,0},{3,1},{4,6},{5,7},{6,4},{7,5},{8,10},{9,11},{10,... | collective-permute-start | bytes 3981320 | tf_op jit(solution)/shard_map/ppermute | solution.py:25
  378.7 39.6 %collective-permute-start.32 = (bf16[144,1152]{1,0:T(8,128)(2,1)}, bf16[144,1152]{1,0:T(8,128)(2,1)}, u32[]{:S(2)}, u32[]{:S(2)}) collective-permute-start(bf16[144,1152]{1,0:T(8,128)(2,1)} %get-tuple-element.134), channel_id=1, source_target_pairs={{0,8},{4,12},{8,0},{12,4},{16,24},{20,28},{24,16},{28,20},{1,9},{5... | collective-permute-start | bytes 995336 | tf_op jit(solution)/shard_map/ppermute | solution.py:30
  382.2 36.7 %collective-permute-start.33 = (bf16[144,1152]{1,0:T(8,128)(2,1)}, bf16[144,1152]{1,0:T(8,128)(2,1)}, u32[]{:S(2)}, u32[]{:S(2)}) collective-permute-start(bf16[144,1152]{1,0:T(8,128)(2,1)} %get-tuple-element.135), channel_id=1, source_target_pairs={{0,16},{4,20},{8,24},{12,28},{16,0},{20,4},{24,8},{28,12},{1,17},{... | collective-permute-start | bytes 995336 | tf_op jit(solution)/shard_map/ppermute | solution.py:30
  383.3 35.5 %collective-permute-start.34 = (bf16[144,1152]{1,0:T(8,128)(2,1)}, bf16[144,1152]{1,0:T(8,128)(2,1)}, u32[]{:S(2)}, u32[]{:S(2)}) collective-permute-start(bf16[144,1152]{1,0:T(8,128)(2,1)} %get-tuple-element.136), channel_id=1, source_target_pairs={{0,24},{4,28},{8,16},{12,20},{16,8},{20,12},{24,0},{28,4},{1,25},{... | collective-permute-start | bytes 995336 | tf_op jit(solution)/shard_map/ppermute | solution.py:30
  424.9 31.4 %collective-permute-start.38 = (bf16[4,144,1152]{2,1,0:T(8,128)(2,1)}, bf16[4,144,1152]{2,1,0:T(8,128)(2,1)}, u32[]{:S(2)}, u32[]{:S(2)}) collective-permute-start(bf16[4,144,1152]{2,1,0:T(8,128)(2,1)} %pad_maximum_fusion.8), channel_id=1, source_target_pairs={{0,4},{4,0},{8,12},{12,8},{16,20},{20,16},{24,28},{28,24},{1,5},{5... | collective-permute-start | bytes 3981320 | tf_op jit(solution)/shard_map/ppermute | solution.py:30
  480.4 34.2 %collective-permute-start.48 = (bf16[144,1152]{1,0:T(8,128)(2,1)S(1)}, bf16[144,1152]{1,0:T(8,128)(2,1)S(1)}, u32[]{:S(2)}, u32[]{:S(2)}) collective-permute-start(bf16[144,1152]{1,0:T(8,128)(2,1)S(1)} %copy-done.44), channel_id=1, source_target_pairs={{0,8},{4,12},{8,0},{12,4},{16,24},{20,28},{24,16},{28,20},{1,9},{5... | collective-permute-start | bytes 995336 | tf_op jit(solution)/shard_map/ppermute | solution.py:30
  481.3 33.3 %collective-permute-start.49 = (bf16[144,1152]{1,0:T(8,128)(2,1)S(1)}, bf16[144,1152]{1,0:T(8,128)(2,1)S(1)}, u32[]{:S(2)}, u32[]{:S(2)}) collective-permute-start(bf16[144,1152]{1,0:T(8,128)(2,1)S(1)} %copy-done.43), channel_id=1, source_target_pairs={{0,16},{4,20},{8,24},{12,28},{16,0},{20,4},{24,8},{28,12},{1,17},{... | collective-permute-start | bytes 995336 | tf_op jit(solution)/shard_map/ppermute | solution.py:30
  482.2 32.4 %collective-permute-start.50 = (bf16[144,1152]{1,0:T(8,128)(2,1)S(1)}, bf16[144,1152]{1,0:T(8,128)(2,1)S(1)}, u32[]{:S(2)}, u32[]{:S(2)}) collective-permute-start(bf16[144,1152]{1,0:T(8,128)(2,1)S(1)} %copy-done.42), channel_id=1, source_target_pairs={{0,24},{4,28},{8,16},{12,20},{16,8},{20,12},{24,0},{28,4},{1,25},{... | collective-permute-start | bytes 995336 | tf_op jit(solution)/shard_map/ppermute | solution.py:30
  (67 other events, 561.9 us)
Sparse Core Ops, SparseCore 0:
  12.1 51.1 all-gather.3
  65.5 67.6 all-gather.5
  136.0 87.1 all-gather.7

commit v5 on v4

--- a/solution.py
+++ b/solution.py
@@ -569,7 +569,7 @@
     )(qkv)
 
 
-def attend_back(qkv, grad_mix, lse, first, heads, block=1024, unroll=2):
+def attend_back(qkv, grad_mix, lse, first, heads, block=1024, unroll=4):
     rows, cols = qkv.shape
     size = HEAD_DIM
     all_heads = cols // (3 * size)

time: 530 us -> 523 us (0.987)
  Pallas kernels: 199 us -> 192 us
    pallas_call x2, Pallas kernels: 39.5 us -> 32.7 us  [attend_back(): pl.pallas_call(kernel, out_shape=jax.ShapeDtypeStruct((rows, heads * 3 *...]
  transfers between devices with their start and end apart: 54 -> 54, of which waited for: 18 -> 18; matrix products, arithmetic and copies ran while one was open for 24% -> 25% of each run, Pallas kernels for 38% -> 37%
where the time goes in v5:
time: 523 us; the launch traced here: 517 us
  Pallas kernels  192 us (37%)
  waiting for transfers between devices  102 us (20%)
  local copies, waits for them, and re-layouts  61.8 us (12%)
  starting transfers between devices  59.5 us (11%)
  other arithmetic  46.9 us (9%)
  matrix products  38.8 us (7%)
  between operations  15.3 us (3%)
    pallas_call x13, Pallas kernels, row_step(): pl.pallas_call(kernel, out_shape=outs, grid=(steps,), in_specs=specs, out...  126 us
    ppermute x31, waiting for transfers between devices, swap_apart(): return lax.ppermute(values, 'dp', [(i, i ^ apart) for i in range(size)])  50.5 us
    ppermute x12, waiting for transfers between devices, swap_y(): return lax.ppermute(values, 'tensor', [(i, i ^ 2) for i in range(4)])  49.5 us
    ppermute x31, starting transfers between devices, swap_apart(): return lax.ppermute(values, 'dp', [(i, i ^ apart) for i in range(size)])  47.7 us
    dot_general x8, matrix products, weight_term(): lax.dot_general(left, right, (((0,), (0,)), ((), ())), preferred_element_...  35.7 us
    pallas_call x2, Pallas kernels, attend_back(): pl.pallas_call(kernel, out_shape=jax.ShapeDtypeStruct((rows, heads * 3 *...  32.7 us
    pallas_call x2, Pallas kernels, attend(): pl.pallas_call(kernel, out_shape=(jax.ShapeDtypeStruct((rows, heads * siz...  18.8 us
    unnamed x97, local copies, waits for them, and re-layouts  14.8 us
  transfers between devices with their start and end apart: 54, of which 18 were waited for; matrix products, arithmetic and copies ran while one was open for 25% of the time, Pallas kernels for 37%

profile of v5, /device:TPU:0, one launch (start us, length us, event | category | flops | bytes accessed | tf_op | source)
XLA Modules:
  0.0 516.8 jit_solution(4147374914347514868)
XLA Ops:
  37.5 4.1 collective-permute-done.6
  45.3 5.7 %collective-permute-done.7 = f32[2,6912]{1,0:T(2,128)S(1)} collective-permute-done((f32[2,6912]{1,0:T(2,128)S(1)}, f32[2,6912]{1,0:T(2,128)S(1)}, u32[]{:S(2)}, u32[]{:S(2)}) %collective-permute-start.7) | collective-permute-done | bytes 55328 | tf_op jit(solution)/shard_map/ppermute | solution.py:30
  71.5 8.5 %norm_project.1 = (bf16[1024,1152]{1,0:T(8,128)(2,1)}, bf16[1024,864]{1,0:T(8,128)(2,1)}) custom-call(bf16[1024,1152]{1,0:T(8,128)(2,1)} %pad_maximum_fusion.1.refs_0_.refs_2_, f32[1,1152]{1,0:T(1,128)} %get-tuple-element.208.refs_1_.refs_4_, f32[1,1152]{1,0:T(1,128)} %get-tuple-element.207.refs_2_, f32[1,864]{1,0:T(1,128)} %reshape.186.refs_3_, ...), custom_call_target="tpu_custom_call" | custom-call | bytes 8565120 | tf_op jit(solution)/shard_map/norm_project/pallas_call | solution.py:170
  81.5 9.3 %attend.2 = (bf16[1024,288]{1,0:T(8,128)(2,1)S(1)}, f32[1024,4]{1,0:T(8,128)S(1)}) custom-call(bf16[1024,864]{1,0:T(8,128)(2,1)S(1)} %copy-done.6), custom_call_target="tpu_custom_call" | custom-call | flops 4831838208 | bytes 2359296 | tf_op jit(solution)/shard_map/attend/pallas_call | solution.py:544
  94.7 15.6 %collective-permute-done.13.refs_2_.refs_1_ = bf16[1152,896]{1,0:T(8,128)(2,1)} collective-permute-done((bf16[1152,896]{1,0:T(8,128)(2,1)}, bf16[1152,896]{1,0:T(8,128)(2,1)}, u32[]{:S(2)}, u32[]{:S(2)}) %collective-permute-start.13) | collective-permute-done | bytes 2064416 | tf_op jit(solution)/shard_map/ppermute | solution.py:25
  110.3 7.3 %project.1.x_ref = bf16[1024,864]{1,0:T(8,128)(2,1)} custom-call(bf16[1024,1152]{1,0:T(8,128)(2,1)} %get-tuple-element.142.refs_0_, f32[1,864]{1,0:T(1,128)} %reshape.187.refs_1_, bf16[1152,896]{1,0:T(8,128)(2,1)} %collective-permute-done.13.refs_2_.refs_1_), custom_call_target="tpu_custom_call" | custom-call | bytes 6196608 | tf_op jit(solution)/shard_map/project/pallas_call | solution.py:170
  119.1 9.5 %attend.3 = (bf16[1024,288]{1,0:T(8,128)(2,1)S(1)}, f32[1024,4]{1,0:T(8,128)S(1)}) custom-call(bf16[1024,864]{1,0:T(8,128)(2,1)S(1)} %copy-done.1), custom_call_target="tpu_custom_call" | custom-call | flops 4831838208 | bytes 2359296 | tf_op jit(solution)/shard_map/attend/pallas_call | solution.py:544
  132.5 7.6 %project_out.1.refs_0_.refs_4_ = bf16[1024,1152]{1,0:T(8,128)(2,1)} custom-call(bf16[1024,288]{1,0:T(8,128)(2,1)} %copy-done.2, bf16[1024,288]{1,0:T(8,128)(2,1)} %copy-done.4, bf16[1152,576]{1,0:T(8,128)(2,1)} %bitcast.180, bf16[1152,576]{1,0:T(8,128)(2,1)} %bitcast.181), custom_call_target="tpu_custom_call" | custom-call | bytes 6193152 | tf_op jit(solution)/shard_map/project_out/pallas_call | solution.py:170
  145.4 8.0 %middle_norm.1 = (f32[1024,1152]{1,0:T(8,128)}, bf16[1024,1152]{1,0:T(8,128)(2,1)}, bf16[1024,1152]{1,0:T(8,128)(2,1)}, f32[1,1152]{1,0:T(1,128)}) custom-call(bf16[1024,1152]{1,0:T(8,128)(2,1)} %project_out.1.refs_0_.refs_4_, bf16[1024,1152]{1,0:T(8,128)(2,1)} %collective-permute-done.15.refs_1_.refs_5_, ...), custom_call_target="tpu_custom_call" | custom-call | bytes 18902016 | tf_op jit(solution)/shard_map/middle_norm/pallas_call | solution.py:170
  153.4 10.1 %feed_forward.2 = (bf16[1024,1152]{1,0:T(8,128)(2,1)}, f32[1024,1152]{1,0:T(8,128)}) custom-call(bf16[1024,1152]{1,0:T(8,128)(2,1)} %get-tuple-element.101.refs_0_, f32[1,1152]{1,0:T(1,128)} %slice.330.refs_1_, bf16[1152,1152]{1,0:T(8,128)(2,1)} %all-gather.6.cloned.1.call-done.refs_2_.refs_3_), custom_call_target="tpu_custom_call" | custom-call | bytes 12096000 | tf_op jit(solution)/shard_map/feed_forward/pallas_call | solution.py:170
  163.6 5.0 fusion.33
  171.7 28.7 %collective-permute-done.16.refs_2_.refs_5_ = bf16[1152,1152]{1,0:T(8,128)(2,1)} collective-permute-done((bf16[1152,1152]{1,0:T(8,128)(2,1)}, bf16[1152,1152]{1,0:T(8,128)(2,1)}, u32[]{:S(2)}, u32[]{:S(2)}) %collective-permute-start.16) | collective-permute-done | bytes 2654240 | tf_op jit(solution)/shard_map/ppermute | solution.py:25
  200.4 10.4 %feed_forward.3 = (bf16[1024,1152]{1,0:T(8,128)(2,1)}, f32[1024,1152]{1,0:T(8,128)}) custom-call(bf16[1024,1152]{1,0:T(8,128)(2,1)} %get-tuple-element.101.refs_0_, f32[1,1152]{1,0:T(1,128)} %slice.333.refs_1_, bf16[1152,1152]{1,0:T(8,128)(2,1)} %collective-permute-done.16.refs_2_.refs_5_), custom_call_target="tpu_custom_call" | custom-call | bytes 12096000 | tf_op jit(solution)/shard_map/feed_forward/pallas_call | solution.py:170
  210.8 5.0 convolution_convert_fusion.1
  223.0 16.5 %feed_back.2 = (bf16[1024,1152]{1,0:T(8,128)(2,1)}, f32[1024,1152]{1,0:T(8,128)}, f32[1024,1152]{1,0:T(8,128)}, f32[1,1152]{1,0:T(1,128)}) custom-call(bf16[1024,1152]{1,0:T(8,128)(2,1)} %get-tuple-element.109.refs_0_, bf16[1024,1152]{1,0:T(8,128)(2,1)} %get-tuple-element.100.refs_1_, f32[1024,1152]{1,0:T(8,128)} %get-tuple-element.105.refs_2_, ...), custom_call_target="tpu_custom_call" | custom-call | bytes 29200896 | tf_op jit(solution)/shard_map/feed_back/pallas_call | solution.py:170
  246.5 17.7 %feed_back.3 = (bf16[1024,1152]{1,0:T(8,128)(2,1)}, bf16[1024,1152]{1,0:T(8,128)(2,1)}, bf16[1024,1152]{1,0:T(8,128)(2,1)}, f32[1,1152]{1,0:T(1,128)}) custom-call(bf16[1024,1152]{1,0:T(8,128)(2,1)} %get-tuple-element.109.refs_0_, bf16[1024,1152]{1,0:T(8,128)(2,1)} %get-tuple-element.103.refs_1_, f32[1024,1152]{1,0:T(8,128)} %get-tuple-element.110.refs_2_, ...), custom_call_target="tpu_custom_call" | custom-call | bytes 33919488 | tf_op jit(solution)/shard_map/feed_back/pallas_call | solution.py:170
  264.4 6.6 %convolution_convert_fusion = bf16[1152,1152]{1,0:T(8,128)(2,1)} fusion(bf16[1024,1152]{1,0:T(8,128)(2,1)S(1)} %copy-done.11, bf16[1024,1152]{1,0:T(8,128)(2,1)} %get-tuple-element.116), kind=kOutput, calls=%fused_computation | convolution fusion | flops 2719236096 | bytes 7372800 | tf_op jit(solution)/shard_map/dot_general | solution.py:424
  282.9 4.7 sum_and_split.3
  292.0 15.1 %middle_back.1 = (f32[1024,1152]{1,0:T(8,128)}, bf16[1024,1152]{1,0:T(8,128)(2,1)}, bf16[1024,288]{1,0:T(8,128)(2,1)}, bf16[1024,288]{1,0:T(8,128)(2,1)}, f32[8,1152]{1,0:T(8,128)}) custom-call(bf16[1024,1152]{1,0:T(8,128)(2,1)} %get-tuple-element.122.refs_0_, bf16[1024,1152]{1,0:T(8,128)(2,1)} %collective-permute-done.21.refs_1_, ...), custom_call_target="tpu_custom_call" | custom-call | bytes 27477504 | tf_op jit(solution)/shard_map/middle_back/pallas_call | solution.py:170
  312.2 4.3 fusion.35
  323.7 16.5 %attend_back.2.refs_0_ = bf16[1024,864]{1,0:T(8,128)(2,1)} custom-call(bf16[1024,864]{1,0:T(8,128)(2,1)} %project.1.x_ref, bf16[1024,288]{1,0:T(8,128)(2,1)} %get-tuple-element.129.g_ref, f32[4,1,1024]{2,1,0:T(1,128)} %reshape.195.lse_ref), custom_call_target="tpu_custom_call" | custom-call | flops 12079595520 | bytes 3538944 | tf_op jit(solution)/shard_map/attend_back/pallas_call | solution.py:629
  342.1 5.4 %convolution_convert_fusion.2 = bf16[1152,864]{0,1:T(8,128)(2,1)} fusion(bf16[1024,1152]{1,0:T(8,128)(2,1)S(1)} %copy-done.20, bf16[1024,864]{1,0:T(8,128)(2,1)} %attend_back.2.refs_0_), kind=kOutput, calls=%fused_computation.8 | convolution fusion | flops 2039427072 | bytes 6119424 | tf_op jit(solution)/shard_map/dot_general | solution.py:424
  354.3 7.9 %project_back.2.refs_1_ = f32[1024,1152]{1,0:T(8,128)} custom-call(bf16[1024,864]{1,0:T(8,128)(2,1)} %attend_back.2.refs_0_, bf16[1152,896]{1,0:T(8,128)(2,1)} %collective-permute-done.13.refs_2_.refs_1_), custom_call_target="tpu_custom_call" | custom-call | bytes 8552448 | tf_op jit(solution)/shard_map/project_back/pallas_call | solution.py:170
  362.4 5.3 %collective-permute-done.30 = bf16[2,144,1152]{2,1,0:T(8,128)(2,1)S(1)} collective-permute-done((bf16[2,144,1152]{2,1,0:T(8,128)(2,1)S(1)}, bf16[2,144,1152]{2,1,0:T(8,128)(2,1)S(1)}, u32[]{:S(2)}, u32[]{:S(2)}) %collective-permute-start.30) | collective-permute-done | bytes 663584 | tf_op jit(solution)/shard_map/ppermute | solution.py:30
  370.5 4.8 sum_and_split.4
  381.5 16.2 %attend_back.3.refs_0_ = bf16[1024,864]{1,0:T(8,128)(2,1)} custom-call(bf16[1024,864]{1,0:T(8,128)(2,1)} %get-tuple-element.88.x_ref, bf16[1024,288]{1,0:T(8,128)(2,1)} %get-tuple-element.137.g_ref, f32[4,1,1024]{2,1,0:T(1,128)} %reshape.197.lse_ref), custom_call_target="tpu_custom_call" | custom-call | flops 12079595520 | bytes 3538944 | tf_op jit(solution)/shard_map/attend_back/pallas_call | solution.py:629
  399.9 8.6 %project_back.3.refs_0_ = bf16[1024,1152]{1,0:T(8,128)(2,1)} custom-call(bf16[1024,864]{1,0:T(8,128)(2,1)} %attend_back.3.refs_0_, f32[1024,1152]{1,0:T(8,128)} %project_back.2.refs_1_, bf16[1152,896]{1,0:T(8,128)(2,1)} %all-gather.4.cloned.1.call-done.refs_4_.refs_2_), custom_call_target="tpu_custom_call" | custom-call | bytes 10911744 | tf_op jit(solution)/shard_map/project_back/pallas_call | solution.py:170
  425.9 4.8 first_back.1
  444.7 4.8 collective-permute-done.38.x_ref
  455.1 4.8 sum_and_split.5
  486.7 10.3 %collective-permute-done.46 = f32[2,2,2,144]{3,2,1,0:T(2,128)S(1)} collective-permute-done((f32[2,2,2,144]{3,2,1,0:T(2,128)S(1)}, f32[2,2,2,144]{3,2,1,0:T(2,128)S(1)}, u32[]{:S(2)}, u32[]{:S(2)}) %collective-permute-start.46) | collective-permute-done | bytes 4640 | tf_op jit(solution)/shard_map/ppermute | solution.py:30
  501.4 6.0 %collective-permute-done.47 = f32[1,2,4,144]{3,2,1,0:T(4,128)S(1)} collective-permute-done((f32[1,2,4,144]{3,2,1,0:T(4,128)S(1)}, f32[1,2,4,144]{3,2,1,0:T(4,128)S(1)}, u32[]{:S(2)}, u32[]{:S(2)}) %collective-permute-start.47) | collective-permute-done | bytes 4640 | tf_op jit(solution)/shard_map/ppermute | solution.py:30
  (373 shorter events, 206.6 us)
Async XLA Ops:
  7.2 57.2 %all-gather.4.cloned.1.call-start = ((), (), s32[]{:S(2)}) async-start(), calls=%async_computation | async-start | bytes 2322432 | tf_op jit(solution)/shard_map/all_gather | solution.py:681
  12.0 128.2 %all-gather.6.cloned.1.call-start = ((), (), s32[]{:S(2)}) async-start(), calls=%async_computation.1 | async-start | bytes 2985984 | tf_op jit(solution)/shard_map/all_gather | solution.py:681
  13.8 43.2 %collective-permute-start.9 = (bf16[144,1440]{1,0:T(8,128)(2,1)}, bf16[144,1440]{1,0:T(8,128)(2,1)}, u32[]{:S(2)}, u32[]{:S(2)}) collective-permute-start(bf16[144,1440]{1,0:T(8,128)(2,1)} %pad_maximum_fusion.12), channel_id=1, source_target_pairs={{0,2},{1,3},{2,0},{3,1},{4,6},{5,7},{6,4},{7,5},{8,10},{9,11},{10,... | collective-permute-start | bytes 1244168 | tf_op jit(solution)/shard_map/ppermute | solution.py:25
  27.9 38.0 %collective-permute-start = (bf16[1024,1152]{1,0:T(8,128)(2,1)}, bf16[1024,1152]{1,0:T(8,128)(2,1)}, u32[]{:S(2)}, u32[]{:S(2)}) collective-permute-start(bf16[1024,1152]{1,0:T(8,128)(2,1)} %pad_maximum_fusion), channel_id=1, source_target_pairs={{0,1},{1,0},{2,3},{3,2},{4,5},{5,4},{6,7},{7,6},{8,9},{9,8},{10,11... | collective-permute-start | bytes 7077896 | tf_op jit(solution)/shard_map/ppermute | solution.py:21
  28.0 195.1 %all-gather.8.cloned.1.call-start = ((), (), s32[]{:S(2)}) async-start(), calls=%async_computation.2 | async-start | bytes 5971968 | tf_op jit(solution)/shard_map/all_gather | solution.py:681
  60.0 31.7 %collective-permute-start.12 = (bf16[144,576]{1,0:T(8,128)(2,1)S(1)}, bf16[144,576]{1,0:T(8,128)(2,1)S(1)}, u32[]{:S(2)}, u32[]{:S(2)}) collective-permute-start(bf16[144,576]{1,0:T(8,128)(2,1)S(1)} %pad_maximum_fusion.14), channel_id=1, source_target_pairs={{0,24},{4,28},{8,16},{12,20},{16,8},{20,12},{24,0},{28,4},{1,25},{... | collective-permute-start | bytes 497672 | tf_op jit(solution)/shard_map/ppermute | solution.py:30
  63.5 28.2 %collective-permute-start.11 = (bf16[144,576]{1,0:T(8,128)(2,1)S(1)}, bf16[144,576]{1,0:T(8,128)(2,1)}, u32[]{:S(2)}, u32[]{:S(2)}) collective-permute-start(bf16[144,576]{1,0:T(8,128)(2,1)S(1)} %pad_maximum_fusion.14), channel_id=1, source_target_pairs={{0,16},{4,20},{8,24},{12,28},{16,0},{20,4},{24,8},{28,12},{1,17},{... | collective-permute-start | bytes 497672 | tf_op jit(solution)/shard_map/ppermute | solution.py:30
  63.5 28.2 %collective-permute-start.10 = (bf16[144,576]{1,0:T(8,128)(2,1)S(1)}, bf16[144,576]{1,0:T(8,128)(2,1)}, u32[]{:S(2)}, u32[]{:S(2)}) collective-permute-start(bf16[144,576]{1,0:T(8,128)(2,1)S(1)} %pad_maximum_fusion.14), channel_id=1, source_target_pairs={{0,8},{4,12},{8,0},{12,4},{16,24},{20,28},{24,16},{28,20},{1,9},{5... | collective-permute-start | bytes 497672 | tf_op jit(solution)/shard_map/ppermute | solution.py:30
  64.4 45.9 %collective-permute-start.13 = (bf16[1152,896]{1,0:T(8,128)(2,1)}, bf16[1152,896]{1,0:T(8,128)(2,1)}, u32[]{:S(2)}, u32[]{:S(2)}) collective-permute-start(bf16[1152,896]{1,0:T(8,128)(2,1)} %all-gather.4.cloned.1.call-done.refs_4_.refs_2_), channel_id=1, source_target_pairs={{0,2},{1,3},{2,0},{3,1},{4,6},{5,7},{6,4},{7,5},{8,10},{9,11},{10,... | collective-permute-start | bytes 6193160 | tf_op jit(solution)/shard_map/ppermute | solution.py:25
  92.9 35.7 %collective-permute-start.14 = (bf16[4,144,576]{2,1,0:T(8,128)(2,1)S(1)}, bf16[4,144,576]{2,1,0:T(8,128)(2,1)}, u32[]{:S(2)}, u32[]{:S(2)}) collective-permute-start(bf16[4,144,576]{2,1,0:T(8,128)(2,1)S(1)} %get-tuple-element.182), channel_id=1, source_target_pairs={{0,4},{4,0},{8,12},{12,8},{16,20},{20,16},{24,28},{28,24},{1,5},{5... | collective-permute-start | bytes 1990664 | tf_op jit(solution)/shard_map/ppermute | solution.py:30
  140.1 60.3 %collective-permute-start.16 = (bf16[1152,1152]{1,0:T(8,128)(2,1)}, bf16[1152,1152]{1,0:T(8,128)(2,1)}, u32[]{:S(2)}, u32[]{:S(2)}) collective-permute-start(bf16[1152,1152]{1,0:T(8,128)(2,1)} %all-gather.6.cloned.1.call-done.refs_2_.refs_3_), channel_id=1, source_target_pairs={{0,2},{1,3},{2,0},{3,1},{4,6},{5,7},{6,4},{7,5},{8,10},{9,11},{10,... | collective-permute-start | bytes 7962632 | tf_op jit(solution)/shard_map/ppermute | solution.py:25
  217.2 22.3 %collective-permute-start.17 = (bf16[2,144,1152]{2,1,0:T(8,128)(2,1)}, bf16[2,144,1152]{2,1,0:T(8,128)(2,1)}, u32[]{:S(2)}, u32[]{:S(2)}) collective-permute-start(bf16[2,144,1152]{2,1,0:T(8,128)(2,1)} %get-tuple-element.175), channel_id=1, source_target_pairs={{0,4},{4,0},{8,12},{12,8},{16,20},{20,16},{24,28},{28,24},{1,5},{5... | collective-permute-start | bytes 1990664 | tf_op jit(solution)/shard_map/ppermute | solution.py:30
  219.1 20.4 %collective-permute-start.18 = (bf16[2,144,1152]{2,1,0:T(8,128)(2,1)}, bf16[2,144,1152]{2,1,0:T(8,128)(2,1)}, u32[]{:S(2)}, u32[]{:S(2)}) collective-permute-start(bf16[2,144,1152]{2,1,0:T(8,128)(2,1)} %get-tuple-element.176), channel_id=1, source_target_pairs={{0,2},{1,3},{2,0},{3,1},{4,6},{5,7},{6,4},{7,5},{8,10},{9,11},{10,... | collective-permute-start | bytes 1990664 | tf_op jit(solution)/shard_map/ppermute | solution.py:25
  243.3 39.6 %collective-permute-start.20 = (bf16[4,144,1152]{2,1,0:T(8,128)(2,1)}, bf16[4,144,1152]{2,1,0:T(8,128)(2,1)}, u32[]{:S(2)}, u32[]{:S(2)}) collective-permute-start(bf16[4,144,1152]{2,1,0:T(8,128)(2,1)} %pad_maximum_fusion.5), channel_id=1, source_target_pairs={{0,2},{1,3},{2,0},{3,1},{4,6},{5,7},{6,4},{7,5},{8,10},{9,11},{10,... | collective-permute-start | bytes 3981320 | tf_op jit(solution)/shard_map/ppermute | solution.py:25
  246.0 37.0 %collective-permute-start.19 = (bf16[4,144,1152]{2,1,0:T(8,128)(2,1)}, bf16[4,144,1152]{2,1,0:T(8,128)(2,1)}, u32[]{:S(2)}, u32[]{:S(2)}) collective-permute-start(bf16[4,144,1152]{2,1,0:T(8,128)(2,1)} %pad_maximum_fusion.4), channel_id=1, source_target_pairs={{0,4},{4,0},{8,12},{12,8},{16,20},{20,16},{24,28},{28,24},{1,5},{5... | collective-permute-start | bytes 3981320 | tf_op jit(solution)/shard_map/ppermute | solution.py:30
  264.2 25.8 %collective-permute-start.21 = (bf16[1024,1152]{1,0:T(8,128)(2,1)}, bf16[1024,1152]{1,0:T(8,128)(2,1)}, u32[]{:S(2)}, u32[]{:S(2)}) collective-permute-start(bf16[1024,1152]{1,0:T(8,128)(2,1)} %get-tuple-element.122.refs_0_), channel_id=1, source_target_pairs={{0,1},{1,0},{2,3},{3,2},{4,5},{5,4},{6,7},{7,6},{8,9},{9,8},{10,11... | collective-permute-start | bytes 7077896 | tf_op jit(solution)/shard_map/ppermute | solution.py:21
  278.2 38.3 %collective-permute-start.22 = (bf16[2,144,1152]{2,1,0:T(8,128)(2,1)}, bf16[2,144,1152]{2,1,0:T(8,128)(2,1)}, u32[]{:S(2)}, u32[]{:S(2)}) collective-permute-start(bf16[2,144,1152]{2,1,0:T(8,128)(2,1)} %get-tuple-element.172), channel_id=1, source_target_pairs={{0,4},{4,0},{8,12},{12,8},{16,20},{20,16},{24,28},{28,24},{1,5},{5... | collective-permute-start | bytes 1990664 | tf_op jit(solution)/shard_map/ppermute | solution.py:30
  279.6 36.8 %collective-permute-start.23 = (bf16[2,144,1152]{2,1,0:T(8,128)(2,1)}, bf16[2,144,1152]{2,1,0:T(8,128)(2,1)}, u32[]{:S(2)}, u32[]{:S(2)}) collective-permute-start(bf16[2,144,1152]{2,1,0:T(8,128)(2,1)} %get-tuple-element.173), channel_id=1, source_target_pairs={{0,2},{1,3},{2,0},{3,1},{4,6},{5,7},{6,4},{7,5},{8,10},{9,11},{10,... | collective-permute-start | bytes 1990664 | tf_op jit(solution)/shard_map/ppermute | solution.py:25
  287.6 28.9 %collective-permute-start.24 = (bf16[144,1152]{1,0:T(8,128)(2,1)}, bf16[144,1152]{1,0:T(8,128)(2,1)}, u32[]{:S(2)}, u32[]{:S(2)}) collective-permute-start(bf16[144,1152]{1,0:T(8,128)(2,1)} %get-tuple-element.119), channel_id=1, source_target_pairs={{0,8},{4,12},{8,0},{12,4},{16,24},{20,28},{24,16},{28,20},{1,9},{5... | collective-permute-start | bytes 995336 | tf_op jit(solution)/shard_map/ppermute | solution.py:30
  288.0 28.5 %collective-permute-start.25 = (bf16[144,1152]{1,0:T(8,128)(2,1)}, bf16[144,1152]{1,0:T(8,128)(2,1)}, u32[]{:S(2)}, u32[]{:S(2)}) collective-permute-start(bf16[144,1152]{1,0:T(8,128)(2,1)} %get-tuple-element.120), channel_id=1, source_target_pairs={{0,16},{4,20},{8,24},{12,28},{16,0},{20,4},{24,8},{28,12},{1,17},{... | collective-permute-start | bytes 995336 | tf_op jit(solution)/shard_map/ppermute | solution.py:30
  290.0 26.5 %collective-permute-start.26 = (bf16[144,1152]{1,0:T(8,128)(2,1)}, bf16[144,1152]{1,0:T(8,128)(2,1)}, u32[]{:S(2)}, u32[]{:S(2)}) collective-permute-start(bf16[144,1152]{1,0:T(8,128)(2,1)} %get-tuple-element.121), channel_id=1, source_target_pairs={{0,24},{4,28},{8,16},{12,20},{16,8},{20,12},{24,0},{28,4},{1,25},{... | collective-permute-start | bytes 995336 | tf_op jit(solution)/shard_map/ppermute | solution.py:30
  320.5 50.0 %collective-permute-start.28 = (bf16[4,144,1152]{2,1,0:T(8,128)(2,1)}, bf16[4,144,1152]{2,1,0:T(8,128)(2,1)}, u32[]{:S(2)}, u32[]{:S(2)}) collective-permute-start(bf16[4,144,1152]{2,1,0:T(8,128)(2,1)} %pad_maximum_fusion.7), channel_id=1, source_target_pairs={{0,2},{1,3},{2,0},{3,1},{4,6},{5,7},{6,4},{7,5},{8,10},{9,11},{10,... | collective-permute-start | bytes 3981320 | tf_op jit(solution)/shard_map/ppermute | solution.py:25
  323.1 47.4 %collective-permute-start.27 = (bf16[4,144,1152]{2,1,0:T(8,128)(2,1)}, bf16[4,144,1152]{2,1,0:T(8,128)(2,1)}, u32[]{:S(2)}, u32[]{:S(2)}) collective-permute-start(bf16[4,144,1152]{2,1,0:T(8,128)(2,1)} %pad_maximum_fusion.6), channel_id=1, source_target_pairs={{0,4},{4,0},{8,12},{12,8},{16,20},{20,16},{24,28},{28,24},{1,5},{5... | collective-permute-start | bytes 3981320 | tf_op jit(solution)/shard_map/ppermute | solution.py:30
  352.0 45.7 %collective-permute-start.31 = (bf16[2,144,1152]{2,1,0:T(8,128)(2,1)S(1)}, bf16[2,144,1152]{2,1,0:T(8,128)(2,1)S(1)}, u32[]{:S(2)}, u32[]{:S(2)}) collective-permute-start(bf16[2,144,1152]{2,1,0:T(8,128)(2,1)S(1)} %get-tuple-element.179), channel_id=1, source_target_pairs={{0,2},{1,3},{2,0},{3,1},{4,6},{5,7},{6,4},{7,5},{8,10},{9,11},{10,... | collective-permute-start | bytes 1990664 | tf_op jit(solution)/shard_map/ppermute | solution.py:25
  369.0 75.7 %collective-permute-start.39 = (bf16[4,144,1152]{2,1,0:T(8,128)(2,1)}, bf16[4,144,1152]{2,1,0:T(8,128)(2,1)}, u32[]{:S(2)}, u32[]{:S(2)}) collective-permute-start(bf16[4,144,1152]{2,1,0:T(8,128)(2,1)} %pad_maximum_fusion.9), channel_id=1, source_target_pairs={{0,2},{1,3},{2,0},{3,1},{4,6},{5,7},{6,4},{7,5},{8,10},{9,11},{10,... | collective-permute-start | bytes 3981320 | tf_op jit(solution)/shard_map/ppermute | solution.py:25
  375.3 36.3 %collective-permute-start.32 = (bf16[144,1152]{1,0:T(8,128)(2,1)}, bf16[144,1152]{1,0:T(8,128)(2,1)}, u32[]{:S(2)}, u32[]{:S(2)}) collective-permute-start(bf16[144,1152]{1,0:T(8,128)(2,1)} %get-tuple-element.134), channel_id=1, source_target_pairs={{0,8},{4,12},{8,0},{12,4},{16,24},{20,28},{24,16},{28,20},{1,9},{5... | collective-permute-start | bytes 995336 | tf_op jit(solution)/shard_map/ppermute | solution.py:30
  378.9 33.2 %collective-permute-start.33 = (bf16[144,1152]{1,0:T(8,128)(2,1)}, bf16[144,1152]{1,0:T(8,128)(2,1)}, u32[]{:S(2)}, u32[]{:S(2)}) collective-permute-start(bf16[144,1152]{1,0:T(8,128)(2,1)} %get-tuple-element.135), channel_id=1, source_target_pairs={{0,16},{4,20},{8,24},{12,28},{16,0},{20,4},{24,8},{28,12},{1,17},{... | collective-permute-start | bytes 995336 | tf_op jit(solution)/shard_map/ppermute | solution.py:30
  380.2 31.9 %collective-permute-start.34 = (bf16[144,1152]{1,0:T(8,128)(2,1)}, bf16[144,1152]{1,0:T(8,128)(2,1)}, u32[]{:S(2)}, u32[]{:S(2)}) collective-permute-start(bf16[144,1152]{1,0:T(8,128)(2,1)} %get-tuple-element.136), channel_id=1, source_target_pairs={{0,24},{4,28},{8,16},{12,20},{16,8},{20,12},{24,0},{28,4},{1,25},{... | collective-permute-start | bytes 995336 | tf_op jit(solution)/shard_map/ppermute | solution.py:30
  418.2 31.4 %collective-permute-start.38 = (bf16[4,144,1152]{2,1,0:T(8,128)(2,1)}, bf16[4,144,1152]{2,1,0:T(8,128)(2,1)}, u32[]{:S(2)}, u32[]{:S(2)}) collective-permute-start(bf16[4,144,1152]{2,1,0:T(8,128)(2,1)} %pad_maximum_fusion.8), channel_id=1, source_target_pairs={{0,4},{4,0},{8,12},{12,8},{16,20},{20,16},{24,28},{28,24},{1,5},{5... | collective-permute-start | bytes 3981320 | tf_op jit(solution)/shard_map/ppermute | solution.py:30
  473.9 34.3 %collective-permute-start.48 = (bf16[144,1152]{1,0:T(8,128)(2,1)S(1)}, bf16[144,1152]{1,0:T(8,128)(2,1)S(1)}, u32[]{:S(2)}, u32[]{:S(2)}) collective-permute-start(bf16[144,1152]{1,0:T(8,128)(2,1)S(1)} %copy-done.44), channel_id=1, source_target_pairs={{0,8},{4,12},{8,0},{12,4},{16,24},{20,28},{24,16},{28,20},{1,9},{5... | collective-permute-start | bytes 995336 | tf_op jit(solution)/shard_map/ppermute | solution.py:30
  474.9 33.3 %collective-permute-start.49 = (bf16[144,1152]{1,0:T(8,128)(2,1)S(1)}, bf16[144,1152]{1,0:T(8,128)(2,1)S(1)}, u32[]{:S(2)}, u32[]{:S(2)}) collective-permute-start(bf16[144,1152]{1,0:T(8,128)(2,1)S(1)} %copy-done.43), channel_id=1, source_target_pairs={{0,16},{4,20},{8,24},{12,28},{16,0},{20,4},{24,8},{28,12},{1,17},{... | collective-permute-start | bytes 995336 | tf_op jit(solution)/shard_map/ppermute | solution.py:30
  475.7 32.5 %collective-permute-start.50 = (bf16[144,1152]{1,0:T(8,128)(2,1)S(1)}, bf16[144,1152]{1,0:T(8,128)(2,1)S(1)}, u32[]{:S(2)}, u32[]{:S(2)}) collective-permute-start(bf16[144,1152]{1,0:T(8,128)(2,1)S(1)} %copy-done.42), channel_id=1, source_target_pairs={{0,24},{4,28},{8,16},{12,20},{16,8},{20,12},{24,0},{28,4},{1,25},{... | collective-permute-start | bytes 995336 | tf_op jit(solution)/shard_map/ppermute | solution.py:30
  (67 other events, 558.7 us)
Sparse Core Ops, SparseCore 0:
  12.1 51.1 all-gather.3
  65.5 67.6 all-gather.5
  135.9 87.0 all-gather.7
